TPU v7x, 32 devices: a whole 2x2x4 slice. The times are simulated.
32 devices in a mesh: strip: 4 (over z), mr: 8 (over y, x, core).
Axes of the slice: x: 2, y: 2, z: 4, core: 2. Of those that a mesh axis runs over, the one named last changes fastest.
Arguments:
- alm: bfloat16 [2, 256, 2048], P(None, ('strip', 'mr')), may hold values from -6 to 6
- beam: float32 [13, 2048], replicated, may hold values from -6 to 6
- wigner: bfloat16 [256, 13, 32, 2048], P(('strip', 'mr')), may hold values from -0.125 to 0.125
- base_index: int32 [8192], P(('strip', 'mr')), may hold values from 0 to 16124
- interp_weights: float32 [12, 8192], P(None, ('strip', 'mr')), may hold values from -3 to 3
- live_counts: int32 [32, 32], P(('strip', 'mr')), may hold values from 0 to 8, as said below
Outputs:
- tod: float32 [8192], P(('strip', 'mr'))
Inputs may be any that keep to these rules, and one draw needn't show every extreme that they name: live_counts[i, d] counts the used slots from device i to block d; blocks differ in how many samples point into them, and some pair uses all 8 slots in every draw.
All inputs are finite; a program needn't handle non-finite values.
Results may differ from a plain program's by a relative error of at most 0.0055.
Values may be sent and summed in bfloat16 or wider, within the bound.
No kernel may reach another device: no remote copies, remote signals or barrier semaphores. Data moves between devices by JAX's collectives and lax.ppermute only.
A program may use at most 64 MiB of HBM per device.

v0:
```python
import math

import jax
import jax.numpy as jnp
from jax import lax
from jax.sharding import PartitionSpec as P


def padded_2(x, sides, width):
    for axis, dim in sides:
        devices, length = (lax.axis_size(axis), x.shape[dim])
        up = [(i, (i + 1) % devices) for i in range(devices)]
        down = [(j, i) for i, j in up]
        last = lax.slice_in_dim(x, length - width, length, axis=dim)
        first = lax.slice_in_dim(x, 0, width, axis=dim)
        before = lax.ppermute(last, axis, up)
        after = lax.ppermute(first, axis, down)
        x = jnp.concatenate([before, x, after], axis=dim)
    return x


def phase_tables(m_first, m_count, phi_count, phi_total):
    m_vals = m_first + jnp.arange(m_count, dtype=jnp.int32)
    phi_vals = jnp.arange(phi_count, dtype=jnp.int32)
    product = phi_vals[:, None] * m_vals[None, :] % phi_total
    angle = 2.0 * math.pi / phi_total * product.astype(jnp.float32)
    return (jnp.cos(angle).astype(jnp.bfloat16), jnp.sin(angle).astype(jnp.bfloat16))


def orient_table(psi_count, k_count):
    product = (
        jnp.arange(psi_count, dtype=jnp.int32)[:, None]
        * jnp.arange(k_count, dtype=jnp.int32)[None, :]
        % psi_count
    )
    angle = 2.0 * math.pi / psi_count * product.astype(jnp.float32)
    return jnp.stack([jnp.cos(angle), -jnp.sin(angle)], axis=1)


def phi_sum(cos_table, sin_table, coef):
    real_part = jnp.dot(cos_table, coef[0], preferred_element_type=jnp.float32) - jnp.dot(
        sin_table, coef[1], preferred_element_type=jnp.float32
    )
    imag_part = jnp.dot(sin_table, coef[0], preferred_element_type=jnp.float32) + jnp.dot(
        cos_table, coef[1], preferred_element_type=jnp.float32
    )
    return jnp.concatenate([real_part, imag_part], axis=1)


def decode(base, lat_dev, phi_dev):
    phi_base = base % (phi_dev + 1)
    rest = base // (phi_dev + 1)
    return (rest // (lat_dev + 1), rest % (lat_dev + 1), phi_base)


def tap_table(index, tap_weights, length):
    positions = jnp.arange(length, dtype=jnp.int32)[:, None]
    table = jnp.zeros((length, index.shape[1]), jnp.float32)
    for offset in range(4):
        table = table + jnp.where(
            positions == index[offset][None, :], tap_weights[offset][None, :], 0.0
        )
    return table


def stencil(cube_block, psi_idx, lat_idx, phi_idx, weights, lat_weight):
    psi_len, lat_len, phi_len = cube_block.shape
    phi_table = tap_table(phi_idx, weights[4:8], phi_len)
    lat_table = tap_table(lat_idx, lat_weight, lat_len)
    psi_table = tap_table(psi_idx, weights[8:12], psi_len)
    along = jnp.dot(
        cube_block.reshape(psi_len * lat_len, phi_len).astype(jnp.float32),
        phi_table,
        precision=lax.Precision.HIGHEST,
    )
    along = along.reshape(psi_len, lat_len, -1)
    across = jnp.sum(along * lat_table[None], axis=1)
    return jnp.sum(across * psi_table, axis=0)


def owner_values(packet_in, padded, lat_dev, phi_dev, psi_count):
    shape = packet_in.shape[1:]
    flat = packet_in.reshape(packet_in.shape[0], -1)
    psi_base, lat_base, phi_base = decode(flat[12].astype(jnp.int32), lat_dev, phi_dev)
    offs = jnp.arange(4, dtype=jnp.int32)[:, None]
    psi_idx = (psi_base[None] + offs) % psi_count
    lat_idx = lat_base[None] + offs
    phi_idx = phi_base[None] + offs
    return stencil(padded, psi_idx, lat_idx, phi_idx, flat[:12], flat[0:4]).reshape(shape)


def on_device(alm, beam, wigner, base_index, interp_weights, live_counts):
    n_strip = lax.axis_size("strip")
    n_mr = lax.axis_size("mr")
    devices = n_strip * n_mr
    k_count = beam.shape[0]
    mixed = (alm[:, :, None, :].astype(jnp.float32) * beam[None, None, :, :]).astype(jnp.bfloat16)
    coef = jnp.einsum("cmkl,mkrl->cmkr", mixed, wigner, preferred_element_type=jnp.float32).astype(
        jnp.bfloat16
    )
    coef = lax.all_to_all(coef, "mr", split_axis=3, concat_axis=1, tiled=True)
    m_here = coef.shape[1]
    lat_dev = coef.shape[3]
    coef = coef.reshape(2, m_here, k_count * lat_dev)
    m_total = m_here * n_strip
    phi_total = 2 * m_total
    phi_dev = phi_total // n_strip
    strip_at = lax.axis_index("strip")
    m_first = strip_at * m_here
    cos_table, sin_table = phase_tables(
        m_first, m_here, phi_dev * lax.axis_size("strip"), phi_total
    )
    spectra = lax.psum_scatter(
        phi_sum(cos_table, sin_table, coef), "strip", scatter_dimension=0, tiled=True
    )
    spectra = spectra.reshape(phi_dev, 2, k_count, lat_dev)
    psi_count = 2 * k_count - 1
    scale = 1.0 / math.sqrt(m_total * k_count)
    cube = (
        jnp.einsum(
            "pckr,tck->trp",
            spectra,
            orient_table(psi_count, k_count),
            precision=lax.Precision.HIGHEST,
        )
        * scale
    ).astype(jnp.bfloat16)
    cap = base_index.shape[0] // devices
    live = (
        jnp.arange(cap, dtype=jnp.int32)[None, :] < live_counts.reshape(devices)[:, None]
    ).astype(jnp.float32)
    weights = interp_weights.reshape(12, devices, cap)
    lat_w = weights[0:4] * live[None]
    weights = jnp.concatenate([lat_w, weights[4:]], axis=0)
    padded = padded_2(cube, (("strip", 2), ("mr", 1)), 2)
    packet = jnp.concatenate(
        [weights, base_index.reshape(1, devices, cap).astype(jnp.float32)], axis=0
    )
    values = owner_values(
        lax.all_to_all(packet, ("strip", "mr"), split_axis=1, concat_axis=1, tiled=True),
        padded,
        lat_dev,
        phi_dev,
        psi_count,
    )
    result = lax.all_to_all(values, ("strip", "mr"), split_axis=0, concat_axis=0, tiled=True)
    return result.reshape(-1)


def solution(mesh):
    placed = (
        P(None, ("strip", "mr"), None),
        P(),
        P(("strip", "mr"), None, None, None),
        P(("strip", "mr")),
        P(None, ("strip", "mr")),
        P(("strip", "mr"), None),
    )
    return jax.shard_map(
        on_device, mesh=mesh, in_specs=placed, out_specs=P(("strip", "mr")), check_vma=False
    )
```

profile of v0, /device:TPU:0, one launch (start us, length us, event | category | flops | bytes accessed | tf_op | source)
XLA Modules:
  0.0 91.3 jit_solution(9475546606668094492)
XLA Ops:
  6.5 1.0 %copy.40 = f32[2,8,2048]{2,0,1:T(2,128)S(1)} copy(bf16[2,8,2048]{2,1,0:T(8,128)(2,1)} %param.6) | data formatting | bytes 196608 | tf_op jit(solution)/shard_map/convert_element_type | solution.py:97
  7.5 6.8 %fusion.2 = bf16[2,8,13,32]{3,0,2,1:T(2,128)(2,1)S(1)} fusion(bf16[8,13,32,2048]{3,2,1,0:T(8,128)(2,1)} %param.8, f32[13,2048]{1,0:T(8,128)} %param.7, f32[2,8,2048]{2,0,1:T(2,128)S(1)} %copy.40), kind=kOutput, calls=%fused_computation.8 | convolution fusion | flops 28121600 | bytes 13882368 | tf_op jit(solution)/shard_map/cmkl,mkrl->cmkr/dot_general | solution.py:98
  14.4 0.2 copy.41
  14.6 0.8 reshape.386
  15.4 5.2 %all-to-all-start = ((bf16[8,2,416]{2,1,0:T(2,128)(2,1)}), bf16[8,2,416]{2,1,0:T(2,128)(2,1)S(1)}, u32[]{:S(2)}, u32[]{:S(2)}) async-start(bf16[8,2,416]{2,1,0:T(2,128)(2,1)} %reshape.386), calls=%async_computation | async-start | bytes 32768 | tf_op jit(solution)/shard_map/all_to_all | solution.py:101
  20.8 0.1 slice.159
  20.9 0.1 slice.161
  21.1 0.9 %copy.46 = f32[13,32,8]{0,2,1:T(8,128)} copy(f32[13,32,8]{2,1,0:T(8,128)S(1)} %pad_maximum_fusion.1) | data formatting | bytes 26624 | tf_op jit(solution)/shard_map/concatenate | solution.py:136
  22.0 3.3 %all-to-all-done = bf16[8,2,416]{2,1,0:T(2,128)(2,1)S(1)} async-done(((bf16[8,2,416]{2,1,0:T(2,128)(2,1)}), bf16[8,2,416]{2,1,0:T(2,128)(2,1)S(1)}, u32[]{:S(2)}, u32[]{:S(2)}) %all-to-all-start) | async-done | bytes 13344 | tf_op jit(solution)/shard_map/all_to_all | solution.py:101
  25.3 4.0 %all-to-all-start.1 = ((f32[13,32,8]{0,2,1:T(8,128)}), f32[13,32,8]{0,2,1:T(8,128)S(1)}, u32[]{:S(2)}, u32[]{:S(2)}) async-start(f32[13,32,8]{0,2,1:T(8,128)} %copy.46), calls=%async_computation.2 | async-start | bytes 262144 | tf_op jit(solution)/shard_map/all_to_all | solution.py:140
  29.3 0.3 reshape.387
  29.7 0.3 copy.43
  30.0 0.1 squeeze.4
  30.1 1.3 %fusion.22 = f32[512,52]{0,1:T(8,128)S(1)} fusion(bf16[64,52]{0,1:T(8,128)(2,1)S(1)} %squeeze.4, s32[64]{0:T(128)S(1)} %iota_add_fusion.2), kind=kOutput, calls=%fused_computation.55 | convolution fusion | flops 3899392 | bytes 113408 | tf_op jit(solution)/shard_map/dot_general | solution.py:44
  31.4 1.3 %fusion.21 = f32[512,52]{0,1:T(8,128)S(1)} fusion(bf16[64,52]{0,1:T(8,128)(2,1)S(1)} %squeeze.4, s32[64]{0:T(128)S(1)} %iota_add_fusion.2), kind=kOutput, calls=%fused_computation.54 | convolution fusion | flops 3899392 | bytes 113408 | tf_op jit(solution)/shard_map/dot_general | solution.py:41
  32.7 0.3 copy.44
  33.0 0.1 squeeze.10
  33.1 1.3 %convolution_add_fusion = f32[512,52]{0,1:T(8,128)S(1)} fusion(f32[512,52]{0,1:T(8,128)S(1)} %fusion.22, bf16[64,52]{0,1:T(8,128)(2,1)S(1)} %squeeze.10, s32[64]{0:T(128)S(1)} %iota_add_fusion.2), kind=kOutput, calls=%fused_computation.3 | convolution fusion | flops 3926016 | bytes 219904 | tf_op jit(solution)/shard_map/dot_general | solution.py:44
  34.4 1.3 %convolution_subtract_fusion = f32[512,52]{0,1:T(8,128)S(1)} fusion(f32[512,52]{0,1:T(8,128)S(1)} %fusion.21, bf16[64,52]{0,1:T(8,128)(2,1)S(1)} %squeeze.10, s32[64]{0:T(128)S(1)} %iota_add_fusion.2), kind=kOutput, calls=%fused_computation.4 | convolution fusion | flops 3926016 | bytes 219904 | tf_op jit(solution)/shard_map/dot_general | solution.py:41
  35.8 0.7 pad_maximum_fusion
  36.5 1.0 %all-to-all-done.1 = f32[13,32,8]{0,2,1:T(8,128)S(1)} async-done(((f32[13,32,8]{0,2,1:T(8,128)}), f32[13,32,8]{0,2,1:T(8,128)S(1)}, u32[]{:S(2)}, u32[]{:S(2)}) %all-to-all-start.1) | async-done | bytes 13344 | tf_op jit(solution)/shard_map/all_to_all | solution.py:140
  37.5 0.7 fusion.23
  38.2 0.1 ne.125
  38.3 1.2 %remainder_reduce_fusion = (s32[32,8]{1,0:T(8,128)S(1)}, s32[32,8]{1,0:T(8,128)S(1)}) fusion(f32[13,32,8]{0,2,1:T(8,128)S(1)} %all-to-all-done.1), kind=kLoop, calls=%fused_computation.53 | loop fusion | flops 768 | bytes 3072 | tf_op jit(solution)/shard_map/jit(remainder)/rem | solution.py:51
  39.5 0.1 rem.103
  39.6 0.1 div.25
  39.8 0.9 slice_reduce_fusion.3
  40.7 0.1 broadcast_in_dim.144
  40.8 0.1 broadcast_in_dim.142
  40.9 0.1 broadcast_in_dim.139
  41.1 16.3 %reduce-scatter.2.cloned.1.call-done = f32[128,104]{0,1:T(8,128)} async-done(((f32[512,104]{0,1:T(8,128)}), f32[128,104]{0,1:T(8,128)}) %reduce-scatter.2.cloned.1.call-update) | async-done | bytes 53264 | tf_op jit(solution)/shard_map/reduce_scatter | solution.py:113
  57.4 1.1 %fusion.4 = bf16[25,4,128]{2,0,1:T(8,128)(2,1)S(1)} fusion(f32[128,2,13,4]{0,3,2,1:T(4,128)} %bitcast.55, f32[25,1,13]{0,2,1:T(8,128)S(1)} %get-tuple-element.40, f32[25,1,13]{0,2,1:T(8,128)S(1)} %get-tuple-element.41), kind=kOutput, calls=%fused_computation.10 | convolution fusion | flops 4019850 | bytes 81448 | tf_op jit(solution)/shard_map/pckr,tck->trp/dot_general | solution.py:120
  58.5 3.8 %collective-permute-start.1 = (bf16[25,4,2]{2,0,1:T(8,128)(2,1)S(1)}, bf16[25,4,2]{2,0,1:T(8,128)(2,1)S(1)}, u32[]{:S(2)}, u32[]{:S(2)}) collective-permute-start(bf16[25,4,2]{2,0,1:T(8,128)(2,1)S(1)} %get-tuple-element.24), channel_id=1, source_target_pairs={{8,0},{16,8},{24,16},{0,24},{9,1},{17,9},{25,17},{1,25},{10,2},{18... | collective-permute-start | bytes 1208 | tf_op jit(solution)/shard_map/ppermute | solution.py:17
  62.4 1.9 %collective-permute-done = bf16[25,4,2]{2,0,1:T(8,128)(2,1)S(1)} collective-permute-done((bf16[25,4,2]{2,0,1:T(8,128)(2,1)S(1)}, bf16[25,4,2]{2,0,1:T(8,128)(2,1)S(1)}, u32[]{:S(2)}, u32[]{:S(2)}) %collective-permute-start) | collective-permute-done | bytes 432 | tf_op jit(solution)/shard_map/ppermute | solution.py:16
  64.2 0.1 pad_maximum_fusion.3
  64.4 2.6 %collective-permute-start.3 = (bf16[25,2,132]{2,0,1:T(8,128)(2,1)S(1)}, bf16[25,2,132]{2,0,1:T(8,128)(2,1)S(1)}, u32[]{:S(2)}, u32[]{:S(2)}) collective-permute-start(bf16[25,2,132]{2,0,1:T(8,128)(2,1)S(1)} %get-tuple-element.22), channel_id=1, source_target_pairs={{1,0},{2,1},{3,2},{4,3},{5,4},{6,5},{7,6},{0,7},{9,8},{10,9},{11,1... | collective-permute-start | bytes 39608 | tf_op jit(solution)/shard_map/ppermute | solution.py:17
  67.2 0.1 broadcast_in_dim.155
  67.3 0.1 broadcast_in_dim.151
  67.4 0.1 broadcast_in_dim.137
  67.6 0.1 broadcast_in_dim.133
  67.7 0.1 broadcast_in_dim.130
  67.8 0.9 collective-permute-done.2
  68.7 0.1 pad_maximum_fusion.2
  68.8 0.4 fusion
  69.3 13.3 %all_to_all.29 = f32[32,1,8]{2,1,0:T(1,128)S(1)} all-to-all(f32[32,1,8]{2,1,0:T(1,128)S(1)} %bitcast.56), channel_id=1, replica_groups=mesh['strip'=4,'mr'=8] {'strip','mr'}, dimensions={0} | all-to-all | bytes 2048 | tf_op jit(solution)/shard_map/all_to_all | solution.py:146
  82.6 0.5 broadcast.328
  83.1 0.7 reduce.33
  83.8 0.7 reshape.358
  (39 shorter events, 1.0 us)
Async XLA Ops:
  6.5 14.0 %copy-start = (f32[12,256]{1,0:T(8,128)S(1)}, f32[12,256]{1,0:T(8,128)}, u32[]{:S(2)}) copy-start(f32[12,256]{1,0:T(8,128)} %param.10) | copy-start | bytes 36868
  6.5 14.3 %slice-start = ((f32[12,256]{1,0:T(8,128)}), f32[4,256]{1,0:T(4,128)S(1)}, s32[]{:S(2)}) async-start(f32[12,256]{1,0:T(8,128)} %param.10), calls=%async_computation.5 | async-start | bytes 8192 | tf_op jit(solution)/shard_map/slice | solution.py:133
  6.5 14.1 %copy-start.1 = (s32[256]{0:T(256)S(1)}, s32[256]{0:T(256)}, u32[]{:S(2)}) copy-start(s32[256]{0:T(256)} %param.9) | copy-start | bytes 3076
  6.5 14.2 %copy-start.2 = (s32[1,32]{1,0:T(1,128)S(1)}, s32[1,32]{1,0:T(1,128)}, u32[]{:S(2)}) copy-start(s32[1,32]{1,0:T(1,128)} %param.11) | copy-start | bytes 388
  15.4 9.9 %all-to-all-start = ((bf16[8,2,416]{2,1,0:T(2,128)(2,1)}), bf16[8,2,416]{2,1,0:T(2,128)(2,1)S(1)}, u32[]{:S(2)}, u32[]{:S(2)}) async-start(bf16[8,2,416]{2,1,0:T(2,128)(2,1)} %reshape.386), calls=%async_computation | async-start | bytes 32768 | tf_op jit(solution)/shard_map/all_to_all | solution.py:101
  25.3 12.2 %all-to-all-start.1 = ((f32[13,32,8]{0,2,1:T(8,128)}), f32[13,32,8]{0,2,1:T(8,128)S(1)}, u32[]{:S(2)}, u32[]{:S(2)}) async-start(f32[13,32,8]{0,2,1:T(8,128)} %copy.46), calls=%async_computation.2 | async-start | bytes 262144 | tf_op jit(solution)/shard_map/all_to_all | solution.py:140
  29.3 28.1 %reduce-scatter.2.cloned.1.call-start = ((), (), s32[]{:S(2)}) async-start(), calls=%async_computation.4 | async-start | bytes 266240 | tf_op jit(solution)/shard_map/reduce_scatter | solution.py:113
  58.5 5.7 %collective-permute-start = (bf16[25,4,2]{2,0,1:T(8,128)(2,1)S(1)}, bf16[25,4,2]{2,0,1:T(8,128)(2,1)S(1)}, u32[]{:S(2)}, u32[]{:S(2)}) collective-permute-start(bf16[25,4,2]{2,0,1:T(8,128)(2,1)S(1)} %get-tuple-element.23), channel_id=1, source_target_pairs={{0,8},{8,16},{16,24},{24,0},{1,9},{9,17},{17,25},{25,1},{2,10},{10... | collective-permute-start | bytes 1208 | tf_op jit(solution)/shard_map/ppermute | solution.py:16
  58.5 5.7 %collective-permute-start.1 = (bf16[25,4,2]{2,0,1:T(8,128)(2,1)S(1)}, bf16[25,4,2]{2,0,1:T(8,128)(2,1)S(1)}, u32[]{:S(2)}, u32[]{:S(2)}) collective-permute-start(bf16[25,4,2]{2,0,1:T(8,128)(2,1)S(1)} %get-tuple-element.24), channel_id=1, source_target_pairs={{8,0},{16,8},{24,16},{0,24},{9,1},{17,9},{25,17},{1,25},{10,2},{18... | collective-permute-start | bytes 1208 | tf_op jit(solution)/shard_map/ppermute | solution.py:17
  64.4 4.3 %collective-permute-start.2 = (bf16[25,2,132]{2,0,1:T(8,128)(2,1)S(1)}, bf16[25,2,132]{2,0,1:T(8,128)(2,1)S(1)}, u32[]{:S(2)}, u32[]{:S(2)}) collective-permute-start(bf16[25,2,132]{2,0,1:T(8,128)(2,1)S(1)} %get-tuple-element.21), channel_id=1, source_target_pairs={{0,1},{1,2},{2,3},{3,4},{4,5},{5,6},{6,7},{7,0},{8,9},{9,10},{10,1... | collective-permute-start | bytes 39608 | tf_op jit(solution)/shard_map/ppermute | solution.py:16
  64.4 4.2 %collective-permute-start.3 = (bf16[25,2,132]{2,0,1:T(8,128)(2,1)S(1)}, bf16[25,2,132]{2,0,1:T(8,128)(2,1)S(1)}, u32[]{:S(2)}, u32[]{:S(2)}) collective-permute-start(bf16[25,2,132]{2,0,1:T(8,128)(2,1)S(1)} %get-tuple-element.22), channel_id=1, source_target_pairs={{1,0},{2,1},{3,2},{4,3},{5,4},{6,5},{7,6},{0,7},{9,8},{10,9},{11,1... | collective-permute-start | bytes 39608 | tf_op jit(solution)/shard_map/ppermute | solution.py:17
Sparse Core Ops, SparseCore 0:
  36.6 20.7 reduce-scatter.1
where the time goes:
time: 91.6 us; the launch traced here: 91.3 us
  waiting for transfers between devices  23.4 us (26%)
  starting transfers between devices  15.7 us (17%)
  between operations  13.7 us (15%)
  matrix products  13.4 us (15%)
  blocking collectives  13.3 us (15%)
  local copies, waits for them, and re-layouts  7.98 us (9%)
  other arithmetic  3.78 us (4%)
    reduce_scatter x1, waiting for transfers between devices, on_device(): lax.psum_scatter(phi_sum(cos_table, sin_table, coef), 'strip', scatter_di...  16.3 us
    all_to_all x1, blocking collectives, on_device(): lax.all_to_all(values, ('strip', 'mr'), split_axis=0, concat_axis=0, tile...  13.3 us
    dot_general x1, matrix products, on_device(): jnp.einsum('cmkl,mkrl->cmkr', mixed, wigner, preferred_element_type=jnp.f...  6.85 us
    ppermute x2, starting transfers between devices, padded_2(): after = lax.ppermute(first, axis, down)  6.45 us
    all_to_all x1, starting transfers between devices, on_device(): coef = lax.all_to_all(coef, 'mr', split_axis=3, concat_axis=1, tiled=True)  5.17 us
    all_to_all x1, starting transfers between devices, on_device(): lax.all_to_all(packet, ('strip', 'mr'), split_axis=1, concat_axis=1, tile...  3.97 us
    all_to_all x1, waiting for transfers between devices, on_device(): coef = lax.all_to_all(coef, 'mr', split_axis=3, concat_axis=1, tiled=True)  3.3 us
    ppermute x2, waiting for transfers between devices, padded_2(): before = lax.ppermute(last, axis, up)  2.75 us
  transfers between devices with their start and end apart: 7, of which 5 were waited for; matrix products, arithmetic and copies ran while one was open for 14% of the time, Pallas kernels for 0%

commit v1 on v0

v1 whole, which is shorter than its diff:
```python
import functools
import math

import jax
import jax.numpy as jnp
import numpy as np
from jax import lax
from jax.experimental import pallas as pl
from jax.experimental.pallas import tpu as pltpu
from jax.sharding import PartitionSpec as P

NT = (((1,), (1,)), ((), ()))
VMEM = pl.BlockSpec(memory_space=pltpu.VMEM)


def coef_kernel(alm_hbm, beam_hbm, table_hbm, out_ref, alm, beam, table, mixed, rows, sems):
    orders, beam_rows, ells = table.shape
    k_count = beam.shape[0]
    lats = beam_rows // k_count
    k_pad = mixed.shape[1] // 2
    small = [
        pltpu.make_async_copy(alm_hbm, alm, sems.at[orders]),
        pltpu.make_async_copy(beam_hbm, beam, sems.at[orders + 1]),
    ]
    big = [
        pltpu.make_async_copy(table_hbm.at[m], table.at[m], sems.at[m]) for m in range(orders)
    ]
    for copy in small + big:
        copy.start()
    mixed[...] = jnp.zeros_like(mixed)
    for copy in small:
        copy.wait()
    for m in range(orders):
        for c in range(2):
            product = alm[c, m, :].astype(jnp.float32)[None, :] * beam[...]
            mixed[m, c * k_pad : c * k_pad + k_count, :] = product.astype(jnp.bfloat16)
    for m in range(orders):
        big[m].wait()
        y = lax.dot_general(mixed[m], table[m], NT, preferred_element_type=jnp.float32)
        of_row = lax.broadcasted_iota(jnp.int32, y.shape, 0) % k_pad
        of_lane = lax.broadcasted_iota(jnp.int32, y.shape, 1) // lats
        y = jnp.where(of_row == of_lane, y, 0.0)
        for c in range(2):
            total = jnp.sum(y[c * k_pad : (c + 1) * k_pad], axis=0, keepdims=True)
            rows[c * orders + m : c * orders + m + 1, :] = total
    out_ref[...] = rows[...].astype(jnp.bfloat16)


def local_coef(alm, beam, wigner):
    orders, k_count, lats, ells = wigner.shape
    k_pad = -(-k_count // 8) * 8
    anywhere = pl.BlockSpec(memory_space=pl.ANY)
    return pl.pallas_call(
        coef_kernel,
        out_shape=jax.ShapeDtypeStruct((2 * orders, k_count * lats), jnp.bfloat16),
        in_specs=[anywhere] * 3,
        out_specs=VMEM,
        scratch_shapes=[
            pltpu.VMEM((2, orders, ells), jnp.bfloat16),
            pltpu.VMEM((k_count, ells), jnp.float32),
            pltpu.VMEM((orders, k_count * lats, ells), jnp.bfloat16),
            pltpu.VMEM((orders, 2 * k_pad, ells), jnp.bfloat16),
            pltpu.VMEM((2 * orders, k_count * lats), jnp.float32),
            pltpu.SemaphoreType.DMA((orders + 2,)),
        ],
        compiler_params=pltpu.CompilerParams(vmem_limit_bytes=40 << 20),
        cost_estimate=pl.CostEstimate(
            flops=4 * wigner.size, bytes_accessed=2 * wigner.size, transcendentals=0
        ),
        name="coef",
    )(alm, beam, wigner.reshape(orders, k_count * lats, ells))


def cos_sin_turns(x):
    x = x - jnp.round(x)
    u = x * x
    cos = jnp.zeros_like(x)
    sin = jnp.zeros_like(x)
    for n in range(9, -1, -1):
        cos = cos * u + (-1) ** n * (2 * math.pi) ** (2 * n) / math.factorial(2 * n)
        sin = sin * u + (-1) ** n * (2 * math.pi) ** (2 * n + 1) / math.factorial(2 * n + 1)
    return cos, sin * x


def remainder(x, n):
    return x - n * jnp.floor((x + 0.5) * (1.0 / n))


def weights_kernel(
    sizes, slots_ref, counts_ref, order_ref, lane_ref, re_ref, im_ref, tail_re_ref, tail_im_ref
):
    cap, phi_total, lats, psi_count, lat_dev, phi_dev, scale = sizes
    cols = slots_ref[...].T
    count = cols.shape[0]
    base, slot_e, strip_phi, mr_lat = (cols[:, i : i + 1] for i in range(12, 16))
    dest = lax.broadcasted_iota(jnp.int32, (count, counts_ref.shape[1]), 1).astype(jnp.float32)
    of_slot = cols[:, 16:17]
    used = jnp.sum(
        jnp.where(dest == of_slot, counts_ref[...].astype(jnp.float32), 0.0), axis=1, keepdims=True
    )
    live = (slot_e < used).astype(jnp.float32)
    rest = jnp.floor((base + 0.5) * (1.0 / (phi_dev + 1)))
    phi_base = base - rest * (phi_dev + 1)
    psi_base = jnp.floor((rest + 0.5) * (1.0 / (lat_dev + 1)))
    lat_base = rest - psi_base * (lat_dev + 1)

    order, quarter = order_ref[0:1], order_ref[1:2]
    cos, sin = cos_sin_turns((strip_phi + phi_base - 2.0) * order * (1.0 / phi_total) + quarter)
    sum_re = cols[:, 4:5] * jnp.ones_like(order)
    sum_im = jnp.zeros_like(sum_re)
    for b in range(1, 4):
        step_cos, step_sin = cos_sin_turns(b * order * (1.0 / phi_total))
        sum_re = sum_re + cols[:, 4 + b : 5 + b] * step_cos
        sum_im = sum_im + cols[:, 4 + b : 5 + b] * step_sin
    re_ref[...] = (cos * sum_re - sin * sum_im).astype(jnp.bfloat16)
    im_ref[...] = (sin * sum_re + cos * sum_im).astype(jnp.bfloat16)

    k_lane, r_lane = lane_ref[0:1], lane_ref[1:2]
    cos, sin = cos_sin_turns(remainder(psi_base * k_lane, psi_count) * (1.0 / psi_count))
    sum_re = cols[:, 8:9] * jnp.ones_like(k_lane)
    sum_im = jnp.zeros_like(sum_re)
    for c in range(1, 4):
        step_cos, step_sin = cos_sin_turns(remainder(c * k_lane, psi_count) * (1.0 / psi_count))
        sum_re = sum_re + cols[:, 8 + c : 9 + c] * step_cos
        sum_im = sum_im + cols[:, 8 + c : 9 + c] * step_sin
    across = jnp.zeros_like(sum_re)
    for a in range(4):
        row = remainder(mr_lat + lat_base - 2.0 + a, lats)
        across = across + jnp.where(row == r_lane, cols[:, a : a + 1] * live, 0.0)
    across = across * scale
    tail_re_ref[...] = (cos * sum_re - sin * sum_im) * across
    tail_im_ref[...] = -(sin * sum_re + cos * sum_im) * across


def sample_weights(base_index, interp_weights, live_counts, order, quarter, sizes, n_mr, k_count):
    cap, phi_total, lats, psi_count, lat_dev, phi_dev, scale = sizes
    slots = base_index.shape[0]
    dest = np.arange(slots) // cap
    fixed = np.zeros((19, slots), np.float32)
    fixed[0] = np.arange(slots) % cap
    fixed[1] = dest // n_mr * phi_dev
    fixed[2] = dest % n_mr * lat_dev
    fixed[3] = dest
    table = jnp.concatenate(
        [interp_weights, base_index[None].astype(jnp.float32), jnp.asarray(fixed)], axis=0
    )
    lane = np.zeros((8, k_count * lats), np.float32)
    lane[0] = np.arange(k_count * lats) // lats
    lane[1] = np.arange(k_count * lats) % lats
    orders = jnp.stack([order, quarter] + [jnp.zeros_like(order)] * 6)
    block = min(slots, 256)
    width = order.shape[0]
    lanes = k_count * lats
    whole = lambda shape: pl.BlockSpec(shape, lambda i: (0, 0))
    return pl.pallas_call(
        functools.partial(weights_kernel, sizes),
        grid=(slots // block,),
        out_shape=(
            jax.ShapeDtypeStruct((slots, width), jnp.bfloat16),
            jax.ShapeDtypeStruct((slots, width), jnp.bfloat16),
            jax.ShapeDtypeStruct((slots, lanes), jnp.float32),
            jax.ShapeDtypeStruct((slots, lanes), jnp.float32),
        ),
        in_specs=[
            pl.BlockSpec((32, block), lambda i: (0, i)),
            whole(live_counts.shape),
            whole(orders.shape),
            whole(lane.shape),
        ],
        out_specs=(
            pl.BlockSpec((block, width), lambda i: (i, 0)),
            pl.BlockSpec((block, width), lambda i: (i, 0)),
            pl.BlockSpec((block, lanes), lambda i: (i, 0)),
            pl.BlockSpec((block, lanes), lambda i: (i, 0)),
        ),
        compiler_params=pltpu.CompilerParams(vmem_limit_bytes=32 << 20),
        cost_estimate=pl.CostEstimate(
            flops=60 * slots * (width + lanes), bytes_accessed=1 << 20, transcendentals=0
        ),
        name="weights",
    )(table, live_counts, orders, jnp.asarray(lane))


def sample_kernel(re_ref, im_ref, tail_re_ref, tail_im_ref, *refs):
    parts, out_ref, coef = refs[:-2], refs[-2], refs[-1]
    start = 0
    for part in parts:
        coef[start : start + part.shape[0], :] = part[...]
        start += part.shape[0]
    real = jnp.dot(re_ref[...], coef[...], preferred_element_type=jnp.float32)
    imag = jnp.dot(im_ref[...], coef[...], preferred_element_type=jnp.float32)
    terms = real * tail_re_ref[...] + imag * tail_im_ref[...]
    out_ref[...] = jnp.sum(terms.T, axis=0, keepdims=True)


def sample(phases, parts):
    slots, width = phases[0].shape
    lanes = phases[2].shape[1]
    block = min(slots, 256)
    rows = lambda n: pl.BlockSpec((block, n), lambda i: (i, 0))
    return pl.pallas_call(
        sample_kernel,
        grid=(slots // block,),
        out_shape=jax.ShapeDtypeStruct((1, slots), jnp.float32),
        in_specs=[rows(width), rows(width), rows(lanes), rows(lanes)]
        + [pl.BlockSpec(part.shape, lambda i: (0, 0)) for part in parts],
        out_specs=pl.BlockSpec((1, block), lambda i: (0, i)),
        scratch_shapes=[pltpu.VMEM((width, lanes), jnp.bfloat16)],
        compiler_params=pltpu.CompilerParams(vmem_limit_bytes=32 << 20),
        cost_estimate=pl.CostEstimate(
            flops=4 * slots * width * lanes, bytes_accessed=1 << 20, transcendentals=0
        ),
        name="sample",
    )(*phases, *parts)


def on_device(alm, beam, wigner, base_index, interp_weights, live_counts):
    n_strip = lax.axis_size("strip")
    n_mr = lax.axis_size("mr")
    devices = n_strip * n_mr
    orders, k_count, lats, _ = wigner.shape
    m_total = orders * devices
    phi_total = 2 * m_total
    psi_count = 2 * k_count - 1
    sizes = (
        base_index.shape[0] // devices,
        phi_total,
        lats,
        psi_count,
        lats // n_mr,
        phi_total // n_strip,
        1.0 / math.sqrt(m_total * k_count),
    )
    chips = n_mr // 2
    strip_at = lax.axis_index("strip")
    mr_at = lax.axis_index("mr")

    shape = (2, chips, n_strip, 2, orders)
    index = lambda axis: lax.broadcasted_iota(jnp.int32, shape, axis)
    from_strip = (strip_at - index(2)) % n_strip
    from_mr = 2 * ((mr_at // 2 - index(1)) % chips) + (mr_at % 2 + index(0)) % 2
    order = (from_strip * n_mr + from_mr) * orders + index(4)
    order = order.reshape(-1).astype(jnp.float32)
    quarter = (0.25 * index(3)).reshape(-1).astype(jnp.float32)
    phases = sample_weights(
        base_index, interp_weights, live_counts, order, quarter, sizes, n_mr, k_count
    )

    mine = local_coef(alm, beam, wigner)
    column = [mine] + [
        lax.ppermute(mine, "strip", [(i, (i + d) % n_strip) for i in range(n_strip)])
        for d in range(1, n_strip)
    ]
    column = jnp.concatenate(column, axis=0)
    plane = [column] + [
        lax.ppermute(column, "mr", [(i, (i + 2 * d) % n_mr) for i in range(n_mr)])
        for d in range(1, chips)
    ]
    other = [lax.ppermute(part, "mr", [(i, i ^ 1) for i in range(n_mr)]) for part in plane]
    return sample(phases, plane + other).reshape(-1)


def solution(mesh):
    placed = (
        P(None, ("strip", "mr"), None),
        P(),
        P(("strip", "mr"), None, None, None),
        P(("strip", "mr")),
        P(None, ("strip", "mr")),
        P(("strip", "mr"), None),
    )
    return jax.shard_map(
        on_device, mesh=mesh, in_specs=placed, out_specs=P(("strip", "mr")), check_vma=False
    )
```

time: 91.6 us -> 36.4 us (0.40)
  waiting for transfers between devices: 23.4 us -> 3.99 us
  between operations: 13.7 us -> 0.15 us
  matrix products: 13.4 us -> 0 us
  blocking collectives: 13.3 us -> 0 us
  Pallas kernels: 0 us -> 12.6 us
  starting transfers between devices: 15.7 us -> 11.6 us
  other arithmetic: 3.78 us -> 0.14 us
    reduce_scatter x1 -> x0, waiting for transfers between devices: 16.3 us -> none  [on_device(): lax.psum_scatter(phi_sum(cos_table, sin_table, coef), 'strip', scatter_di...]
    dot_general x7 -> x0, matrix products: 13.4 us -> none  [the longest x1 6.85 us: on_device(): jnp.einsum('cmkl,mkrl->cmkr', mixed, wigner, preferred_element_type=jnp.f...]
    all_to_all x1 -> x0, blocking collectives: 13.3 us -> none  [on_device(): lax.all_to_all(values, ('strip', 'mr'), split_axis=0, concat_axis=0, tile...]
    pallas_call x0 -> x3, Pallas kernels: none -> 12.6 us  [the longest x1 8.29 us: local_coef(): pl.pallas_call(coef_kernel, out_shape=jax.ShapeDtypeStruct((2 * orders, k...]
    all_to_all x2 -> x0, starting transfers between devices: 9.14 us -> none  [the longest x1 5.17 us: on_device(): coef = lax.all_to_all(coef, 'mr', split_axis=3, concat_axis=1, tiled=True)]
    unnamed x8 -> x16, local copies, waits for them, and re-layouts: 1.11 us -> 6.66 us
    ppermute x4 -> x10, starting transfers between devices: 6.51 us -> 11.6 us  [the longest x3 7.01 us: on_device(): lax.ppermute(mine, 'strip', [(i, (i + d) % n_strip) for i in range(n_stri...]
    all_to_all x2 -> x0, waiting for transfers between devices: 4.32 us -> none  [the longest x1 3.3 us: on_device(): coef = lax.all_to_all(coef, 'mr', split_axis=3, concat_axis=1, tiled=True)]
  transfers between devices with their start and end apart: 7 -> 10, of which waited for: 5 -> 4; matrix products, arithmetic and copies ran while one was open for 14% -> 3% of each run, Pallas kernels for 0% -> 9%
where the time goes in v1:
time: 36.4 us; the launch traced here: 36.1 us
  Pallas kernels  12.6 us (35%)
  starting transfers between devices  11.6 us (32%)
  local copies, waits for them, and re-layouts  7.67 us (21%)
  waiting for transfers between devices  3.99 us (11%)
    pallas_call x1, Pallas kernels, local_coef(): pl.pallas_call(coef_kernel, out_shape=jax.ShapeDtypeStruct((2 * orders, k...  8.29 us
    ppermute x3, starting transfers between devices, on_device(): lax.ppermute(mine, 'strip', [(i, (i + d) % n_strip) for i in range(n_stri...  7.01 us
    unnamed x16, local copies, waits for them, and re-layouts  6.66 us
    ppermute x3, starting transfers between devices, on_device(): lax.ppermute(column, 'mr', [(i, (i + 2 * d) % n_mr) for i in range(n_mr)])  4.5 us
    pallas_call x1, Pallas kernels, sample_weights(): pl.pallas_call(functools.partial(weights_kernel, sizes), grid=(slots // b...  3.12 us
    ppermute x3, waiting for transfers between devices, on_device(): lax.ppermute(column, 'mr', [(i, (i + 2 * d) % n_mr) for i in range(n_mr)])  2.7 us
    ppermute x3, waiting for transfers between devices, on_device(): lax.ppermute(mine, 'strip', [(i, (i + d) % n_strip) for i in range(n_stri...  1.28 us
    pallas_call x1, Pallas kernels, sample(): pl.pallas_call(sample_kernel, grid=(slots // block,), out_shape=jax.Shape...  1.19 us
  transfers between devices with their start and end apart: 10, of which 4 were waited for; matrix products, arithmetic and copies ran while one was open for 3% of the time, Pallas kernels for 9%

profile of v1, /device:TPU:0, one launch (start us, length us, event | category | flops | bytes accessed | tf_op | source)
XLA Modules:
  0.0 36.1 jit_solution(6264802266025274822)
XLA Ops:
  0.0 0.0 copy-start.7
  0.0 0.0 copy-start.4
  0.0 0.0 copy-start
  0.0 4.9 %copy-done = bf16[8,13,32,2048]{3,2,1,0:T(8,128)(2,1)S(1)} copy-done((bf16[8,13,32,2048]{3,2,1,0:T(8,128)(2,1)S(1)}, bf16[8,13,32,2048]{3,2,1,0:T(8,128)(2,1)}, u32[]{:S(2)}) %copy-start) | copy-done | bytes 13631512
  4.9 0.0 copy-start.1
  4.9 0.9 %copy-done.1 = f32[13,2048]{1,0:T(8,128)S(1)} copy-done((f32[13,2048]{1,0:T(8,128)S(1)}, f32[13,2048]{1,0:T(8,128)}, u32[]{:S(2)}) %copy-start.1) | copy-done | bytes 106520
  5.8 0.0 copy-start.2
  5.8 0.8 %copy-done.2 = bf16[2,8,2048]{2,1,0:T(8,128)(2,1)S(1)} copy-done((bf16[2,8,2048]{2,1,0:T(8,128)(2,1)S(1)}, bf16[2,8,2048]{2,1,0:T(8,128)(2,1)}, u32[]{:S(2)}) %copy-start.2) | copy-done | bytes 65560
  6.7 8.3 %coef.1 = bf16[16,416]{1,0:T(8,128)(2,1)S(1)} custom-call(bf16[2,8,2048]{2,1,0:T(8,128)(2,1)S(1)} %copy-done.2, f32[13,2048]{1,0:T(8,128)S(1)} %copy-done.1, bf16[8,416,2048]{2,1,0:T(8,128)(2,1)S(1)} %bitcast.3), custom_call_target="tpu_custom_call" | custom-call | flops 27262976 | bytes 13631488 | tf_op jit(solution)/shard_map/coef/pallas_call | solution.py:53
  15.0 3.1 %collective-permute-start = (bf16[16,416]{1,0:T(8,128)(2,1)S(1)}, bf16[16,416]{1,0:T(8,128)(2,1)S(1)}, u32[]{:S(2)}, u32[]{:S(2)}) collective-permute-start(bf16[16,416]{1,0:T(8,128)(2,1)S(1)} %coef.1), channel_id=1, source_target_pairs={{0,8},{8,16},{16,24},{24,0},{1,9},{9,17},{17,25},{25,1},{2,10},{10... | collective-permute-start | bytes 39944 | tf_op jit(solution)/shard_map/ppermute | solution.py:251
  18.0 2.6 %collective-permute-start.1 = (bf16[16,416]{1,0:T(8,128)(2,1)S(1)}, bf16[16,416]{1,0:T(8,128)(2,1)S(1)}, u32[]{:S(2)}, u32[]{:S(2)}) collective-permute-start(bf16[16,416]{1,0:T(8,128)(2,1)S(1)} %coef.1), channel_id=1, source_target_pairs={{0,16},{8,24},{16,0},{24,8},{1,17},{9,25},{17,1},{25,9},{2,18},{10... | collective-permute-start | bytes 39944 | tf_op jit(solution)/shard_map/ppermute | solution.py:251
  20.6 1.3 %collective-permute-start.2 = (bf16[16,416]{1,0:T(8,128)(2,1)S(1)}, bf16[16,416]{1,0:T(8,128)(2,1)S(1)}, u32[]{:S(2)}, u32[]{:S(2)}) collective-permute-start(bf16[16,416]{1,0:T(8,128)(2,1)S(1)} %coef.1), channel_id=1, source_target_pairs={{0,24},{8,0},{16,8},{24,16},{1,25},{9,1},{17,9},{25,17},{2,26},{10... | collective-permute-start | bytes 39944 | tf_op jit(solution)/shard_map/ppermute | solution.py:251
  22.0 0.1 iota.46
  22.0 0.1 iota.47
  22.2 0.1 iota.43
  22.3 0.1 iota.44
  22.4 0.1 iota.40
  22.4 0.1 iota.41
  22.6 0.1 iota.49
  22.7 0.1 iota.51
  22.8 0.1 mul.59
  22.9 0.1 pad.6.clone
  23.0 0.1 pad.7.clone
  23.1 0.0 collective-permute-done
  23.1 0.0 collective-permute-done.1
  23.1 1.3 %collective-permute-done.2 = bf16[16,416]{1,0:T(8,128)(2,1)S(1)} collective-permute-done((bf16[16,416]{1,0:T(8,128)(2,1)S(1)}, bf16[16,416]{1,0:T(8,128)(2,1)S(1)}, u32[]{:S(2)}, u32[]{:S(2)}) %collective-permute-start.2) | collective-permute-done | bytes 13344 | tf_op jit(solution)/shard_map/ppermute | solution.py:251
  24.4 1.5 %collective-permute-start.3 = (bf16[64,416]{1,0:T(8,128)(2,1)S(1)}, bf16[64,416]{1,0:T(8,128)(2,1)S(1)}, u32[]{:S(2)}, u32[]{:S(2)}) collective-permute-start(bf16[64,416]{1,0:T(8,128)(2,1)S(1)} %pad_maximum_fusion.refs_0_), channel_id=1, source_target_pairs={{0,2},{1,3},{2,4},{3,5},{4,6},{5,7},{6,0},{7,1},{8,10},{9,11},{10,... | collective-permute-start | bytes 159752 | tf_op jit(solution)/shard_map/ppermute | solution.py:256
  25.9 1.5 %collective-permute-start.4 = (bf16[64,416]{1,0:T(8,128)(2,1)S(1)}, bf16[64,416]{1,0:T(8,128)(2,1)S(1)}, u32[]{:S(2)}, u32[]{:S(2)}) collective-permute-start(bf16[64,416]{1,0:T(8,128)(2,1)S(1)} %pad_maximum_fusion.refs_0_), channel_id=1, source_target_pairs={{0,4},{1,5},{2,6},{3,7},{4,0},{5,1},{6,2},{7,3},{8,12},{9,13},{10,... | collective-permute-start | bytes 159752 | tf_op jit(solution)/shard_map/ppermute | solution.py:256
  27.4 1.4 %collective-permute-start.5 = (bf16[64,416]{1,0:T(8,128)(2,1)S(1)}, bf16[64,416]{1,0:T(8,128)(2,1)S(1)}, u32[]{:S(2)}, u32[]{:S(2)}) collective-permute-start(bf16[64,416]{1,0:T(8,128)(2,1)S(1)} %pad_maximum_fusion.refs_0_), channel_id=1, source_target_pairs={{0,6},{1,7},{2,0},{3,1},{4,2},{5,3},{6,4},{7,5},{8,14},{9,15},{10,... | collective-permute-start | bytes 159752 | tf_op jit(solution)/shard_map/ppermute | solution.py:256
  28.9 0.1 maximum_maximum_fusion.order_ref
  28.9 0.0 copy-done.7
  28.9 0.0 collective-permute-start.6
  29.0 0.6 %collective-permute-done.3.refs_1_ = bf16[64,416]{1,0:T(8,128)(2,1)S(1)} collective-permute-done((bf16[64,416]{1,0:T(8,128)(2,1)S(1)}, bf16[64,416]{1,0:T(8,128)(2,1)S(1)}, u32[]{:S(2)}, u32[]{:S(2)}) %collective-permute-start.3) | collective-permute-done | bytes 53280 | tf_op jit(solution)/shard_map/ppermute | solution.py:256
  29.6 0.0 collective-permute-start.7
  29.6 0.7 %collective-permute-done.4.refs_2_ = bf16[64,416]{1,0:T(8,128)(2,1)S(1)} collective-permute-done((bf16[64,416]{1,0:T(8,128)(2,1)S(1)}, bf16[64,416]{1,0:T(8,128)(2,1)S(1)}, u32[]{:S(2)}, u32[]{:S(2)}) %collective-permute-start.4) | collective-permute-done | bytes 53280 | tf_op jit(solution)/shard_map/ppermute | solution.py:256
  30.3 0.0 collective-permute-start.8
  30.3 1.4 %collective-permute-done.5.refs_3_ = bf16[64,416]{1,0:T(8,128)(2,1)S(1)} collective-permute-done((bf16[64,416]{1,0:T(8,128)(2,1)S(1)}, bf16[64,416]{1,0:T(8,128)(2,1)S(1)}, u32[]{:S(2)}, u32[]{:S(2)}) %collective-permute-start.5) | collective-permute-done | bytes 53280 | tf_op jit(solution)/shard_map/ppermute | solution.py:256
  31.7 0.0 collective-permute-start.9
  31.7 0.0 copy-done.5
  31.7 0.0 copy-done.6
  31.7 0.0 copy-done.4
  31.7 0.0 copy-done.3
  31.8 3.1 %weights.1 = (bf16[256,512]{1,0:T(8,128)(2,1)S(1)}, bf16[256,512]{1,0:T(8,128)(2,1)S(1)}, f32[256,416]{1,0:T(8,128)S(1)}, f32[256,416]{1,0:T(8,128)S(1)}) custom-call(f32[32,256]{1,0:T(8,128)S(1)} %pad_maximum_fusion.1.slots_ref, s32[1,32]{1,0:T(1,128)S(1)} %copy-done.4, f32[8,512]{1,0:T(8,128)S(1)} %maximum_maximum_fusion.order_ref, f32[8,416]{1,0:T(8,128)S(1)} %copy-done.3), custom_call_target="tpu_custom_call" | custom-call | flops 14254080 | bytes 1048576 | tf_op jit(solution)/shard_map/weights/pallas_call | solution.py:155
  34.9 0.0 collective-permute-done.6.refs_4_
  34.9 0.0 collective-permute-done.7.refs_5_
  34.9 0.0 collective-permute-done.8.refs_6_
  34.9 0.0 collective-permute-done.9.refs_7_
  34.9 1.2 %sample.1 = f32[1,256]{1,0:T(1,128)} custom-call(bf16[256,512]{1,0:T(8,128)(2,1)S(1)} %get-tuple-element.9.re_ref, bf16[256,512]{1,0:T(8,128)(2,1)S(1)} %get-tuple-element.10.im_ref, f32[256,416]{1,0:T(8,128)S(1)} %get-tuple-element.11.tail_re_ref, f32[256,416]{1,0:T(8,128)S(1)} %get-tuple-element.12.tail_im_ref, ...), custom_call_target="tpu_custom_call" | custom-call | flops 218103808 | bytes 1048576 | tf_op jit(solution)/shard_map/sample/pallas_call | solution.py:201
  (14 shorter events, 0.1 us)
Async XLA Ops:
  0.0 28.9 %copy-start.7 = (s32[256]{0:T(256)S(1)}, s32[256]{0:T(256)}, u32[]{:S(2)}) copy-start(s32[256]{0:T(256)} %param.11) | copy-start | bytes 3076
  0.0 31.7 %copy-start.4 = (s32[1,32]{1,0:T(1,128)S(1)}, s32[1,32]{1,0:T(1,128)}, u32[]{:S(2)}) copy-start(s32[1,32]{1,0:T(1,128)} %counts_ref.1) | copy-start | bytes 388
  0.0 4.9 %copy-start = (bf16[8,13,32,2048]{3,2,1,0:T(8,128)(2,1)S(1)}, bf16[8,13,32,2048]{3,2,1,0:T(8,128)(2,1)}, u32[]{:S(2)}) copy-start(bf16[8,13,32,2048]{3,2,1,0:T(8,128)(2,1)} %param.10) | copy-start | bytes 40894468
  4.9 0.9 %copy-start.1 = (f32[13,2048]{1,0:T(8,128)S(1)}, f32[13,2048]{1,0:T(8,128)}, u32[]{:S(2)}) copy-start(f32[13,2048]{1,0:T(8,128)} %beam_hbm.1) | copy-start | bytes 319492
  5.8 0.8 %copy-start.2 = (bf16[2,8,2048]{2,1,0:T(8,128)(2,1)S(1)}, bf16[2,8,2048]{2,1,0:T(8,128)(2,1)}, u32[]{:S(2)}) copy-start(bf16[2,8,2048]{2,1,0:T(8,128)(2,1)} %alm_hbm.1) | copy-start | bytes 196612
  6.7 25.1 %copy-start.5 = (f32[19,256]{1,0:T(8,128)S(1)}, f32[19,256]{1,0:T(8,128)}, u32[]{:S(2)}) copy-start(f32[19,256]{1,0:T(8,128)} %constant.68.clone) | copy-start | bytes 58372
  6.7 25.1 %copy-start.6 = (f32[12,256]{1,0:T(8,128)S(1)}, f32[12,256]{1,0:T(8,128)}, u32[]{:S(2)}) copy-start(f32[12,256]{1,0:T(8,128)} %param.12) | copy-start | bytes 36868
  6.7 25.1 %copy-start.3 = (f32[8,416]{1,0:T(8,128)S(1)}, f32[8,416]{1,0:T(8,128)}, u32[]{:S(2)}) copy-start(f32[8,416]{1,0:T(8,128)} %constant.69.clone.lane_ref) | copy-start | bytes 39940
  15.0 8.1 %collective-permute-start = (bf16[16,416]{1,0:T(8,128)(2,1)S(1)}, bf16[16,416]{1,0:T(8,128)(2,1)S(1)}, u32[]{:S(2)}, u32[]{:S(2)}) collective-permute-start(bf16[16,416]{1,0:T(8,128)(2,1)S(1)} %coef.1), channel_id=1, source_target_pairs={{0,8},{8,16},{16,24},{24,0},{1,9},{9,17},{17,25},{25,1},{2,10},{10... | collective-permute-start | bytes 39944 | tf_op jit(solution)/shard_map/ppermute | solution.py:251
  18.0 5.0 %collective-permute-start.1 = (bf16[16,416]{1,0:T(8,128)(2,1)S(1)}, bf16[16,416]{1,0:T(8,128)(2,1)S(1)}, u32[]{:S(2)}, u32[]{:S(2)}) collective-permute-start(bf16[16,416]{1,0:T(8,128)(2,1)S(1)} %coef.1), channel_id=1, source_target_pairs={{0,16},{8,24},{16,0},{24,8},{1,17},{9,25},{17,1},{25,9},{2,18},{10... | collective-permute-start | bytes 39944 | tf_op jit(solution)/shard_map/ppermute | solution.py:251
  20.6 3.7 %collective-permute-start.2 = (bf16[16,416]{1,0:T(8,128)(2,1)S(1)}, bf16[16,416]{1,0:T(8,128)(2,1)S(1)}, u32[]{:S(2)}, u32[]{:S(2)}) collective-permute-start(bf16[16,416]{1,0:T(8,128)(2,1)S(1)} %coef.1), channel_id=1, source_target_pairs={{0,24},{8,0},{16,8},{24,16},{1,25},{9,1},{17,9},{25,17},{2,26},{10... | collective-permute-start | bytes 39944 | tf_op jit(solution)/shard_map/ppermute | solution.py:251
  24.4 5.2 %collective-permute-start.3 = (bf16[64,416]{1,0:T(8,128)(2,1)S(1)}, bf16[64,416]{1,0:T(8,128)(2,1)S(1)}, u32[]{:S(2)}, u32[]{:S(2)}) collective-permute-start(bf16[64,416]{1,0:T(8,128)(2,1)S(1)} %pad_maximum_fusion.refs_0_), channel_id=1, source_target_pairs={{0,2},{1,3},{2,4},{3,5},{4,6},{5,7},{6,0},{7,1},{8,10},{9,11},{10,... | collective-permute-start | bytes 159752 | tf_op jit(solution)/shard_map/ppermute | solution.py:256
  25.9 4.4 %collective-permute-start.4 = (bf16[64,416]{1,0:T(8,128)(2,1)S(1)}, bf16[64,416]{1,0:T(8,128)(2,1)S(1)}, u32[]{:S(2)}, u32[]{:S(2)}) collective-permute-start(bf16[64,416]{1,0:T(8,128)(2,1)S(1)} %pad_maximum_fusion.refs_0_), channel_id=1, source_target_pairs={{0,4},{1,5},{2,6},{3,7},{4,0},{5,1},{6,2},{7,3},{8,12},{9,13},{10,... | collective-permute-start | bytes 159752 | tf_op jit(solution)/shard_map/ppermute | solution.py:256
  27.4 4.3 %collective-permute-start.5 = (bf16[64,416]{1,0:T(8,128)(2,1)S(1)}, bf16[64,416]{1,0:T(8,128)(2,1)S(1)}, u32[]{:S(2)}, u32[]{:S(2)}) collective-permute-start(bf16[64,416]{1,0:T(8,128)(2,1)S(1)} %pad_maximum_fusion.refs_0_), channel_id=1, source_target_pairs={{0,6},{1,7},{2,0},{3,1},{4,2},{5,3},{6,4},{7,5},{8,14},{9,15},{10,... | collective-permute-start | bytes 159752 | tf_op jit(solution)/shard_map/ppermute | solution.py:256
  28.9 5.9 %collective-permute-start.6 = (bf16[64,416]{1,0:T(8,128)(2,1)S(1)}, bf16[64,416]{1,0:T(8,128)(2,1)S(1)}, u32[]{:S(2)}, u32[]{:S(2)}) collective-permute-start(bf16[64,416]{1,0:T(8,128)(2,1)S(1)} %pad_maximum_fusion.refs_0_), channel_id=1, source_target_pairs={{0,1},{1,0},{2,3},{3,2},{4,5},{5,4},{6,7},{7,6},{8,9},{9,8},{10,11... | collective-permute-start | bytes 159752 | tf_op jit(solution)/shard_map/ppermute | solution.py:259
  29.6 5.3 %collective-permute-start.7 = (bf16[64,416]{1,0:T(8,128)(2,1)S(1)}, bf16[64,416]{1,0:T(8,128)(2,1)S(1)}, u32[]{:S(2)}, u32[]{:S(2)}) collective-permute-start(bf16[64,416]{1,0:T(8,128)(2,1)S(1)} %collective-permute-done.3.refs_1_), channel_id=1, source_target_pairs={{0,1},{1,0},{2,3},{3,2},{4,5},{5,4},{6,7},{7,6},{8,9},{9,8},{10,11... | collective-permute-start | bytes 159752 | tf_op jit(solution)/shard_map/ppermute | solution.py:259
  30.3 4.6 %collective-permute-start.8 = (bf16[64,416]{1,0:T(8,128)(2,1)S(1)}, bf16[64,416]{1,0:T(8,128)(2,1)S(1)}, u32[]{:S(2)}, u32[]{:S(2)}) collective-permute-start(bf16[64,416]{1,0:T(8,128)(2,1)S(1)} %collective-permute-done.4.refs_2_), channel_id=1, source_target_pairs={{0,1},{1,0},{2,3},{3,2},{4,5},{5,4},{6,7},{7,6},{8,9},{9,8},{10,11... | collective-permute-start | bytes 159752 | tf_op jit(solution)/shard_map/ppermute | solution.py:259
  31.7 3.2 %collective-permute-start.9 = (bf16[64,416]{1,0:T(8,128)(2,1)S(1)}, bf16[64,416]{1,0:T(8,128)(2,1)S(1)}, u32[]{:S(2)}, u32[]{:S(2)}) collective-permute-start(bf16[64,416]{1,0:T(8,128)(2,1)S(1)} %collective-permute-done.5.refs_3_), channel_id=1, source_target_pairs={{0,1},{1,0},{2,3},{3,2},{4,5},{5,4},{6,7},{7,6},{8,9},{9,8},{10,11... | collective-permute-start | bytes 159752 | tf_op jit(solution)/shard_map/ppermute | solution.py:259

commit v2 on v1

v2 whole, which is shorter than its diff:
```python
import functools
import math

import jax
import jax.numpy as jnp
import numpy as np
from jax import lax
from jax.experimental import pallas as pl
from jax.experimental.pallas import tpu as pltpu
from jax.sharding import PartitionSpec as P

NT = (((1,), (1,)), ((), ()))
VMEM = pl.BlockSpec(memory_space=pltpu.VMEM)


def cos_sin_turns(x):
    x = x - jnp.round(x)
    u = x * x
    cos = jnp.zeros_like(x)
    sin = jnp.zeros_like(x)
    for n in range(9, -1, -1):
        cos = cos * u + (-1) ** n * (2 * math.pi) ** (2 * n) / math.factorial(2 * n)
        sin = sin * u + (-1) ** n * (2 * math.pi) ** (2 * n + 1) / math.factorial(2 * n + 1)
    return cos, sin * x


def remainder(x, n):
    return x - n * jnp.floor((x + 0.5) * (1.0 / n))


def tap_phases(taps, turns):
    total_re = taps[0] * jnp.ones_like(turns)
    total_im = jnp.zeros_like(total_re)
    for tap in range(1, 4):
        cos, sin = cos_sin_turns(tap * turns)
        total_re = total_re + taps[tap] * cos
        total_im = total_im + taps[tap] * sin
    return total_re, total_im


def turned(turns, values):
    cos, sin = cos_sin_turns(turns)
    return cos * values[0] - sin * values[1], sin * values[0] + cos * values[1]


def slot_weights(sizes, cols, counts, order, quarter, k_lane, r_lane):
    phi_total, lats, psi_count, lat_dev, phi_dev, scale = sizes
    col = lambda i: cols[:, i : i + 1]
    base, slot_e, strip_phi, mr_lat, of_slot = (col(i) for i in range(12, 17))
    dest = lax.broadcasted_iota(jnp.int32, (cols.shape[0], counts.shape[1]), 1)
    used = jnp.where(dest.astype(jnp.float32) == of_slot, counts, 0.0)
    live = (slot_e < jnp.sum(used, axis=1, keepdims=True)).astype(jnp.float32)
    rest = jnp.floor((base + 0.5) * (1.0 / (phi_dev + 1)))
    phi_base = base - rest * (phi_dev + 1)
    psi_base = jnp.floor((rest + 0.5) * (1.0 / (lat_dev + 1)))
    lat_base = rest - psi_base * (lat_dev + 1)
    phases = turned(
        (strip_phi + phi_base - 2.0) * (order * (1.0 / phi_total)) + quarter,
        tap_phases([col(4 + b) for b in range(4)], order * (1.0 / phi_total)),
    )
    across = jnp.zeros((cols.shape[0], k_lane.shape[1]), jnp.float32)
    for a in range(4):
        row = remainder(mr_lat + lat_base - 2.0 + a, lats)
        across = across + jnp.where(row == r_lane, col(a) * live, 0.0)
    across = across * scale
    tail_re, tail_im = turned(
        remainder(psi_base * k_lane, psi_count) * (1.0 / psi_count),
        tap_phases([col(8 + c) for c in range(4)], k_lane * (1.0 / psi_count)),
    )
    return phases + (tail_re * across, -tail_im * across)


def coef_kernel(
    sizes,
    alm_hbm,
    beam_hbm,
    table_hbm,
    slots_ref,
    counts_ref,
    from_ref,
    lane_ref,
    out_ref,
    re_ref,
    im_ref,
    tail_re_ref,
    tail_im_ref,
    alm,
    beam,
    table,
    mixed,
    rows,
    cols,
    sems,
):
    orders, beam_rows, ells = table.shape
    k_count = beam.shape[0]
    lats = beam_rows // k_count
    k_pad = mixed.shape[1] // 2
    small = [
        pltpu.make_async_copy(alm_hbm, alm, sems.at[orders]),
        pltpu.make_async_copy(beam_hbm, beam, sems.at[orders + 1]),
    ]
    big = [
        pltpu.make_async_copy(table_hbm.at[m], table.at[m], sems.at[m]) for m in range(orders)
    ]
    for copy in small + big:
        copy.start()
    mixed[...] = jnp.zeros_like(mixed)
    cols[...] = slots_ref[...].T
    strip_at, mr_at = lax.axis_index("strip"), lax.axis_index("mr")
    source = (from_ref[0:1] ^ strip_at) * lax.axis_size("mr") + (from_ref[1:2] ^ mr_at)
    order = (source * orders + from_ref[2:3]).astype(jnp.float32)
    quarter = 0.25 * from_ref[3:4].astype(jnp.float32)
    counts = counts_ref[...].astype(jnp.float32)
    block = cols.shape[0] // orders

    def mix(m):
        for c in range(2):
            product = alm[c, m, :].astype(jnp.float32)[None, :] * beam[...]
            mixed[m, c * k_pad : c * k_pad + k_count, :] = product.astype(jnp.bfloat16)

    for copy in small:
        copy.wait()
    mix(0)
    for m in range(orders):
        big[m].wait()
        y = lax.dot_general(mixed[m], table[m], NT, preferred_element_type=jnp.float32)
        of_row = lax.broadcasted_iota(jnp.int32, y.shape, 0) % k_pad
        of_lane = lax.broadcasted_iota(jnp.int32, y.shape, 1) // lats
        y = jnp.where(of_row == of_lane, y, 0.0)
        for c in range(2):
            total = jnp.sum(y[c * k_pad : (c + 1) * k_pad], axis=0, keepdims=True)
            rows[c * orders + m : c * orders + m + 1, :] = total
        here = slice(m * block, (m + 1) * block)
        re, im, tail_re, tail_im = slot_weights(
            sizes, cols[here], counts, order, quarter, lane_ref[0:1], lane_ref[1:2]
        )
        re_ref[here] = re.astype(jnp.bfloat16)
        im_ref[here] = im.astype(jnp.bfloat16)
        tail_re_ref[here] = tail_re
        tail_im_ref[here] = tail_im
        if m + 1 < orders:
            mix(m + 1)
    out_ref[...] = rows[...].astype(jnp.bfloat16)


def local_part(alm, beam, wigner, base_index, interp_weights, live_counts, n_strip, n_mr):
    orders, k_count, lats, ells = wigner.shape
    k_pad = -(-k_count // 8) * 8
    lanes = k_count * lats
    slots = base_index.shape[0]
    devices = n_strip * n_mr
    width = 2 * orders * devices
    m_total = orders * devices
    phi_total = 2 * m_total
    lat_dev, phi_dev = lats // n_mr, phi_total // n_strip
    scale = 1.0 / math.sqrt(m_total * k_count)
    sizes = (phi_total, lats, 2 * k_count - 1, lat_dev, phi_dev, scale)

    dest = np.arange(slots) // (slots // devices)
    fixed = np.zeros((19, slots), np.float32)
    fixed[0] = np.arange(slots) % (slots // devices)
    fixed[1] = dest // n_mr * phi_dev
    fixed[2] = dest % n_mr * lat_dev
    fixed[3] = dest
    table = jnp.concatenate(
        [interp_weights, base_index[None].astype(jnp.float32), jnp.asarray(fixed)], axis=0
    )
    core, chip, strip, part, m = np.indices((2, n_mr // 2, n_strip, 2, orders)).reshape(5, -1)
    source = np.zeros((8, width), np.int32)
    source[:4] = [strip, 2 * chip + core, m, part]
    lane = np.zeros((8, lanes), np.float32)
    lane[0] = np.arange(lanes) // lats
    lane[1] = np.arange(lanes) % lats
    hbm = pl.BlockSpec(memory_space=pltpu.HBM)
    return pl.pallas_call(
        functools.partial(coef_kernel, sizes),
        out_shape=(
            jax.ShapeDtypeStruct((2 * orders, lanes), jnp.bfloat16),
            jax.ShapeDtypeStruct((slots, width), jnp.bfloat16),
            jax.ShapeDtypeStruct((slots, width), jnp.bfloat16),
            jax.ShapeDtypeStruct((slots, lanes), jnp.float32),
            jax.ShapeDtypeStruct((slots, lanes), jnp.float32),
        ),
        in_specs=[hbm] * 3 + [VMEM] * 4,
        out_specs=(VMEM,) * 5,
        scratch_shapes=[
            pltpu.VMEM((2, orders, ells), jnp.bfloat16),
            pltpu.VMEM((k_count, ells), jnp.float32),
            pltpu.VMEM((orders, lanes, ells), jnp.bfloat16),
            pltpu.VMEM((orders, 2 * k_pad, ells), jnp.bfloat16),
            pltpu.VMEM((2 * orders, lanes), jnp.float32),
            pltpu.VMEM((slots, 32), jnp.float32),
            pltpu.SemaphoreType.DMA((orders + 2,)),
        ],
        compiler_params=pltpu.CompilerParams(vmem_limit_bytes=48 << 20),
        cost_estimate=pl.CostEstimate(
            flops=4 * wigner.size, bytes_accessed=2 * wigner.size, transcendentals=0
        ),
        name="coef",
    )(
        alm,
        beam,
        wigner.reshape(orders, lanes, ells),
        table,
        live_counts,
        jnp.asarray(source),
        jnp.asarray(lane),
    )


def sample_kernel(re_ref, im_ref, tail_re_ref, tail_im_ref, *refs):
    parts, out_ref, coef = refs[:-2], refs[-2], refs[-1]
    start = 0
    for part in parts:
        coef[start : start + part.shape[0], :] = part[...]
        start += part.shape[0]
    real = jnp.dot(re_ref[...], coef[...], preferred_element_type=jnp.float32)
    imag = jnp.dot(im_ref[...], coef[...], preferred_element_type=jnp.float32)
    terms = real * tail_re_ref[...] + imag * tail_im_ref[...]
    lanes = terms.shape[1]
    whole = lanes // 128 * 128
    total = jnp.zeros((1, terms.shape[0]), jnp.float32)
    if whole:
        tiles = [terms[:, i : i + 128] for i in range(0, whole, 128)]
        total = total + jnp.sum(sum(tiles).T, axis=0, keepdims=True)
    if whole < lanes:
        total = total + jnp.sum(terms[:, whole:].T, axis=0, keepdims=True)
    out_ref[...] = total


def sample(phases, parts):
    slots, width = phases[0].shape
    lanes = phases[2].shape[1]
    block = min(slots, 256)
    rows = lambda n: pl.BlockSpec((block, n), lambda i: (i, 0))
    return pl.pallas_call(
        sample_kernel,
        grid=(slots // block,),
        out_shape=jax.ShapeDtypeStruct((1, slots), jnp.float32),
        in_specs=[rows(width), rows(width), rows(lanes), rows(lanes)]
        + [pl.BlockSpec(part.shape, lambda i: (0, 0)) for part in parts],
        out_specs=pl.BlockSpec((1, block), lambda i: (0, i)),
        scratch_shapes=[pltpu.VMEM((width, lanes), jnp.bfloat16)],
        compiler_params=pltpu.CompilerParams(vmem_limit_bytes=32 << 20),
        cost_estimate=pl.CostEstimate(
            flops=4 * slots * width * lanes, bytes_accessed=1 << 20, transcendentals=0
        ),
        name="sample",
    )(*phases, *parts)


def on_device(alm, beam, wigner, base_index, interp_weights, live_counts):
    n_strip = lax.axis_size("strip")
    n_mr = lax.axis_size("mr")
    mine, *phases = local_part(
        alm, beam, wigner, base_index, interp_weights, live_counts, n_strip, n_mr
    )

    def swap(x, axis, d):
        return lax.ppermute(x, axis, [(i, i ^ d) for i in range(lax.axis_size(axis))])

    column = [swap(mine, "strip", d) for d in range(n_strip - 1, 0, -1)][::-1]
    column = jnp.concatenate([mine] + column, axis=0)
    plane = [column] + [swap(column, "mr", d) for d in range(n_mr - 2, 0, -2)][::-1]
    other = [swap(part, "mr", 1) for part in plane]
    return sample(phases, plane + other).reshape(-1)


def solution(mesh):
    placed = (
        P(None, ("strip", "mr"), None),
        P(),
        P(("strip", "mr"), None, None, None),
        P(("strip", "mr")),
        P(None, ("strip", "mr")),
        P(("strip", "mr"), None),
    )
    return jax.shard_map(
        on_device, mesh=mesh, in_specs=placed, out_specs=P(("strip", "mr")), check_vma=False
    )
```

time: 36.4 us -> 33.5 us (0.920)
  waiting for transfers between devices: 3.99 us -> 8.96 us
  local copies, waits for them, and re-layouts: 7.67 us -> 3.84 us
  Pallas kernels: 12.6 us -> 9.51 us
  starting transfers between devices: 11.6 us -> 9.32 us
  other arithmetic: 0.14 us -> 1.43 us
    ppermute x10, waiting for transfers between devices: 3.99 us -> 8.96 us  [swap(): lax.ppermute(x, axis, [(i, i ^ d) for i in range(lax.axis_size(axis))])]
    pallas_call x2 -> x1, Pallas kernels: 11.4 us -> 8.39 us  [local_part(): pl.pallas_call(functools.partial(coef_kernel, sizes), out_shape=(jax.Shap...]
    unnamed x16 -> x13, local copies, waits for them, and re-layouts: 6.66 us -> 3.83 us
    ppermute x10, starting transfers between devices: 11.6 us -> 9.32 us  [swap(): lax.ppermute(x, axis, [(i, i ^ d) for i in range(lax.axis_size(axis))])]
    iota x9 -> x0, local copies, waits for them, and re-layouts: 0.75 us -> none  [on_device(): index = lambda axis: lax.broadcasted_iota(jnp.int32, shape, axis)]
    concatenate x2 -> x1, other arithmetic: 0.02 us -> 0.75 us  [local_part(): jnp.concatenate([interp_weights, base_index[None].astype(jnp.float32), jn...]
    convert_element_type x2 -> x1, other arithmetic: 0.03 us -> 0.68 us  [local_part(): base_index[None].astype(jnp.float32)]
  transfers between devices with their start and end apart: 10 -> 10, of which waited for: 4 -> 7; matrix products, arithmetic and copies ran while one was open for 3% -> 0% of each run, Pallas kernels for 9% -> 0%
where the time goes in v2:
time: 33.5 us; the launch traced here: 33.1 us
  Pallas kernels  9.51 us (28%)
  starting transfers between devices  9.32 us (28%)
  waiting for transfers between devices  8.96 us (27%)
  local copies, waits for them, and re-layouts  3.84 us (11%)
  other arithmetic  1.43 us (4%)
    ppermute x10, starting transfers between devices, swap(): lax.ppermute(x, axis, [(i, i ^ d) for i in range(lax.axis_size(axis))])  9.32 us
    ppermute x10, waiting for transfers between devices, swap(): lax.ppermute(x, axis, [(i, i ^ d) for i in range(lax.axis_size(axis))])  8.96 us
    pallas_call x1, Pallas kernels, local_part(): pl.pallas_call(functools.partial(coef_kernel, sizes), out_shape=(jax.Shap...  8.39 us
    unnamed x13, local copies, waits for them, and re-layouts  3.83 us
    pallas_call x1, Pallas kernels, sample(): pl.pallas_call(sample_kernel, grid=(slots // block,), out_shape=jax.Shape...  1.12 us
    concatenate x1, other arithmetic, local_part(): jnp.concatenate([interp_weights, base_index[None].astype(jnp.float32), jn...  0.75 us
    convert_element_type x1, other arithmetic, local_part(): base_index[None].astype(jnp.float32)  0.68 us
  transfers between devices with their start and end apart: 10, of which 7 were waited for; matrix products, arithmetic and copies ran while one was open for 0% of the time, Pallas kernels for 0%

profile of v2, /device:TPU:0, one launch (start us, length us, event | category | flops | bytes accessed | tf_op | source)
XLA Modules:
  0.0 33.1 jit_solution(11850315512263347859)
XLA Ops:
  0.0 0.7 %convert_element_type.6 = f32[256]{0:T(256)S(1)} convert(s32[256]{0:T(256)} %param.12) | non-fusion elementwise | flops 256 | bytes 2048 | tf_op jit(solution)/shard_map/convert_element_type | solution.py:167
  0.7 0.7 %pad_maximum_fusion.slots_ref = f32[32,256]{1,0:T(8,128)S(1)} fusion(f32[19,256]{1,0:T(8,128)} %constant.6.clone, f32[1,256]{1,0:T(1,128)S(1)} %bitcast.4, f32[12,256]{1,0:T(8,128)} %param.13), kind=kLoop, calls=%fused_computation | loop fusion | flops 16384 | bytes 65536 | tf_op jit(solution)/shard_map/concatenate | solution.py:166
  1.4 0.0 copy-start
  1.4 0.9 %copy-done = f32[13,2048]{1,0:T(8,128)S(1)} copy-done((f32[13,2048]{1,0:T(8,128)S(1)}, f32[13,2048]{1,0:T(8,128)}, u32[]{:S(2)}) %copy-start) | copy-done | bytes 106520
  2.3 0.0 copy-start.1
  2.3 0.8 %copy-done.1 = bf16[2,8,2048]{2,1,0:T(8,128)(2,1)S(1)} copy-done((bf16[2,8,2048]{2,1,0:T(8,128)(2,1)S(1)}, bf16[2,8,2048]{2,1,0:T(8,128)(2,1)}, u32[]{:S(2)}) %copy-start.1) | copy-done | bytes 65560
  3.2 0.0 copy-start.2
  3.2 0.7 %copy-done.2 = f32[8,416]{1,0:T(8,128)S(1)} copy-done((f32[8,416]{1,0:T(8,128)S(1)}, f32[8,416]{1,0:T(8,128)}, u32[]{:S(2)}) %copy-start.2) | copy-done | bytes 13336
  3.9 0.0 copy-start.3
  3.9 0.7 %copy-done.3 = s32[8,512]{1,0:T(8,128)S(1)} copy-done((s32[8,512]{1,0:T(8,128)S(1)}, s32[8,512]{1,0:T(8,128)}, u32[]{:S(2)}) %copy-start.3) | copy-done | bytes 16408
  4.6 0.0 copy-start.4
  4.6 0.7 %copy-done.4 = s32[1,32]{1,0:T(1,128)S(1)} copy-done((s32[1,32]{1,0:T(1,128)S(1)}, s32[1,32]{1,0:T(1,128)}, u32[]{:S(2)}) %copy-start.4) | copy-done | bytes 152
  5.3 8.4 %coef.1 = (bf16[16,416]{1,0:T(8,128)(2,1)S(1)}, bf16[256,512]{1,0:T(8,128)(2,1)S(1)}, bf16[256,512]{1,0:T(8,128)(2,1)S(1)}, f32[256,416]{1,0:T(8,128)S(1)}, f32[256,416]{1,0:T(8,128)S(1)}) custom-call(bf16[2,8,2048]{2,1,0:T(8,128)(2,1)S(1)} %copy-done.1, f32[13,2048]{1,0:T(8,128)S(1)} %copy-done, bf16[8,416,2048]{2,1,0:T(8,128)(2,1)} %bitcast.3, ...), custom_call_target="tpu_custom_call" | custom-call | flops 27262976 | bytes 13631488 | tf_op jit(solution)/shard_map/coef/pallas_call | solution.py:176
  13.7 5.1 %collective-permute-start.2 = (bf16[16,416]{1,0:T(8,128)(2,1)S(1)}, bf16[16,416]{1,0:T(8,128)(2,1)S(1)}, u32[]{:S(2)}, u32[]{:S(2)}) collective-permute-start(bf16[16,416]{1,0:T(8,128)(2,1)S(1)} %get-tuple-element.14), channel_id=1, source_target_pairs={{0,24},{8,16},{16,8},{24,0},{1,25},{9,17},{17,9},{25,1},{2,26},{10... | collective-permute-start | bytes 39944 | tf_op jit(solution)/shard_map/ppermute | solution.py:261
  18.8 0.0 collective-permute-start.1
  18.8 0.6 %collective-permute-start = (bf16[16,416]{1,0:T(8,128)(2,1)S(1)}, bf16[16,416]{1,0:T(8,128)(2,1)S(1)}, u32[]{:S(2)}, u32[]{:S(2)}) collective-permute-start(bf16[16,416]{1,0:T(8,128)(2,1)S(1)} %get-tuple-element.14), channel_id=1, source_target_pairs={{0,8},{8,0},{16,24},{24,16},{1,9},{9,1},{17,25},{25,17},{2,10},{10... | collective-permute-start | bytes 39944 | tf_op jit(solution)/shard_map/ppermute | solution.py:261
  19.4 3.1 %collective-permute-done = bf16[16,416]{1,0:T(8,128)(2,1)S(1)} collective-permute-done((bf16[16,416]{1,0:T(8,128)(2,1)S(1)}, bf16[16,416]{1,0:T(8,128)(2,1)S(1)}, u32[]{:S(2)}, u32[]{:S(2)}) %collective-permute-start) | collective-permute-done | bytes 13344 | tf_op jit(solution)/shard_map/ppermute | solution.py:261
  22.5 0.9 %collective-permute-done.1 = bf16[16,416]{1,0:T(8,128)(2,1)S(1)} collective-permute-done((bf16[16,416]{1,0:T(8,128)(2,1)S(1)}, bf16[16,416]{1,0:T(8,128)(2,1)S(1)}, u32[]{:S(2)}, u32[]{:S(2)}) %collective-permute-start.1) | collective-permute-done | bytes 13344 | tf_op jit(solution)/shard_map/ppermute | solution.py:261
  23.4 0.0 collective-permute-done.2
  23.4 2.5 %collective-permute-start.5 = (bf16[64,416]{1,0:T(8,128)(2,1)S(1)}, bf16[64,416]{1,0:T(8,128)(2,1)S(1)}, u32[]{:S(2)}, u32[]{:S(2)}) collective-permute-start(bf16[64,416]{1,0:T(8,128)(2,1)S(1)} %constant_dynamic-update-slice_fusion.refs_0_), channel_id=1, source_target_pairs={{0,6},{1,7},{2,4},{3,5},{4,2},{5,3},{6,0},{7,1},{8,14},{9,15},{10,... | collective-permute-start | bytes 159752 | tf_op jit(solution)/shard_map/ppermute | solution.py:261
  25.9 0.5 %collective-permute-start.4 = (bf16[64,416]{1,0:T(8,128)(2,1)S(1)}, bf16[64,416]{1,0:T(8,128)(2,1)S(1)}, u32[]{:S(2)}, u32[]{:S(2)}) collective-permute-start(bf16[64,416]{1,0:T(8,128)(2,1)S(1)} %constant_dynamic-update-slice_fusion.refs_0_), channel_id=1, source_target_pairs={{0,4},{1,5},{2,6},{3,7},{4,0},{5,1},{6,2},{7,3},{8,12},{9,13},{10,... | collective-permute-start | bytes 159752 | tf_op jit(solution)/shard_map/ppermute | solution.py:261
  26.5 0.5 %collective-permute-start.3 = (bf16[64,416]{1,0:T(8,128)(2,1)S(1)}, bf16[64,416]{1,0:T(8,128)(2,1)S(1)}, u32[]{:S(2)}, u32[]{:S(2)}) collective-permute-start(bf16[64,416]{1,0:T(8,128)(2,1)S(1)} %constant_dynamic-update-slice_fusion.refs_0_), channel_id=1, source_target_pairs={{0,2},{1,3},{2,0},{3,1},{4,6},{5,7},{6,4},{7,5},{8,10},{9,11},{10,... | collective-permute-start | bytes 159752 | tf_op jit(solution)/shard_map/ppermute | solution.py:261
  27.0 0.0 collective-permute-start.6
  27.0 2.3 %collective-permute-done.5.refs_3_ = bf16[64,416]{1,0:T(8,128)(2,1)S(1)} collective-permute-done((bf16[64,416]{1,0:T(8,128)(2,1)S(1)}, bf16[64,416]{1,0:T(8,128)(2,1)S(1)}, u32[]{:S(2)}, u32[]{:S(2)}) %collective-permute-start.5) | collective-permute-done | bytes 53280 | tf_op jit(solution)/shard_map/ppermute | solution.py:261
  29.3 0.0 collective-permute-start.9
  29.3 1.0 %collective-permute-done.4.refs_2_ = bf16[64,416]{1,0:T(8,128)(2,1)S(1)} collective-permute-done((bf16[64,416]{1,0:T(8,128)(2,1)S(1)}, bf16[64,416]{1,0:T(8,128)(2,1)S(1)}, u32[]{:S(2)}, u32[]{:S(2)}) %collective-permute-start.4) | collective-permute-done | bytes 53280 | tf_op jit(solution)/shard_map/ppermute | solution.py:261
  30.2 0.0 collective-permute-start.8
  30.2 0.5 %collective-permute-done.3.refs_1_ = bf16[64,416]{1,0:T(8,128)(2,1)S(1)} collective-permute-done((bf16[64,416]{1,0:T(8,128)(2,1)S(1)}, bf16[64,416]{1,0:T(8,128)(2,1)S(1)}, u32[]{:S(2)}, u32[]{:S(2)}) %collective-permute-start.3) | collective-permute-done | bytes 53280 | tf_op jit(solution)/shard_map/ppermute | solution.py:261
  30.7 0.0 collective-permute-start.7
  30.7 0.0 collective-permute-done.6.refs_4_
  30.7 0.0 collective-permute-done.9.refs_7_
  30.7 0.7 %collective-permute-done.8.refs_6_ = bf16[64,416]{1,0:T(8,128)(2,1)S(1)} collective-permute-done((bf16[64,416]{1,0:T(8,128)(2,1)S(1)}, bf16[64,416]{1,0:T(8,128)(2,1)S(1)}, u32[]{:S(2)}, u32[]{:S(2)}) %collective-permute-start.8) | collective-permute-done | bytes 53280 | tf_op jit(solution)/shard_map/ppermute | solution.py:261
  31.5 0.5 %collective-permute-done.7.refs_5_ = bf16[64,416]{1,0:T(8,128)(2,1)S(1)} collective-permute-done((bf16[64,416]{1,0:T(8,128)(2,1)S(1)}, bf16[64,416]{1,0:T(8,128)(2,1)S(1)}, u32[]{:S(2)}, u32[]{:S(2)}) %collective-permute-start.7) | collective-permute-done | bytes 53280 | tf_op jit(solution)/shard_map/ppermute | solution.py:261
  32.0 1.1 %sample.1 = f32[1,256]{1,0:T(1,128)} custom-call(bf16[256,512]{1,0:T(8,128)(2,1)S(1)} %get-tuple-element.10.re_ref, bf16[256,512]{1,0:T(8,128)(2,1)S(1)} %get-tuple-element.11.im_ref, f32[256,416]{1,0:T(8,128)S(1)} %get-tuple-element.12.tail_re_ref, f32[256,416]{1,0:T(8,128)S(1)} %get-tuple-element.13.tail_im_ref, ...), custom_call_target="tpu_custom_call" | custom-call | flops 218103808 | bytes 1048576 | tf_op jit(solution)/shard_map/sample/pallas_call | solution.py:237
  (4 shorter events, 0.0 us)
Async XLA Ops:
  1.4 0.9 %copy-start = (f32[13,2048]{1,0:T(8,128)S(1)}, f32[13,2048]{1,0:T(8,128)}, u32[]{:S(2)}) copy-start(f32[13,2048]{1,0:T(8,128)} %beam_hbm.1) | copy-start | bytes 319492
  2.3 0.8 %copy-start.1 = (bf16[2,8,2048]{2,1,0:T(8,128)(2,1)S(1)}, bf16[2,8,2048]{2,1,0:T(8,128)(2,1)}, u32[]{:S(2)}) copy-start(bf16[2,8,2048]{2,1,0:T(8,128)(2,1)} %alm_hbm.1) | copy-start | bytes 196612
  3.2 0.7 %copy-start.2 = (f32[8,416]{1,0:T(8,128)S(1)}, f32[8,416]{1,0:T(8,128)}, u32[]{:S(2)}) copy-start(f32[8,416]{1,0:T(8,128)} %constant.8.clone.lane_ref) | copy-start | bytes 39940
  3.9 0.7 %copy-start.3 = (s32[8,512]{1,0:T(8,128)S(1)}, s32[8,512]{1,0:T(8,128)}, u32[]{:S(2)}) copy-start(s32[8,512]{1,0:T(8,128)} %constant.7.clone.from_ref) | copy-start | bytes 49156
  4.6 0.7 %copy-start.4 = (s32[1,32]{1,0:T(1,128)S(1)}, s32[1,32]{1,0:T(1,128)}, u32[]{:S(2)}) copy-start(s32[1,32]{1,0:T(1,128)} %counts_ref.1) | copy-start | bytes 388
  13.7 9.8 %collective-permute-start.2 = (bf16[16,416]{1,0:T(8,128)(2,1)S(1)}, bf16[16,416]{1,0:T(8,128)(2,1)S(1)}, u32[]{:S(2)}, u32[]{:S(2)}) collective-permute-start(bf16[16,416]{1,0:T(8,128)(2,1)S(1)} %get-tuple-element.14), channel_id=1, source_target_pairs={{0,24},{8,16},{16,8},{24,0},{1,25},{9,17},{17,9},{25,1},{2,26},{10... | collective-permute-start | bytes 39944 | tf_op jit(solution)/shard_map/ppermute | solution.py:261
  18.8 4.6 %collective-permute-start.1 = (bf16[16,416]{1,0:T(8,128)(2,1)S(1)}, bf16[16,416]{1,0:T(8,128)(2,1)S(1)}, u32[]{:S(2)}, u32[]{:S(2)}) collective-permute-start(bf16[16,416]{1,0:T(8,128)(2,1)S(1)} %get-tuple-element.14), channel_id=1, source_target_pairs={{0,16},{8,24},{16,0},{24,8},{1,17},{9,25},{17,1},{25,9},{2,18},{10... | collective-permute-start | bytes 39944 | tf_op jit(solution)/shard_map/ppermute | solution.py:261
  18.8 3.7 %collective-permute-start = (bf16[16,416]{1,0:T(8,128)(2,1)S(1)}, bf16[16,416]{1,0:T(8,128)(2,1)S(1)}, u32[]{:S(2)}, u32[]{:S(2)}) collective-permute-start(bf16[16,416]{1,0:T(8,128)(2,1)S(1)} %get-tuple-element.14), channel_id=1, source_target_pairs={{0,8},{8,0},{16,24},{24,16},{1,9},{9,1},{17,25},{25,17},{2,10},{10... | collective-permute-start | bytes 39944 | tf_op jit(solution)/shard_map/ppermute | solution.py:261
  23.4 5.8 %collective-permute-start.5 = (bf16[64,416]{1,0:T(8,128)(2,1)S(1)}, bf16[64,416]{1,0:T(8,128)(2,1)S(1)}, u32[]{:S(2)}, u32[]{:S(2)}) collective-permute-start(bf16[64,416]{1,0:T(8,128)(2,1)S(1)} %constant_dynamic-update-slice_fusion.refs_0_), channel_id=1, source_target_pairs={{0,6},{1,7},{2,4},{3,5},{4,2},{5,3},{6,0},{7,1},{8,14},{9,15},{10,... | collective-permute-start | bytes 159752 | tf_op jit(solution)/shard_map/ppermute | solution.py:261
  25.9 4.3 %collective-permute-start.4 = (bf16[64,416]{1,0:T(8,128)(2,1)S(1)}, bf16[64,416]{1,0:T(8,128)(2,1)S(1)}, u32[]{:S(2)}, u32[]{:S(2)}) collective-permute-start(bf16[64,416]{1,0:T(8,128)(2,1)S(1)} %constant_dynamic-update-slice_fusion.refs_0_), channel_id=1, source_target_pairs={{0,4},{1,5},{2,6},{3,7},{4,0},{5,1},{6,2},{7,3},{8,12},{9,13},{10,... | collective-permute-start | bytes 159752 | tf_op jit(solution)/shard_map/ppermute | solution.py:261
  26.5 4.3 %collective-permute-start.3 = (bf16[64,416]{1,0:T(8,128)(2,1)S(1)}, bf16[64,416]{1,0:T(8,128)(2,1)S(1)}, u32[]{:S(2)}, u32[]{:S(2)}) collective-permute-start(bf16[64,416]{1,0:T(8,128)(2,1)S(1)} %constant_dynamic-update-slice_fusion.refs_0_), channel_id=1, source_target_pairs={{0,2},{1,3},{2,0},{3,1},{4,6},{5,7},{6,4},{7,5},{8,10},{9,11},{10,... | collective-permute-start | bytes 159752 | tf_op jit(solution)/shard_map/ppermute | solution.py:261
  27.0 3.7 %collective-permute-start.6 = (bf16[64,416]{1,0:T(8,128)(2,1)S(1)}, bf16[64,416]{1,0:T(8,128)(2,1)S(1)}, u32[]{:S(2)}, u32[]{:S(2)}) collective-permute-start(bf16[64,416]{1,0:T(8,128)(2,1)S(1)} %constant_dynamic-update-slice_fusion.refs_0_), channel_id=1, source_target_pairs={{0,1},{1,0},{2,3},{3,2},{4,5},{5,4},{6,7},{7,6},{8,9},{9,8},{10,11... | collective-permute-start | bytes 159752 | tf_op jit(solution)/shard_map/ppermute | solution.py:261
  29.3 1.5 %collective-permute-start.9 = (bf16[64,416]{1,0:T(8,128)(2,1)S(1)}, bf16[64,416]{1,0:T(8,128)(2,1)S(1)}, u32[]{:S(2)}, u32[]{:S(2)}) collective-permute-start(bf16[64,416]{1,0:T(8,128)(2,1)S(1)} %collective-permute-done.5.refs_3_), channel_id=1, source_target_pairs={{0,1},{1,0},{2,3},{3,2},{4,5},{5,4},{6,7},{7,6},{8,9},{9,8},{10,11... | collective-permute-start | bytes 159752 | tf_op jit(solution)/shard_map/ppermute | solution.py:261
  30.2 1.3 %collective-permute-start.8 = (bf16[64,416]{1,0:T(8,128)(2,1)S(1)}, bf16[64,416]{1,0:T(8,128)(2,1)S(1)}, u32[]{:S(2)}, u32[]{:S(2)}) collective-permute-start(bf16[64,416]{1,0:T(8,128)(2,1)S(1)} %collective-permute-done.4.refs_2_), channel_id=1, source_target_pairs={{0,1},{1,0},{2,3},{3,2},{4,5},{5,4},{6,7},{7,6},{8,9},{9,8},{10,11... | collective-permute-start | bytes 159752 | tf_op jit(solution)/shard_map/ppermute | solution.py:261
  30.7 1.3 %collective-permute-start.7 = (bf16[64,416]{1,0:T(8,128)(2,1)S(1)}, bf16[64,416]{1,0:T(8,128)(2,1)S(1)}, u32[]{:S(2)}, u32[]{:S(2)}) collective-permute-start(bf16[64,416]{1,0:T(8,128)(2,1)S(1)} %collective-permute-done.3.refs_1_), channel_id=1, source_target_pairs={{0,1},{1,0},{2,3},{3,2},{4,5},{5,4},{6,7},{7,6},{8,9},{9,8},{10,11... | collective-permute-start | bytes 159752 | tf_op jit(solution)/shard_map/ppermute | solution.py:261

commit v3 on v2

--- a/solution.py
+++ b/solution.py
@@ -3,7 +3,6 @@
 
 import jax
 import jax.numpy as jnp
-import numpy as np
 from jax import lax
 from jax.experimental import pallas as pl
 from jax.experimental.pallas import tpu as pltpu
@@ -24,10 +23,6 @@
     return cos, sin * x
 
 
-def remainder(x, n):
-    return x - n * jnp.floor((x + 0.5) * (1.0 / n))
-
-
 def tap_phases(taps, turns):
     total_re = taps[0] * jnp.ones_like(turns)
     total_im = jnp.zeros_like(total_re)
@@ -43,28 +38,51 @@
     return cos * values[0] - sin * values[1], sin * values[0] + cos * values[1]
 
 
-def slot_weights(sizes, cols, counts, order, quarter, k_lane, r_lane):
-    phi_total, lats, psi_count, lat_dev, phi_dev, scale = sizes
+def divide(x, n):
+    quotient = jnp.floor((x + 0.5) * (1.0 / n))
+    return quotient, x - n * quotient
+
+
+def slot_rows(sizes, weights, base, counts, n_strip, n_mr):
+    phi_total, lats, psi_count, scale = sizes
+    slots = weights.shape[1]
+    devices = n_strip * n_mr
+    lat_dev, phi_dev = lats // n_mr, phi_total // n_strip
+    slot = lax.broadcasted_iota(jnp.int32, (1, slots), 1).astype(jnp.float32)
+    dest, at = divide(slot, slots // devices)
+    dest_strip, dest_mr = divide(dest, n_mr)
+    dests = lax.broadcasted_iota(jnp.int32, (devices, slots), 0).astype(jnp.float32)
+    counts = jnp.broadcast_to(counts.astype(jnp.float32), (8, devices)).astype(jnp.bfloat16)
+    used = jnp.dot(
+        counts, (dests == dest).astype(jnp.bfloat16), preferred_element_type=jnp.float32
+    )
+    live = (at < used[0:1]).astype(jnp.float32)
+    rest, phi_base = divide(base.astype(jnp.float32), phi_dev + 1)
+    psi_base, lat_base = divide(rest, lat_dev + 1)
+    return jnp.concatenate(
+        [
+            weights[0:4] * (live * scale),
+            weights[4:],
+            dest_strip * phi_dev + phi_base - 2.0,
+            dest_mr * lat_dev + lat_base - 2.0,
+            psi_base,
+            jnp.zeros_like(base, jnp.float32),
+        ],
+        axis=0,
+    )
+
+
+def slot_weights(sizes, cols, order, quarter, k_lane, r_lane):
+    phi_total, lats, psi_count, _ = sizes
     col = lambda i: cols[:, i : i + 1]
-    base, slot_e, strip_phi, mr_lat, of_slot = (col(i) for i in range(12, 17))
-    dest = lax.broadcasted_iota(jnp.int32, (cols.shape[0], counts.shape[1]), 1)
-    used = jnp.where(dest.astype(jnp.float32) == of_slot, counts, 0.0)
-    live = (slot_e < jnp.sum(used, axis=1, keepdims=True)).astype(jnp.float32)
-    rest = jnp.floor((base + 0.5) * (1.0 / (phi_dev + 1)))
-    phi_base = base - rest * (phi_dev + 1)
-    psi_base = jnp.floor((rest + 0.5) * (1.0 / (lat_dev + 1)))
-    lat_base = rest - psi_base * (lat_dev + 1)
-    phases = turned(
-        (strip_phi + phi_base - 2.0) * (order * (1.0 / phi_total)) + quarter,
-        tap_phases([col(4 + b) for b in range(4)], order * (1.0 / phi_total)),
-    )
+    turns = order * (1.0 / phi_total)
+    phases = turned(col(12) * turns + quarter, tap_phases([col(4 + b) for b in range(4)], turns))
     across = jnp.zeros((cols.shape[0], k_lane.shape[1]), jnp.float32)
     for a in range(4):
-        row = remainder(mr_lat + lat_base - 2.0 + a, lats)
-        across = across + jnp.where(row == r_lane, col(a) * live, 0.0)
-    across = across * scale
+        _, row = divide(col(13) + a, lats)
+        across = across + jnp.where(row == r_lane, col(a), 0.0)
     tail_re, tail_im = turned(
-        remainder(psi_base * k_lane, psi_count) * (1.0 / psi_count),
+        divide(col(14) * k_lane, psi_count)[1] * (1.0 / psi_count),
         tap_phases([col(8 + c) for c in range(4)], k_lane * (1.0 / psi_count)),
     )
     return phases + (tail_re * across, -tail_im * across)
@@ -75,10 +93,9 @@
     alm_hbm,
     beam_hbm,
     table_hbm,
-    slots_ref,
-    counts_ref,
-    from_ref,
-    lane_ref,
+    weights_hbm,
+    base_hbm,
+    counts_hbm,
     out_ref,
     re_ref,
     im_ref,
@@ -87,31 +104,47 @@
     alm,
     beam,
     table,
+    weights,
+    base,
+    counts,
     mixed,
     rows,
     cols,
     sems,
 ):
-    orders, beam_rows, ells = table.shape
+    n_strip, n_mr = lax.axis_size("strip"), lax.axis_size("mr")
+    orders, lanes, ells = table.shape
     k_count = beam.shape[0]
-    lats = beam_rows // k_count
+    lats = lanes // k_count
     k_pad = mixed.shape[1] // 2
-    small = [
-        pltpu.make_async_copy(alm_hbm, alm, sems.at[orders]),
-        pltpu.make_async_copy(beam_hbm, beam, sems.at[orders + 1]),
+    small = [(alm_hbm, alm), (beam_hbm, beam)]
+    slot = [(weights_hbm, weights), (base_hbm, base), (counts_hbm, counts)]
+    pairs = small + slot + [(table_hbm.at[m], table.at[m]) for m in range(orders)]
+    copies = [
+        pltpu.make_async_copy(source, target, sems.at[i])
+        for i, (source, target) in enumerate(pairs)
     ]
-    big = [
-        pltpu.make_async_copy(table_hbm.at[m], table.at[m], sems.at[m]) for m in range(orders)
-    ]
-    for copy in small + big:
+    small, slot, big = copies[:2], copies[2:5], copies[5:]
+    for copy in copies:
         copy.start()
     mixed[...] = jnp.zeros_like(mixed)
-    cols[...] = slots_ref[...].T
-    strip_at, mr_at = lax.axis_index("strip"), lax.axis_index("mr")
-    source = (from_ref[0:1] ^ strip_at) * lax.axis_size("mr") + (from_ref[1:2] ^ mr_at)
-    order = (source * orders + from_ref[2:3]).astype(jnp.float32)
-    quarter = 0.25 * from_ref[3:4].astype(jnp.float32)
-    counts = counts_ref[...].astype(jnp.float32)
+
+    width = re_ref.shape[1]
+    at = lax.broadcasted_iota(jnp.int32, (1, width), 1).astype(jnp.float32)
+    at, m_row = divide(at, orders)
+    at, part = divide(at, 2)
+    at, strip = divide(at, n_strip)
+    core, chip = divide(at, n_mr // 2)
+    strip = strip.astype(jnp.int32) ^ lax.axis_index("strip")
+    mr = (2.0 * chip + core).astype(jnp.int32) ^ lax.axis_index("mr")
+    order = ((strip * n_mr + mr) * orders).astype(jnp.float32) + m_row
+    quarter = 0.25 * part
+    lane = lax.broadcasted_iota(jnp.int32, (1, lanes), 1).astype(jnp.float32)
+    k_lane, r_lane = divide(lane, lats)
+
+    for copy in slot:
+        copy.wait()
+    cols[...] = slot_rows(sizes, weights[...], base[...], counts[...], n_strip, n_mr).T
     block = cols.shape[0] // orders
 
     def mix(m):
@@ -133,7 +166,7 @@
             rows[c * orders + m : c * orders + m + 1, :] = total
         here = slice(m * block, (m + 1) * block)
         re, im, tail_re, tail_im = slot_weights(
-            sizes, cols[here], counts, order, quarter, lane_ref[0:1], lane_ref[1:2]
+            sizes, cols[here], order, quarter, k_lane, r_lane
         )
         re_ref[here] = re.astype(jnp.bfloat16)
         im_ref[here] = im.astype(jnp.bfloat16)
@@ -149,30 +182,10 @@
     k_pad = -(-k_count // 8) * 8
     lanes = k_count * lats
     slots = base_index.shape[0]
-    devices = n_strip * n_mr
-    width = 2 * orders * devices
-    m_total = orders * devices
-    phi_total = 2 * m_total
-    lat_dev, phi_dev = lats // n_mr, phi_total // n_strip
-    scale = 1.0 / math.sqrt(m_total * k_count)
-    sizes = (phi_total, lats, 2 * k_count - 1, lat_dev, phi_dev, scale)
-
-    dest = np.arange(slots) // (slots // devices)
-    fixed = np.zeros((19, slots), np.float32)
-    fixed[0] = np.arange(slots) % (slots // devices)
-    fixed[1] = dest // n_mr * phi_dev
-    fixed[2] = dest % n_mr * lat_dev
-    fixed[3] = dest
-    table = jnp.concatenate(
-        [interp_weights, base_index[None].astype(jnp.float32), jnp.asarray(fixed)], axis=0
-    )
-    core, chip, strip, part, m = np.indices((2, n_mr // 2, n_strip, 2, orders)).reshape(5, -1)
-    source = np.zeros((8, width), np.int32)
-    source[:4] = [strip, 2 * chip + core, m, part]
-    lane = np.zeros((8, lanes), np.float32)
-    lane[0] = np.arange(lanes) // lats
-    lane[1] = np.arange(lanes) % lats
-    hbm = pl.BlockSpec(memory_space=pltpu.HBM)
+    m_total = orders * n_strip * n_mr
+    width = 2 * m_total
+    sizes = (2 * m_total, lats, 2 * k_count - 1, 1.0 / math.sqrt(m_total * k_count))
+    base = base_index.reshape(1, slots)
     return pl.pallas_call(
         functools.partial(coef_kernel, sizes),
         out_shape=(
@@ -182,31 +195,26 @@
             jax.ShapeDtypeStruct((slots, lanes), jnp.float32),
             jax.ShapeDtypeStruct((slots, lanes), jnp.float32),
         ),
-        in_specs=[hbm] * 3 + [VMEM] * 4,
+        in_specs=[pl.BlockSpec(memory_space=pltpu.HBM)] * 6,
         out_specs=(VMEM,) * 5,
         scratch_shapes=[
-            pltpu.VMEM((2, orders, ells), jnp.bfloat16),
-            pltpu.VMEM((k_count, ells), jnp.float32),
-            pltpu.VMEM((orders, lanes, ells), jnp.bfloat16),
+            pltpu.VMEM(alm.shape, alm.dtype),
+            pltpu.VMEM(beam.shape, beam.dtype),
+            pltpu.VMEM((orders, lanes, ells), wigner.dtype),
+            pltpu.VMEM(interp_weights.shape, interp_weights.dtype),
+            pltpu.VMEM(base.shape, base.dtype),
+            pltpu.VMEM(live_counts.shape, live_counts.dtype),
             pltpu.VMEM((orders, 2 * k_pad, ells), jnp.bfloat16),
             pltpu.VMEM((2 * orders, lanes), jnp.float32),
-            pltpu.VMEM((slots, 32), jnp.float32),
-            pltpu.SemaphoreType.DMA((orders + 2,)),
+            pltpu.VMEM((slots, 16), jnp.float32),
+            pltpu.SemaphoreType.DMA((orders + 5,)),
         ],
         compiler_params=pltpu.CompilerParams(vmem_limit_bytes=48 << 20),
         cost_estimate=pl.CostEstimate(
             flops=4 * wigner.size, bytes_accessed=2 * wigner.size, transcendentals=0
         ),
         name="coef",
-    )(
-        alm,
-        beam,
-        wigner.reshape(orders, lanes, ells),
-        table,
-        live_counts,
-        jnp.asarray(source),
-        jnp.asarray(lane),
-    )
+    )(alm, beam, wigner.reshape(orders, lanes, ells), interp_weights, base, live_counts)
 
 
 def sample_kernel(re_ref, im_ref, tail_re_ref, tail_im_ref, *refs):
@@ -263,7 +271,7 @@
     column = [swap(mine, "strip", d) for d in range(n_strip - 1, 0, -1)][::-1]
     column = jnp.concatenate([mine] + column, axis=0)
     plane = [column] + [swap(column, "mr", d) for d in range(n_mr - 2, 0, -2)][::-1]
-    other = [swap(part, "mr", 1) for part in plane]
+    other = [swap(column, "mr", 1), swap(jnp.concatenate(plane[1:], axis=0), "mr", 1)]
     return sample(phases, plane + other).reshape(-1)
 
 

time: 33.5 us -> 34.7 us (1.036)
  waiting for transfers between devices: 8.96 us -> 11.2 us
  other arithmetic: 1.43 us -> 0.02 us
  starting transfers between devices: 9.32 us -> 9.74 us
    ppermute x10 -> x8, waiting for transfers between devices: 8.96 us -> 11.2 us  [swap(): lax.ppermute(x, axis, [(i, i ^ d) for i in range(lax.axis_size(axis))])]
    concatenate x1, other arithmetic: 0.75 us -> 0.02 us  [on_device(): jnp.concatenate(plane[1:], axis=0)]
    convert_element_type x1 -> x0, other arithmetic: 0.68 us -> none  [local_part(): base_index[None].astype(jnp.float32)]
    ppermute x10 -> x8, starting transfers between devices: 9.32 us -> 9.74 us  [swap(): lax.ppermute(x, axis, [(i, i ^ d) for i in range(lax.axis_size(axis))])]
  transfers between devices with their start and end apart: 10 -> 8, of which waited for: 7 -> 6; matrix products, arithmetic and copies ran while one was open for 0% -> 0% of each run, Pallas kernels for 0% -> 0%
where the time goes in v3:
time: 34.7 us; the launch traced here: 34.5 us
  waiting for transfers between devices  11.2 us (32%)
  starting transfers between devices  9.74 us (28%)
  Pallas kernels  9.63 us (28%)
  local copies, waits for them, and re-layouts  3.8 us (11%)
    ppermute x8, waiting for transfers between devices, swap(): lax.ppermute(x, axis, [(i, i ^ d) for i in range(lax.axis_size(axis))])  11.2 us
    ppermute x8, starting transfers between devices, swap(): lax.ppermute(x, axis, [(i, i ^ d) for i in range(lax.axis_size(axis))])  9.74 us
    pallas_call x1, Pallas kernels, local_part(): pl.pallas_call(functools.partial(coef_kernel, sizes), out_shape=(jax.Shap...  8.51 us
    unnamed x13, local copies, waits for them, and re-layouts  3.8 us
    pallas_call x1, Pallas kernels, sample(): pl.pallas_call(sample_kernel, grid=(slots // block,), out_shape=jax.Shape...  1.12 us
  transfers between devices with their start and end apart: 8, of which 6 were waited for; matrix products, arithmetic and copies ran while one was open for 0% of the time, Pallas kernels for 0%

profile of v3, /device:TPU:0, one launch (start us, length us, event | category | flops | bytes accessed | tf_op | source)
XLA Modules:
  0.0 34.5 jit_solution(3170010724978215052)
XLA Ops:
  0.0 0.0 copy-start
  0.0 0.9 %copy-done = f32[13,2048]{1,0:T(8,128)S(1)} copy-done((f32[13,2048]{1,0:T(8,128)S(1)}, f32[13,2048]{1,0:T(8,128)}, u32[]{:S(2)}) %copy-start) | copy-done | bytes 106520
  0.9 0.0 copy-start.1
  0.9 0.8 %copy-done.1 = bf16[2,8,2048]{2,1,0:T(8,128)(2,1)S(1)} copy-done((bf16[2,8,2048]{2,1,0:T(8,128)(2,1)S(1)}, bf16[2,8,2048]{2,1,0:T(8,128)(2,1)}, u32[]{:S(2)}) %copy-start.1) | copy-done | bytes 65560
  1.7 0.0 copy-start.2
  1.7 0.7 %copy-done.2 = f32[12,256]{1,0:T(8,128)S(1)} copy-done((f32[12,256]{1,0:T(8,128)S(1)}, f32[12,256]{1,0:T(8,128)}, u32[]{:S(2)}) %copy-start.2) | copy-done | bytes 12312
  2.5 0.0 copy-start.3
  2.5 0.7 %copy-done.3 = s32[256]{0:T(256)S(1)} copy-done((s32[256]{0:T(256)S(1)}, s32[256]{0:T(256)}, u32[]{:S(2)}) %copy-start.3) | copy-done | bytes 1048
  3.1 0.0 copy-start.4
  3.1 0.7 %copy-done.4 = s32[1,32]{1,0:T(1,128)S(1)} copy-done((s32[1,32]{1,0:T(1,128)S(1)}, s32[1,32]{1,0:T(1,128)}, u32[]{:S(2)}) %copy-start.4) | copy-done | bytes 152
  3.8 8.5 %coef.1 = (bf16[16,416]{1,0:T(8,128)(2,1)S(1)}, bf16[256,512]{1,0:T(8,128)(2,1)S(1)}, bf16[256,512]{1,0:T(8,128)(2,1)S(1)}, f32[256,416]{1,0:T(8,128)S(1)}, f32[256,416]{1,0:T(8,128)S(1)}) custom-call(bf16[2,8,2048]{2,1,0:T(8,128)(2,1)S(1)} %copy-done.1, f32[13,2048]{1,0:T(8,128)S(1)} %copy-done, bf16[8,416,2048]{2,1,0:T(8,128)(2,1)} %bitcast.4, ...), custom_call_target="tpu_custom_call" | custom-call | flops 27262976 | bytes 13631488 | tf_op jit(solution)/shard_map/coef/pallas_call | solution.py:189
  12.3 3.1 %collective-permute-start = (bf16[16,416]{1,0:T(8,128)(2,1)S(1)}, bf16[16,416]{1,0:T(8,128)(2,1)S(1)}, u32[]{:S(2)}, u32[]{:S(2)}) collective-permute-start(bf16[16,416]{1,0:T(8,128)(2,1)S(1)} %get-tuple-element.14), channel_id=1, source_target_pairs={{0,8},{8,0},{16,24},{24,16},{1,9},{9,1},{17,25},{25,17},{2,10},{10... | collective-permute-start | bytes 39944 | tf_op jit(solution)/shard_map/ppermute | solution.py:269
  15.4 2.6 %collective-permute-start.1 = (bf16[16,416]{1,0:T(8,128)(2,1)S(1)}, bf16[16,416]{1,0:T(8,128)(2,1)S(1)}, u32[]{:S(2)}, u32[]{:S(2)}) collective-permute-start(bf16[16,416]{1,0:T(8,128)(2,1)S(1)} %get-tuple-element.14), channel_id=1, source_target_pairs={{0,16},{8,24},{16,0},{24,8},{1,17},{9,25},{17,1},{25,9},{2,18},{10... | collective-permute-start | bytes 39944 | tf_op jit(solution)/shard_map/ppermute | solution.py:269
  18.0 0.0 collective-permute-start.2
  18.0 0.0 collective-permute-done
  18.0 2.1 %collective-permute-done.1 = bf16[16,416]{1,0:T(8,128)(2,1)S(1)} collective-permute-done((bf16[16,416]{1,0:T(8,128)(2,1)S(1)}, bf16[16,416]{1,0:T(8,128)(2,1)S(1)}, u32[]{:S(2)}, u32[]{:S(2)}) %collective-permute-start.1) | collective-permute-done | bytes 13344 | tf_op jit(solution)/shard_map/ppermute | solution.py:269
  20.1 3.4 %collective-permute-done.2 = bf16[16,416]{1,0:T(8,128)(2,1)S(1)} collective-permute-done((bf16[16,416]{1,0:T(8,128)(2,1)S(1)}, bf16[16,416]{1,0:T(8,128)(2,1)S(1)}, u32[]{:S(2)}, u32[]{:S(2)}) %collective-permute-start.2) | collective-permute-done | bytes 13344 | tf_op jit(solution)/shard_map/ppermute | solution.py:269
  23.5 1.5 %collective-permute-start.3 = (bf16[64,416]{1,0:T(8,128)(2,1)S(1)}, bf16[64,416]{1,0:T(8,128)(2,1)S(1)}, u32[]{:S(2)}, u32[]{:S(2)}) collective-permute-start(bf16[64,416]{1,0:T(8,128)(2,1)S(1)} %constant_dynamic-update-slice_fusion.refs_0_), channel_id=1, source_target_pairs={{0,2},{1,3},{2,0},{3,1},{4,6},{5,7},{6,4},{7,5},{8,10},{9,11},{10,... | collective-permute-start | bytes 159752 | tf_op jit(solution)/shard_map/ppermute | solution.py:269
  25.0 1.5 %collective-permute-start.4 = (bf16[64,416]{1,0:T(8,128)(2,1)S(1)}, bf16[64,416]{1,0:T(8,128)(2,1)S(1)}, u32[]{:S(2)}, u32[]{:S(2)}) collective-permute-start(bf16[64,416]{1,0:T(8,128)(2,1)S(1)} %constant_dynamic-update-slice_fusion.refs_0_), channel_id=1, source_target_pairs={{0,4},{1,5},{2,6},{3,7},{4,0},{5,1},{6,2},{7,3},{8,12},{9,13},{10,... | collective-permute-start | bytes 159752 | tf_op jit(solution)/shard_map/ppermute | solution.py:269
  26.5 0.5 %collective-permute-start.5 = (bf16[64,416]{1,0:T(8,128)(2,1)S(1)}, bf16[64,416]{1,0:T(8,128)(2,1)S(1)}, u32[]{:S(2)}, u32[]{:S(2)}) collective-permute-start(bf16[64,416]{1,0:T(8,128)(2,1)S(1)} %constant_dynamic-update-slice_fusion.refs_0_), channel_id=1, source_target_pairs={{0,6},{1,7},{2,4},{3,5},{4,2},{5,3},{6,0},{7,1},{8,14},{9,15},{10,... | collective-permute-start | bytes 159752 | tf_op jit(solution)/shard_map/ppermute | solution.py:269
  27.0 1.0 %collective-permute-done.3.refs_1_ = bf16[64,416]{1,0:T(8,128)(2,1)S(1)} collective-permute-done((bf16[64,416]{1,0:T(8,128)(2,1)S(1)}, bf16[64,416]{1,0:T(8,128)(2,1)S(1)}, u32[]{:S(2)}, u32[]{:S(2)}) %collective-permute-start.3) | collective-permute-done | bytes 53280 | tf_op jit(solution)/shard_map/ppermute | solution.py:269
  28.1 1.3 %collective-permute-done.4.refs_2_ = bf16[64,416]{1,0:T(8,128)(2,1)S(1)} collective-permute-done((bf16[64,416]{1,0:T(8,128)(2,1)S(1)}, bf16[64,416]{1,0:T(8,128)(2,1)S(1)}, u32[]{:S(2)}, u32[]{:S(2)}) %collective-permute-start.4) | collective-permute-done | bytes 53280 | tf_op jit(solution)/shard_map/ppermute | solution.py:269
  29.3 2.4 %collective-permute-done.5.refs_3_ = bf16[64,416]{1,0:T(8,128)(2,1)S(1)} collective-permute-done((bf16[64,416]{1,0:T(8,128)(2,1)S(1)}, bf16[64,416]{1,0:T(8,128)(2,1)S(1)}, u32[]{:S(2)}, u32[]{:S(2)}) %collective-permute-start.5) | collective-permute-done | bytes 53280 | tf_op jit(solution)/shard_map/ppermute | solution.py:269
  31.7 0.1 collective-permute-start.7
  31.8 0.5 %collective-permute-start.6 = (bf16[64,416]{1,0:T(8,128)(2,1)S(1)}, bf16[64,416]{1,0:T(8,128)(2,1)S(1)}, u32[]{:S(2)}, u32[]{:S(2)}) collective-permute-start(bf16[64,416]{1,0:T(8,128)(2,1)S(1)} %constant_dynamic-update-slice_fusion.refs_0_), channel_id=1, source_target_pairs={{0,1},{1,0},{2,3},{3,2},{4,5},{5,4},{6,7},{7,6},{8,9},{9,8},{10,11... | collective-permute-start | bytes 159752 | tf_op jit(solution)/shard_map/ppermute | solution.py:269
  32.3 1.0 %collective-permute-done.6.refs_4_ = bf16[64,416]{1,0:T(8,128)(2,1)S(1)} collective-permute-done((bf16[64,416]{1,0:T(8,128)(2,1)S(1)}, bf16[64,416]{1,0:T(8,128)(2,1)S(1)}, u32[]{:S(2)}, u32[]{:S(2)}) %collective-permute-start.6) | collective-permute-done | bytes 53280 | tf_op jit(solution)/shard_map/ppermute | solution.py:269
  33.3 0.0 collective-permute-done.7.refs_5_
  33.3 1.1 %sample.1 = f32[1,256]{1,0:T(1,128)} custom-call(bf16[256,512]{1,0:T(8,128)(2,1)S(1)} %get-tuple-element.10.re_ref, bf16[256,512]{1,0:T(8,128)(2,1)S(1)} %get-tuple-element.11.im_ref, f32[256,416]{1,0:T(8,128)S(1)} %get-tuple-element.12.tail_re_ref, f32[256,416]{1,0:T(8,128)S(1)} %get-tuple-element.13.tail_im_ref, ...), custom_call_target="tpu_custom_call" | custom-call | flops 218103808 | bytes 1048576 | tf_op jit(solution)/shard_map/sample/pallas_call | solution.py:245
  (5 shorter events, 0.0 us)
Async XLA Ops:
  0.0 0.9 %copy-start = (f32[13,2048]{1,0:T(8,128)S(1)}, f32[13,2048]{1,0:T(8,128)}, u32[]{:S(2)}) copy-start(f32[13,2048]{1,0:T(8,128)} %beam_hbm.1) | copy-start | bytes 319492
  0.9 0.8 %copy-start.1 = (bf16[2,8,2048]{2,1,0:T(8,128)(2,1)S(1)}, bf16[2,8,2048]{2,1,0:T(8,128)(2,1)}, u32[]{:S(2)}) copy-start(bf16[2,8,2048]{2,1,0:T(8,128)(2,1)} %alm_hbm.1) | copy-start | bytes 196612
  1.7 0.7 %copy-start.2 = (f32[12,256]{1,0:T(8,128)S(1)}, f32[12,256]{1,0:T(8,128)}, u32[]{:S(2)}) copy-start(f32[12,256]{1,0:T(8,128)} %weights_hbm.1) | copy-start | bytes 36868
  2.5 0.7 %copy-start.3 = (s32[256]{0:T(256)S(1)}, s32[256]{0:T(256)}, u32[]{:S(2)}) copy-start(s32[256]{0:T(256)} %param.9) | copy-start | bytes 3076
  3.1 0.7 %copy-start.4 = (s32[1,32]{1,0:T(1,128)S(1)}, s32[1,32]{1,0:T(1,128)}, u32[]{:S(2)}) copy-start(s32[1,32]{1,0:T(1,128)} %counts_hbm.1) | copy-start | bytes 388
  12.3 5.7 %collective-permute-start = (bf16[16,416]{1,0:T(8,128)(2,1)S(1)}, bf16[16,416]{1,0:T(8,128)(2,1)S(1)}, u32[]{:S(2)}, u32[]{:S(2)}) collective-permute-start(bf16[16,416]{1,0:T(8,128)(2,1)S(1)} %get-tuple-element.14), channel_id=1, source_target_pairs={{0,8},{8,0},{16,24},{24,16},{1,9},{9,1},{17,25},{25,17},{2,10},{10... | collective-permute-start | bytes 39944 | tf_op jit(solution)/shard_map/ppermute | solution.py:269
  15.4 4.7 %collective-permute-start.1 = (bf16[16,416]{1,0:T(8,128)(2,1)S(1)}, bf16[16,416]{1,0:T(8,128)(2,1)S(1)}, u32[]{:S(2)}, u32[]{:S(2)}) collective-permute-start(bf16[16,416]{1,0:T(8,128)(2,1)S(1)} %get-tuple-element.14), channel_id=1, source_target_pairs={{0,16},{8,24},{16,0},{24,8},{1,17},{9,25},{17,1},{25,9},{2,18},{10... | collective-permute-start | bytes 39944 | tf_op jit(solution)/shard_map/ppermute | solution.py:269
  18.0 5.5 %collective-permute-start.2 = (bf16[16,416]{1,0:T(8,128)(2,1)S(1)}, bf16[16,416]{1,0:T(8,128)(2,1)S(1)}, u32[]{:S(2)}, u32[]{:S(2)}) collective-permute-start(bf16[16,416]{1,0:T(8,128)(2,1)S(1)} %get-tuple-element.14), channel_id=1, source_target_pairs={{0,24},{8,16},{16,8},{24,0},{1,25},{9,17},{17,9},{25,1},{2,26},{10... | collective-permute-start | bytes 39944 | tf_op jit(solution)/shard_map/ppermute | solution.py:269
  23.5 4.5 %collective-permute-start.3 = (bf16[64,416]{1,0:T(8,128)(2,1)S(1)}, bf16[64,416]{1,0:T(8,128)(2,1)S(1)}, u32[]{:S(2)}, u32[]{:S(2)}) collective-permute-start(bf16[64,416]{1,0:T(8,128)(2,1)S(1)} %constant_dynamic-update-slice_fusion.refs_0_), channel_id=1, source_target_pairs={{0,2},{1,3},{2,0},{3,1},{4,6},{5,7},{6,4},{7,5},{8,10},{9,11},{10,... | collective-permute-start | bytes 159752 | tf_op jit(solution)/shard_map/ppermute | solution.py:269
  25.0 4.3 %collective-permute-start.4 = (bf16[64,416]{1,0:T(8,128)(2,1)S(1)}, bf16[64,416]{1,0:T(8,128)(2,1)S(1)}, u32[]{:S(2)}, u32[]{:S(2)}) collective-permute-start(bf16[64,416]{1,0:T(8,128)(2,1)S(1)} %constant_dynamic-update-slice_fusion.refs_0_), channel_id=1, source_target_pairs={{0,4},{1,5},{2,6},{3,7},{4,0},{5,1},{6,2},{7,3},{8,12},{9,13},{10,... | collective-permute-start | bytes 159752 | tf_op jit(solution)/shard_map/ppermute | solution.py:269
  26.5 5.2 %collective-permute-start.5 = (bf16[64,416]{1,0:T(8,128)(2,1)S(1)}, bf16[64,416]{1,0:T(8,128)(2,1)S(1)}, u32[]{:S(2)}, u32[]{:S(2)}) collective-permute-start(bf16[64,416]{1,0:T(8,128)(2,1)S(1)} %constant_dynamic-update-slice_fusion.refs_0_), channel_id=1, source_target_pairs={{0,6},{1,7},{2,4},{3,5},{4,2},{5,3},{6,0},{7,1},{8,14},{9,15},{10,... | collective-permute-start | bytes 159752 | tf_op jit(solution)/shard_map/ppermute | solution.py:269
  31.7 1.6 %collective-permute-start.7 = (bf16[192,416]{1,0:T(8,128)(2,1)S(1)}, bf16[192,416]{1,0:T(8,128)(2,1)S(1)}, u32[]{:S(2)}, u32[]{:S(2)}) collective-permute-start(bf16[192,416]{1,0:T(8,128)(2,1)S(1)} %pad_maximum_fusion), channel_id=1, source_target_pairs={{0,1},{1,0},{2,3},{3,2},{4,5},{5,4},{6,7},{7,6},{8,9},{9,8},{10,11... | collective-permute-start | bytes 479240 | tf_op jit(solution)/shard_map/ppermute | solution.py:269
  31.8 1.5 %collective-permute-start.6 = (bf16[64,416]{1,0:T(8,128)(2,1)S(1)}, bf16[64,416]{1,0:T(8,128)(2,1)S(1)}, u32[]{:S(2)}, u32[]{:S(2)}) collective-permute-start(bf16[64,416]{1,0:T(8,128)(2,1)S(1)} %constant_dynamic-update-slice_fusion.refs_0_), channel_id=1, source_target_pairs={{0,1},{1,0},{2,3},{3,2},{4,5},{5,4},{6,7},{7,6},{8,9},{9,8},{10,11... | collective-permute-start | bytes 159752 | tf_op jit(solution)/shard_map/ppermute | solution.py:269

commit v4 on v3

--- a/solution.py
+++ b/solution.py
@@ -214,7 +214,19 @@
             flops=4 * wigner.size, bytes_accessed=2 * wigner.size, transcendentals=0
         ),
         name="coef",
-    )(alm, beam, wigner.reshape(orders, lanes, ells), interp_weights, base, live_counts)
+    )(
+        *(
+            pltpu.with_memory_space_constraint(x, pltpu.HBM)
+            for x in (
+                alm,
+                beam,
+                wigner.reshape(orders, lanes, ells),
+                interp_weights,
+                base,
+                live_counts,
+            )
+        )
+    )
 
 
 def sample_kernel(re_ref, im_ref, tail_re_ref, tail_im_ref, *refs):
@@ -271,7 +283,7 @@
     column = [swap(mine, "strip", d) for d in range(n_strip - 1, 0, -1)][::-1]
     column = jnp.concatenate([mine] + column, axis=0)
     plane = [column] + [swap(column, "mr", d) for d in range(n_mr - 2, 0, -2)][::-1]
-    other = [swap(column, "mr", 1), swap(jnp.concatenate(plane[1:], axis=0), "mr", 1)]
+    other = [swap(part, "mr", 1) for part in plane]
     return sample(phases, plane + other).reshape(-1)
 
 

time: 34.7 us -> 28 us (0.81)
  local copies, waits for them, and re-layouts: 3.8 us -> 0.01 us
  waiting for transfers between devices: 11.2 us -> 8.96 us
  starting transfers between devices: 9.74 us -> 9.33 us
    unnamed x13 -> x3, local copies, waits for them, and re-layouts: 3.8 us -> 0.01 us
    ppermute x8 -> x10, waiting for transfers between devices: 11.2 us -> 8.96 us  [swap(): lax.ppermute(x, axis, [(i, i ^ d) for i in range(lax.axis_size(axis))])]
    ppermute x8 -> x10, starting transfers between devices: 9.74 us -> 9.33 us  [swap(): lax.ppermute(x, axis, [(i, i ^ d) for i in range(lax.axis_size(axis))])]
  transfers between devices with their start and end apart: 8 -> 10, of which waited for: 6 -> 7; matrix products, arithmetic and copies ran while one was open for 0% -> 0% of each run, Pallas kernels for 0% -> 0%
where the time goes in v4:
time: 28 us; the launch traced here: 27.9 us
  Pallas kernels  9.54 us (34%)
  starting transfers between devices  9.33 us (33%)
  waiting for transfers between devices  8.96 us (32%)
    ppermute x10, starting transfers between devices, swap(): lax.ppermute(x, axis, [(i, i ^ d) for i in range(lax.axis_size(axis))])  9.33 us
    ppermute x10, waiting for transfers between devices, swap(): lax.ppermute(x, axis, [(i, i ^ d) for i in range(lax.axis_size(axis))])  8.96 us
    pallas_call x1, Pallas kernels, local_part(): pl.pallas_call(functools.partial(coef_kernel, sizes), out_shape=(jax.Shap...  8.44 us
    pallas_call x1, Pallas kernels, sample(): pl.pallas_call(sample_kernel, grid=(slots // block,), out_shape=jax.Shape...  1.1 us
  transfers between devices with their start and end apart: 10, of which 7 were waited for; matrix products, arithmetic and copies ran while one was open for 0% of the time, Pallas kernels for 0%

profile of v4, /device:TPU:0, one launch (start us, length us, event | category | flops | bytes accessed | tf_op | source)
XLA Modules:
  0.0 27.9 jit_solution(579191671760883791)
XLA Ops:
  0.0 8.4 %coef.1 = (bf16[16,416]{1,0:T(8,128)(2,1)S(1)}, bf16[256,512]{1,0:T(8,128)(2,1)S(1)}, bf16[256,512]{1,0:T(8,128)(2,1)S(1)}, f32[256,416]{1,0:T(8,128)S(1)}, f32[256,416]{1,0:T(8,128)S(1)}) custom-call(bf16[2,8,2048]{2,1,0:T(8,128)(2,1)} %alm_hbm.1, f32[13,2048]{1,0:T(8,128)} %beam_hbm.1, bf16[8,416,2048]{2,1,0:T(8,128)(2,1)} %bitcast.3, ...), custom_call_target="tpu_custom_call" | custom-call | flops 27262976 | bytes 13631488 | tf_op jit(solution)/shard_map/coef/pallas_call | solution.py:189
  8.4 5.1 %collective-permute-start.2 = (bf16[16,416]{1,0:T(8,128)(2,1)S(1)}, bf16[16,416]{1,0:T(8,128)(2,1)S(1)}, u32[]{:S(2)}, u32[]{:S(2)}) collective-permute-start(bf16[16,416]{1,0:T(8,128)(2,1)S(1)} %get-tuple-element.14), channel_id=1, source_target_pairs={{0,24},{8,16},{16,8},{24,0},{1,25},{9,17},{17,9},{25,1},{2,26},{10... | collective-permute-start | bytes 39944 | tf_op jit(solution)/shard_map/ppermute | solution.py:281
  13.6 0.0 collective-permute-start.1
  13.6 0.6 %collective-permute-start = (bf16[16,416]{1,0:T(8,128)(2,1)S(1)}, bf16[16,416]{1,0:T(8,128)(2,1)S(1)}, u32[]{:S(2)}, u32[]{:S(2)}) collective-permute-start(bf16[16,416]{1,0:T(8,128)(2,1)S(1)} %get-tuple-element.14), channel_id=1, source_target_pairs={{0,8},{8,0},{16,24},{24,16},{1,9},{9,1},{17,25},{25,17},{2,10},{10... | collective-permute-start | bytes 39944 | tf_op jit(solution)/shard_map/ppermute | solution.py:281
  14.2 3.1 %collective-permute-done = bf16[16,416]{1,0:T(8,128)(2,1)S(1)} collective-permute-done((bf16[16,416]{1,0:T(8,128)(2,1)S(1)}, bf16[16,416]{1,0:T(8,128)(2,1)S(1)}, u32[]{:S(2)}, u32[]{:S(2)}) %collective-permute-start) | collective-permute-done | bytes 13344 | tf_op jit(solution)/shard_map/ppermute | solution.py:281
  17.3 0.9 %collective-permute-done.1 = bf16[16,416]{1,0:T(8,128)(2,1)S(1)} collective-permute-done((bf16[16,416]{1,0:T(8,128)(2,1)S(1)}, bf16[16,416]{1,0:T(8,128)(2,1)S(1)}, u32[]{:S(2)}, u32[]{:S(2)}) %collective-permute-start.1) | collective-permute-done | bytes 13344 | tf_op jit(solution)/shard_map/ppermute | solution.py:281
  18.2 0.0 collective-permute-done.2
  18.2 2.5 %collective-permute-start.5 = (bf16[64,416]{1,0:T(8,128)(2,1)S(1)}, bf16[64,416]{1,0:T(8,128)(2,1)S(1)}, u32[]{:S(2)}, u32[]{:S(2)}) collective-permute-start(bf16[64,416]{1,0:T(8,128)(2,1)S(1)} %constant_dynamic-update-slice_fusion.refs_0_), channel_id=1, source_target_pairs={{0,6},{1,7},{2,4},{3,5},{4,2},{5,3},{6,0},{7,1},{8,14},{9,15},{10,... | collective-permute-start | bytes 159752 | tf_op jit(solution)/shard_map/ppermute | solution.py:281
  20.7 0.5 %collective-permute-start.4 = (bf16[64,416]{1,0:T(8,128)(2,1)S(1)}, bf16[64,416]{1,0:T(8,128)(2,1)S(1)}, u32[]{:S(2)}, u32[]{:S(2)}) collective-permute-start(bf16[64,416]{1,0:T(8,128)(2,1)S(1)} %constant_dynamic-update-slice_fusion.refs_0_), channel_id=1, source_target_pairs={{0,4},{1,5},{2,6},{3,7},{4,0},{5,1},{6,2},{7,3},{8,12},{9,13},{10,... | collective-permute-start | bytes 159752 | tf_op jit(solution)/shard_map/ppermute | solution.py:281
  21.2 0.5 %collective-permute-start.3 = (bf16[64,416]{1,0:T(8,128)(2,1)S(1)}, bf16[64,416]{1,0:T(8,128)(2,1)S(1)}, u32[]{:S(2)}, u32[]{:S(2)}) collective-permute-start(bf16[64,416]{1,0:T(8,128)(2,1)S(1)} %constant_dynamic-update-slice_fusion.refs_0_), channel_id=1, source_target_pairs={{0,2},{1,3},{2,0},{3,1},{4,6},{5,7},{6,4},{7,5},{8,10},{9,11},{10,... | collective-permute-start | bytes 159752 | tf_op jit(solution)/shard_map/ppermute | solution.py:281
  21.8 0.0 collective-permute-start.6
  21.8 2.3 %collective-permute-done.5.refs_3_ = bf16[64,416]{1,0:T(8,128)(2,1)S(1)} collective-permute-done((bf16[64,416]{1,0:T(8,128)(2,1)S(1)}, bf16[64,416]{1,0:T(8,128)(2,1)S(1)}, u32[]{:S(2)}, u32[]{:S(2)}) %collective-permute-start.5) | collective-permute-done | bytes 53280 | tf_op jit(solution)/shard_map/ppermute | solution.py:281
  24.0 0.0 collective-permute-start.9
  24.0 1.0 %collective-permute-done.4.refs_2_ = bf16[64,416]{1,0:T(8,128)(2,1)S(1)} collective-permute-done((bf16[64,416]{1,0:T(8,128)(2,1)S(1)}, bf16[64,416]{1,0:T(8,128)(2,1)S(1)}, u32[]{:S(2)}, u32[]{:S(2)}) %collective-permute-start.4) | collective-permute-done | bytes 53280 | tf_op jit(solution)/shard_map/ppermute | solution.py:281
  25.0 0.0 collective-permute-start.8
  25.0 0.5 %collective-permute-done.3.refs_1_ = bf16[64,416]{1,0:T(8,128)(2,1)S(1)} collective-permute-done((bf16[64,416]{1,0:T(8,128)(2,1)S(1)}, bf16[64,416]{1,0:T(8,128)(2,1)S(1)}, u32[]{:S(2)}, u32[]{:S(2)}) %collective-permute-start.3) | collective-permute-done | bytes 53280 | tf_op jit(solution)/shard_map/ppermute | solution.py:281
  25.5 0.0 collective-permute-start.7
  25.5 0.0 collective-permute-done.6.refs_4_
  25.5 0.0 collective-permute-done.9.refs_7_
  25.5 0.7 %collective-permute-done.8.refs_6_ = bf16[64,416]{1,0:T(8,128)(2,1)S(1)} collective-permute-done((bf16[64,416]{1,0:T(8,128)(2,1)S(1)}, bf16[64,416]{1,0:T(8,128)(2,1)S(1)}, u32[]{:S(2)}, u32[]{:S(2)}) %collective-permute-start.8) | collective-permute-done | bytes 53280 | tf_op jit(solution)/shard_map/ppermute | solution.py:281
  26.2 0.5 %collective-permute-done.7.refs_5_ = bf16[64,416]{1,0:T(8,128)(2,1)S(1)} collective-permute-done((bf16[64,416]{1,0:T(8,128)(2,1)S(1)}, bf16[64,416]{1,0:T(8,128)(2,1)S(1)}, u32[]{:S(2)}, u32[]{:S(2)}) %collective-permute-start.7) | collective-permute-done | bytes 53280 | tf_op jit(solution)/shard_map/ppermute | solution.py:281
  26.8 1.1 %sample.1 = f32[1,256]{1,0:T(1,128)} custom-call(bf16[256,512]{1,0:T(8,128)(2,1)S(1)} %get-tuple-element.10.re_ref, bf16[256,512]{1,0:T(8,128)(2,1)S(1)} %get-tuple-element.11.im_ref, f32[256,416]{1,0:T(8,128)S(1)} %get-tuple-element.12.tail_re_ref, f32[256,416]{1,0:T(8,128)S(1)} %get-tuple-element.13.tail_im_ref, ...), custom_call_target="tpu_custom_call" | custom-call | flops 218103808 | bytes 1048576 | tf_op jit(solution)/shard_map/sample/pallas_call | solution.py:257
  (4 shorter events, 0.0 us)
Async XLA Ops:
  8.4 9.8 %collective-permute-start.2 = (bf16[16,416]{1,0:T(8,128)(2,1)S(1)}, bf16[16,416]{1,0:T(8,128)(2,1)S(1)}, u32[]{:S(2)}, u32[]{:S(2)}) collective-permute-start(bf16[16,416]{1,0:T(8,128)(2,1)S(1)} %get-tuple-element.14), channel_id=1, source_target_pairs={{0,24},{8,16},{16,8},{24,0},{1,25},{9,17},{17,9},{25,1},{2,26},{10... | collective-permute-start | bytes 39944 | tf_op jit(solution)/shard_map/ppermute | solution.py:281
  13.6 4.6 %collective-permute-start.1 = (bf16[16,416]{1,0:T(8,128)(2,1)S(1)}, bf16[16,416]{1,0:T(8,128)(2,1)S(1)}, u32[]{:S(2)}, u32[]{:S(2)}) collective-permute-start(bf16[16,416]{1,0:T(8,128)(2,1)S(1)} %get-tuple-element.14), channel_id=1, source_target_pairs={{0,16},{8,24},{16,0},{24,8},{1,17},{9,25},{17,1},{25,9},{2,18},{10... | collective-permute-start | bytes 39944 | tf_op jit(solution)/shard_map/ppermute | solution.py:281
  13.6 3.7 %collective-permute-start = (bf16[16,416]{1,0:T(8,128)(2,1)S(1)}, bf16[16,416]{1,0:T(8,128)(2,1)S(1)}, u32[]{:S(2)}, u32[]{:S(2)}) collective-permute-start(bf16[16,416]{1,0:T(8,128)(2,1)S(1)} %get-tuple-element.14), channel_id=1, source_target_pairs={{0,8},{8,0},{16,24},{24,16},{1,9},{9,1},{17,25},{25,17},{2,10},{10... | collective-permute-start | bytes 39944 | tf_op jit(solution)/shard_map/ppermute | solution.py:281
  18.2 5.8 %collective-permute-start.5 = (bf16[64,416]{1,0:T(8,128)(2,1)S(1)}, bf16[64,416]{1,0:T(8,128)(2,1)S(1)}, u32[]{:S(2)}, u32[]{:S(2)}) collective-permute-start(bf16[64,416]{1,0:T(8,128)(2,1)S(1)} %constant_dynamic-update-slice_fusion.refs_0_), channel_id=1, source_target_pairs={{0,6},{1,7},{2,4},{3,5},{4,2},{5,3},{6,0},{7,1},{8,14},{9,15},{10,... | collective-permute-start | bytes 159752 | tf_op jit(solution)/shard_map/ppermute | solution.py:281
  20.7 4.3 %collective-permute-start.4 = (bf16[64,416]{1,0:T(8,128)(2,1)S(1)}, bf16[64,416]{1,0:T(8,128)(2,1)S(1)}, u32[]{:S(2)}, u32[]{:S(2)}) collective-permute-start(bf16[64,416]{1,0:T(8,128)(2,1)S(1)} %constant_dynamic-update-slice_fusion.refs_0_), channel_id=1, source_target_pairs={{0,4},{1,5},{2,6},{3,7},{4,0},{5,1},{6,2},{7,3},{8,12},{9,13},{10,... | collective-permute-start | bytes 159752 | tf_op jit(solution)/shard_map/ppermute | solution.py:281
  21.2 4.3 %collective-permute-start.3 = (bf16[64,416]{1,0:T(8,128)(2,1)S(1)}, bf16[64,416]{1,0:T(8,128)(2,1)S(1)}, u32[]{:S(2)}, u32[]{:S(2)}) collective-permute-start(bf16[64,416]{1,0:T(8,128)(2,1)S(1)} %constant_dynamic-update-slice_fusion.refs_0_), channel_id=1, source_target_pairs={{0,2},{1,3},{2,0},{3,1},{4,6},{5,7},{6,4},{7,5},{8,10},{9,11},{10,... | collective-permute-start | bytes 159752 | tf_op jit(solution)/shard_map/ppermute | solution.py:281
  21.8 3.7 %collective-permute-start.6 = (bf16[64,416]{1,0:T(8,128)(2,1)S(1)}, bf16[64,416]{1,0:T(8,128)(2,1)S(1)}, u32[]{:S(2)}, u32[]{:S(2)}) collective-permute-start(bf16[64,416]{1,0:T(8,128)(2,1)S(1)} %constant_dynamic-update-slice_fusion.refs_0_), channel_id=1, source_target_pairs={{0,1},{1,0},{2,3},{3,2},{4,5},{5,4},{6,7},{7,6},{8,9},{9,8},{10,11... | collective-permute-start | bytes 159752 | tf_op jit(solution)/shard_map/ppermute | solution.py:281
  24.0 1.5 %collective-permute-start.9 = (bf16[64,416]{1,0:T(8,128)(2,1)S(1)}, bf16[64,416]{1,0:T(8,128)(2,1)S(1)}, u32[]{:S(2)}, u32[]{:S(2)}) collective-permute-start(bf16[64,416]{1,0:T(8,128)(2,1)S(1)} %collective-permute-done.5.refs_3_), channel_id=1, source_target_pairs={{0,1},{1,0},{2,3},{3,2},{4,5},{5,4},{6,7},{7,6},{8,9},{9,8},{10,11... | collective-permute-start | bytes 159752 | tf_op jit(solution)/shard_map/ppermute | solution.py:281
  25.0 1.3 %collective-permute-start.8 = (bf16[64,416]{1,0:T(8,128)(2,1)S(1)}, bf16[64,416]{1,0:T(8,128)(2,1)S(1)}, u32[]{:S(2)}, u32[]{:S(2)}) collective-permute-start(bf16[64,416]{1,0:T(8,128)(2,1)S(1)} %collective-permute-done.4.refs_2_), channel_id=1, source_target_pairs={{0,1},{1,0},{2,3},{3,2},{4,5},{5,4},{6,7},{7,6},{8,9},{9,8},{10,11... | collective-permute-start | bytes 159752 | tf_op jit(solution)/shard_map/ppermute | solution.py:281
  25.5 1.3 %collective-permute-start.7 = (bf16[64,416]{1,0:T(8,128)(2,1)S(1)}, bf16[64,416]{1,0:T(8,128)(2,1)S(1)}, u32[]{:S(2)}, u32[]{:S(2)}) collective-permute-start(bf16[64,416]{1,0:T(8,128)(2,1)S(1)} %collective-permute-done.3.refs_1_), channel_id=1, source_target_pairs={{0,1},{1,0},{2,3},{3,2},{4,5},{5,4},{6,7},{7,6},{8,9},{9,8},{10,11... | collective-permute-start | bytes 159752 | tf_op jit(solution)/shard_map/ppermute | solution.py:281

commit v5 on v4

--- a/solution.py
+++ b/solution.py
@@ -9,6 +9,7 @@
 from jax.sharding import PartitionSpec as P
 
 NT = (((1,), (1,)), ((), ()))
+LANES = 128
 VMEM = pl.BlockSpec(memory_space=pltpu.VMEM)
 
 
@@ -23,19 +24,18 @@
     return cos, sin * x
 
 
-def tap_phases(taps, turns):
-    total_re = taps[0] * jnp.ones_like(turns)
-    total_im = jnp.zeros_like(total_re)
-    for tap in range(1, 4):
-        cos, sin = cos_sin_turns(tap * turns)
-        total_re = total_re + taps[tap] * cos
-        total_im = total_im + taps[tap] * sin
-    return total_re, total_im
-
-
-def turned(turns, values):
-    cos, sin = cos_sin_turns(turns)
-    return cos * values[0] - sin * values[1], sin * values[0] + cos * values[1]
+def times(x, y):
+    return x[0] * y[0] - x[1] * y[1], x[1] * y[0] + x[0] * y[1]
+
+
+def tap_steps(turns):
+    return [cos_sin_turns(tap * turns) for tap in range(1, 4)]
+
+
+def tap_sum(taps, steps):
+    re = taps[0] + taps[1] * steps[0][0] + taps[2] * steps[1][0] + taps[3] * steps[2][0]
+    im = taps[1] * steps[0][1] + taps[2] * steps[1][1] + taps[3] * steps[2][1]
+    return re, im
 
 
 def divide(x, n):
@@ -72,20 +72,70 @@
     )
 
 
-def slot_weights(sizes, cols, order, quarter, k_lane, r_lane):
-    phi_total, lats, psi_count, _ = sizes
-    col = lambda i: cols[:, i : i + 1]
-    turns = order * (1.0 / phi_total)
-    phases = turned(col(12) * turns + quarter, tap_phases([col(4 + b) for b in range(4)], turns))
-    across = jnp.zeros((cols.shape[0], k_lane.shape[1]), jnp.float32)
+def lane_row():
+    return lax.broadcasted_iota(jnp.int32, (1, LANES), 1).astype(jnp.float32)
+
+
+def spread(values, first, each):
+    index = lax.broadcasted_iota(jnp.int32, values.shape, 1) // each + first
+    return jnp.take_along_axis(values, index, axis=1)
+
+
+def fixed_rows(sizes, n_strip, n_mr, orders, width):
+    phi_total, _, psi_count, _ = sizes
+
+    def first_order(source):
+        at, strip = divide(source, n_strip)
+        core, chip = divide(at, n_mr // 2)
+        strip = strip.astype(jnp.int32) ^ lax.axis_index("strip")
+        mr = (2.0 * chip + core).astype(jnp.int32) ^ lax.axis_index("mr")
+        return ((strip * n_mr + mr) * orders).astype(jnp.float32)
+
+    column = lax.broadcasted_iota(jnp.int32, (1, width), 1).astype(jnp.float32)
+    at, m_there = divide(column, orders)
+    source, _ = divide(at, 2)
+    order = first_order(source) + m_there
+    _, source = divide(lane_row(), n_strip * n_mr)
+    at, m_here = divide(lane_row(), orders)
+    _, part = divide(at, 2)
+    return (
+        first_order(source) * (1.0 / phi_total),
+        m_here * (1.0 / phi_total),
+        0.25 * part,
+        tap_steps(order * (1.0 / phi_total)),
+        tap_steps(lane_row() * (1.0 / psi_count)),
+    )
+
+
+def slot_weights(sizes, cols, fixed, orders, refs, here):
+    _, lats, psi_count, _ = sizes
+    source_turns, own_turns, quarter, phi_steps, psi_steps = fixed
+    re_ref, im_ref, tail_re_ref, tail_im_ref = refs
+    col = [jnp.broadcast_to(cols[:, i : i + 1], (cols.shape[0], LANES)) for i in range(15)]
+    source = cos_sin_turns(col[12] * source_turns)
+    own = cos_sin_turns(col[12] * own_turns + quarter)
+    for tile in range(0, re_ref.shape[1], LANES):
+        there = slice(tile, tile + LANES)
+        first = tile // (2 * orders)
+        steps = [(cos[:, there], sin[:, there]) for cos, sin in phi_steps]
+        turn = times(own, [spread(x, first, 2 * orders) for x in source])
+        re, im = times(turn, tap_sum(col[4:8], steps))
+        re_ref[here, there] = re.astype(jnp.bfloat16)
+        im_ref[here, there] = im.astype(jnp.bfloat16)
+    _, r_lane = divide(lane_row(), lats)
+    across = jnp.zeros_like(col[0])
     for a in range(4):
-        _, row = divide(col(13) + a, lats)
-        across = across + jnp.where(row == r_lane, col(a), 0.0)
-    tail_re, tail_im = turned(
-        divide(col(14) * k_lane, psi_count)[1] * (1.0 / psi_count),
-        tap_phases([col(8 + c) for c in range(4)], k_lane * (1.0 / psi_count)),
-    )
-    return phases + (tail_re * across, -tail_im * across)
+        _, row = divide(col[13] + a, lats)
+        across = across + jnp.where(row == r_lane, col[a], 0.0)
+    _, psi_turns = divide(col[14] * lane_row(), psi_count)
+    turn = cos_sin_turns(psi_turns * (1.0 / psi_count))
+    along_re, along_im = times(turn, tap_sum(col[8:12], psi_steps))
+    for tile in range(0, tail_re_ref.shape[1], LANES):
+        there = slice(tile, min(tile + LANES, tail_re_ref.shape[1]))
+        size = there.stop - there.start
+        first = tile // lats
+        tail_re_ref[here, there] = (spread(along_re, first, lats) * across)[:, :size]
+        tail_im_ref[here, there] = -(spread(along_im, first, lats) * across)[:, :size]
 
 
 def coef_kernel(
@@ -129,19 +179,7 @@
         copy.start()
     mixed[...] = jnp.zeros_like(mixed)
 
-    width = re_ref.shape[1]
-    at = lax.broadcasted_iota(jnp.int32, (1, width), 1).astype(jnp.float32)
-    at, m_row = divide(at, orders)
-    at, part = divide(at, 2)
-    at, strip = divide(at, n_strip)
-    core, chip = divide(at, n_mr // 2)
-    strip = strip.astype(jnp.int32) ^ lax.axis_index("strip")
-    mr = (2.0 * chip + core).astype(jnp.int32) ^ lax.axis_index("mr")
-    order = ((strip * n_mr + mr) * orders).astype(jnp.float32) + m_row
-    quarter = 0.25 * part
-    lane = lax.broadcasted_iota(jnp.int32, (1, lanes), 1).astype(jnp.float32)
-    k_lane, r_lane = divide(lane, lats)
-
+    fixed = fixed_rows(sizes, n_strip, n_mr, orders, re_ref.shape[1])
     for copy in slot:
         copy.wait()
     cols[...] = slot_rows(sizes, weights[...], base[...], counts[...], n_strip, n_mr).T
@@ -155,25 +193,30 @@
     for copy in small:
         copy.wait()
     mix(0)
-    for m in range(orders):
-        big[m].wait()
-        y = lax.dot_general(mixed[m], table[m], NT, preferred_element_type=jnp.float32)
-        of_row = lax.broadcasted_iota(jnp.int32, y.shape, 0) % k_pad
-        of_lane = lax.broadcasted_iota(jnp.int32, y.shape, 1) // lats
-        y = jnp.where(of_row == of_lane, y, 0.0)
-        for c in range(2):
-            total = jnp.sum(y[c * k_pad : (c + 1) * k_pad], axis=0, keepdims=True)
-            rows[c * orders + m : c * orders + m + 1, :] = total
-        here = slice(m * block, (m + 1) * block)
-        re, im, tail_re, tail_im = slot_weights(
-            sizes, cols[here], order, quarter, k_lane, r_lane
-        )
-        re_ref[here] = re.astype(jnp.bfloat16)
-        im_ref[here] = im.astype(jnp.bfloat16)
-        tail_re_ref[here] = tail_re
-        tail_im_ref[here] = tail_im
-        if m + 1 < orders:
-            mix(m + 1)
+    steps = [[0]] + [[m, m + 1] for m in range(1, orders - 1, 2)] + [[orders - 1]]
+    for step in steps:
+        for m in step:
+            big[m].wait()
+        for m in step:
+            y = lax.dot_general(mixed[m], table[m], NT, preferred_element_type=jnp.float32)
+            of_row = lax.broadcasted_iota(jnp.int32, y.shape, 0) % k_pad
+            of_lane = lax.broadcasted_iota(jnp.int32, y.shape, 1) // lats
+            y = jnp.where(of_row == of_lane, y, 0.0)
+            for c in range(2):
+                total = jnp.sum(y[c * k_pad : (c + 1) * k_pad], axis=0, keepdims=True)
+                rows[c * orders + m : c * orders + m + 1, :] = total
+        for m in step:
+            here = slice(m * block, (m + 1) * block)
+            slot_weights(
+                sizes,
+                cols[here],
+                fixed,
+                orders,
+                (re_ref, im_ref, tail_re_ref, tail_im_ref),
+                here,
+            )
+        for m in range(step[-1] + 1, min(step[-1] + 3, orders)):
+            mix(m)
     out_ref[...] = rows[...].astype(jnp.bfloat16)
 
 
@@ -235,9 +278,10 @@
     for part in parts:
         coef[start : start + part.shape[0], :] = part[...]
         start += part.shape[0]
-    real = jnp.dot(re_ref[...], coef[...], preferred_element_type=jnp.float32)
-    imag = jnp.dot(im_ref[...], coef[...], preferred_element_type=jnp.float32)
-    terms = real * tail_re_ref[...] + imag * tail_im_ref[...]
+    both = jnp.concatenate([re_ref[...], im_ref[...]], axis=0)
+    both = jnp.dot(both, coef[...], preferred_element_type=jnp.float32)
+    slots = re_ref.shape[0]
+    terms = both[:slots] * tail_re_ref[...] + both[slots:] * tail_im_ref[...]
     lanes = terms.shape[1]
     whole = lanes // 128 * 128
     total = jnp.zeros((1, terms.shape[0]), jnp.float32)

time: 28 us -> 26.4 us (0.943)
  Pallas kernels: 9.54 us -> 7.9 us
    pallas_call x1, Pallas kernels: 8.44 us -> 6.79 us  [local_part(): pl.pallas_call(functools.partial(coef_kernel, sizes), out_shape=(jax.Shap...]
where the time goes in v5:
time: 26.4 us; the launch traced here: 26.2 us
  starting transfers between devices  9.33 us (35%)
  waiting for transfers between devices  8.96 us (34%)
  Pallas kernels  7.9 us (30%)
    ppermute x10, starting transfers between devices, swap(): lax.ppermute(x, axis, [(i, i ^ d) for i in range(lax.axis_size(axis))])  9.33 us
    ppermute x10, waiting for transfers between devices, swap(): lax.ppermute(x, axis, [(i, i ^ d) for i in range(lax.axis_size(axis))])  8.96 us
    pallas_call x1, Pallas kernels, local_part(): pl.pallas_call(functools.partial(coef_kernel, sizes), out_shape=(jax.Shap...  6.79 us
    pallas_call x1, Pallas kernels, sample(): pl.pallas_call(sample_kernel, grid=(slots // block,), out_shape=jax.Shape...  1.11 us
  transfers between devices with their start and end apart: 10, of which 7 were waited for; matrix products, arithmetic and copies ran while one was open for 0% of the time, Pallas kernels for 0%

profile of v5, /device:TPU:0, one launch (start us, length us, event | category | flops | bytes accessed | tf_op | source)
XLA Modules:
  0.0 26.2 jit_solution(9751674023352960455)
XLA Ops:
  0.0 6.8 %coef.1 = (bf16[16,416]{1,0:T(8,128)(2,1)S(1)}, bf16[256,512]{1,0:T(8,128)(2,1)S(1)}, bf16[256,512]{1,0:T(8,128)(2,1)S(1)}, f32[256,416]{1,0:T(8,128)S(1)}, f32[256,416]{1,0:T(8,128)S(1)}) custom-call(bf16[2,8,2048]{2,1,0:T(8,128)(2,1)} %alm_hbm.1, f32[13,2048]{1,0:T(8,128)} %beam_hbm.1, bf16[8,416,2048]{2,1,0:T(8,128)(2,1)} %bitcast.3, ...), custom_call_target="tpu_custom_call" | custom-call | flops 27262976 | bytes 13631488 | tf_op jit(solution)/shard_map/coef/pallas_call | solution.py:232
  6.8 5.1 %collective-permute-start.2 = (bf16[16,416]{1,0:T(8,128)(2,1)S(1)}, bf16[16,416]{1,0:T(8,128)(2,1)S(1)}, u32[]{:S(2)}, u32[]{:S(2)}) collective-permute-start(bf16[16,416]{1,0:T(8,128)(2,1)S(1)} %get-tuple-element.14), channel_id=1, source_target_pairs={{0,24},{8,16},{16,8},{24,0},{1,25},{9,17},{17,9},{25,1},{2,26},{10... | collective-permute-start | bytes 39944 | tf_op jit(solution)/shard_map/ppermute | solution.py:325
  11.9 0.0 collective-permute-start.1
  11.9 0.6 %collective-permute-start = (bf16[16,416]{1,0:T(8,128)(2,1)S(1)}, bf16[16,416]{1,0:T(8,128)(2,1)S(1)}, u32[]{:S(2)}, u32[]{:S(2)}) collective-permute-start(bf16[16,416]{1,0:T(8,128)(2,1)S(1)} %get-tuple-element.14), channel_id=1, source_target_pairs={{0,8},{8,0},{16,24},{24,16},{1,9},{9,1},{17,25},{25,17},{2,10},{10... | collective-permute-start | bytes 39944 | tf_op jit(solution)/shard_map/ppermute | solution.py:325
  12.6 3.1 %collective-permute-done = bf16[16,416]{1,0:T(8,128)(2,1)S(1)} collective-permute-done((bf16[16,416]{1,0:T(8,128)(2,1)S(1)}, bf16[16,416]{1,0:T(8,128)(2,1)S(1)}, u32[]{:S(2)}, u32[]{:S(2)}) %collective-permute-start) | collective-permute-done | bytes 13344 | tf_op jit(solution)/shard_map/ppermute | solution.py:325
  15.7 0.9 %collective-permute-done.1 = bf16[16,416]{1,0:T(8,128)(2,1)S(1)} collective-permute-done((bf16[16,416]{1,0:T(8,128)(2,1)S(1)}, bf16[16,416]{1,0:T(8,128)(2,1)S(1)}, u32[]{:S(2)}, u32[]{:S(2)}) %collective-permute-start.1) | collective-permute-done | bytes 13344 | tf_op jit(solution)/shard_map/ppermute | solution.py:325
  16.6 0.0 collective-permute-done.2
  16.6 2.5 %collective-permute-start.5 = (bf16[64,416]{1,0:T(8,128)(2,1)S(1)}, bf16[64,416]{1,0:T(8,128)(2,1)S(1)}, u32[]{:S(2)}, u32[]{:S(2)}) collective-permute-start(bf16[64,416]{1,0:T(8,128)(2,1)S(1)} %constant_dynamic-update-slice_fusion.refs_0_), channel_id=1, source_target_pairs={{0,6},{1,7},{2,4},{3,5},{4,2},{5,3},{6,0},{7,1},{8,14},{9,15},{10,... | collective-permute-start | bytes 159752 | tf_op jit(solution)/shard_map/ppermute | solution.py:325
  19.1 0.5 %collective-permute-start.4 = (bf16[64,416]{1,0:T(8,128)(2,1)S(1)}, bf16[64,416]{1,0:T(8,128)(2,1)S(1)}, u32[]{:S(2)}, u32[]{:S(2)}) collective-permute-start(bf16[64,416]{1,0:T(8,128)(2,1)S(1)} %constant_dynamic-update-slice_fusion.refs_0_), channel_id=1, source_target_pairs={{0,4},{1,5},{2,6},{3,7},{4,0},{5,1},{6,2},{7,3},{8,12},{9,13},{10,... | collective-permute-start | bytes 159752 | tf_op jit(solution)/shard_map/ppermute | solution.py:325
  19.6 0.5 %collective-permute-start.3 = (bf16[64,416]{1,0:T(8,128)(2,1)S(1)}, bf16[64,416]{1,0:T(8,128)(2,1)S(1)}, u32[]{:S(2)}, u32[]{:S(2)}) collective-permute-start(bf16[64,416]{1,0:T(8,128)(2,1)S(1)} %constant_dynamic-update-slice_fusion.refs_0_), channel_id=1, source_target_pairs={{0,2},{1,3},{2,0},{3,1},{4,6},{5,7},{6,4},{7,5},{8,10},{9,11},{10,... | collective-permute-start | bytes 159752 | tf_op jit(solution)/shard_map/ppermute | solution.py:325
  20.1 0.0 collective-permute-start.6
  20.1 2.3 %collective-permute-done.5.refs_3_ = bf16[64,416]{1,0:T(8,128)(2,1)S(1)} collective-permute-done((bf16[64,416]{1,0:T(8,128)(2,1)S(1)}, bf16[64,416]{1,0:T(8,128)(2,1)S(1)}, u32[]{:S(2)}, u32[]{:S(2)}) %collective-permute-start.5) | collective-permute-done | bytes 53280 | tf_op jit(solution)/shard_map/ppermute | solution.py:325
  22.4 0.0 collective-permute-start.9
  22.4 1.0 %collective-permute-done.4.refs_2_ = bf16[64,416]{1,0:T(8,128)(2,1)S(1)} collective-permute-done((bf16[64,416]{1,0:T(8,128)(2,1)S(1)}, bf16[64,416]{1,0:T(8,128)(2,1)S(1)}, u32[]{:S(2)}, u32[]{:S(2)}) %collective-permute-start.4) | collective-permute-done | bytes 53280 | tf_op jit(solution)/shard_map/ppermute | solution.py:325
  23.3 0.0 collective-permute-start.8
  23.3 0.5 %collective-permute-done.3.refs_1_ = bf16[64,416]{1,0:T(8,128)(2,1)S(1)} collective-permute-done((bf16[64,416]{1,0:T(8,128)(2,1)S(1)}, bf16[64,416]{1,0:T(8,128)(2,1)S(1)}, u32[]{:S(2)}, u32[]{:S(2)}) %collective-permute-start.3) | collective-permute-done | bytes 53280 | tf_op jit(solution)/shard_map/ppermute | solution.py:325
  23.8 0.0 collective-permute-start.7
  23.9 0.0 collective-permute-done.6.refs_4_
  23.9 0.0 collective-permute-done.9.refs_7_
  23.9 0.7 %collective-permute-done.8.refs_6_ = bf16[64,416]{1,0:T(8,128)(2,1)S(1)} collective-permute-done((bf16[64,416]{1,0:T(8,128)(2,1)S(1)}, bf16[64,416]{1,0:T(8,128)(2,1)S(1)}, u32[]{:S(2)}, u32[]{:S(2)}) %collective-permute-start.8) | collective-permute-done | bytes 53280 | tf_op jit(solution)/shard_map/ppermute | solution.py:325
  24.6 0.5 %collective-permute-done.7.refs_5_ = bf16[64,416]{1,0:T(8,128)(2,1)S(1)} collective-permute-done((bf16[64,416]{1,0:T(8,128)(2,1)S(1)}, bf16[64,416]{1,0:T(8,128)(2,1)S(1)}, u32[]{:S(2)}, u32[]{:S(2)}) %collective-permute-start.7) | collective-permute-done | bytes 53280 | tf_op jit(solution)/shard_map/ppermute | solution.py:325
  25.1 1.1 %sample.1 = f32[1,256]{1,0:T(1,128)} custom-call(bf16[256,512]{1,0:T(8,128)(2,1)S(1)} %get-tuple-element.10.re_ref, bf16[256,512]{1,0:T(8,128)(2,1)S(1)} %get-tuple-element.11.im_ref, f32[256,416]{1,0:T(8,128)S(1)} %get-tuple-element.12.tail_re_ref, f32[256,416]{1,0:T(8,128)S(1)} %get-tuple-element.13.tail_im_ref, ...), custom_call_target="tpu_custom_call" | custom-call | flops 218103808 | bytes 1048576 | tf_op jit(solution)/shard_map/sample/pallas_call | solution.py:301
  (4 shorter events, 0.0 us)
Async XLA Ops:
  6.8 9.8 %collective-permute-start.2 = (bf16[16,416]{1,0:T(8,128)(2,1)S(1)}, bf16[16,416]{1,0:T(8,128)(2,1)S(1)}, u32[]{:S(2)}, u32[]{:S(2)}) collective-permute-start(bf16[16,416]{1,0:T(8,128)(2,1)S(1)} %get-tuple-element.14), channel_id=1, source_target_pairs={{0,24},{8,16},{16,8},{24,0},{1,25},{9,17},{17,9},{25,1},{2,26},{10... | collective-permute-start | bytes 39944 | tf_op jit(solution)/shard_map/ppermute | solution.py:325
  11.9 4.6 %collective-permute-start.1 = (bf16[16,416]{1,0:T(8,128)(2,1)S(1)}, bf16[16,416]{1,0:T(8,128)(2,1)S(1)}, u32[]{:S(2)}, u32[]{:S(2)}) collective-permute-start(bf16[16,416]{1,0:T(8,128)(2,1)S(1)} %get-tuple-element.14), channel_id=1, source_target_pairs={{0,16},{8,24},{16,0},{24,8},{1,17},{9,25},{17,1},{25,9},{2,18},{10... | collective-permute-start | bytes 39944 | tf_op jit(solution)/shard_map/ppermute | solution.py:325
  11.9 3.7 %collective-permute-start = (bf16[16,416]{1,0:T(8,128)(2,1)S(1)}, bf16[16,416]{1,0:T(8,128)(2,1)S(1)}, u32[]{:S(2)}, u32[]{:S(2)}) collective-permute-start(bf16[16,416]{1,0:T(8,128)(2,1)S(1)} %get-tuple-element.14), channel_id=1, source_target_pairs={{0,8},{8,0},{16,24},{24,16},{1,9},{9,1},{17,25},{25,17},{2,10},{10... | collective-permute-start | bytes 39944 | tf_op jit(solution)/shard_map/ppermute | solution.py:325
  16.6 5.8 %collective-permute-start.5 = (bf16[64,416]{1,0:T(8,128)(2,1)S(1)}, bf16[64,416]{1,0:T(8,128)(2,1)S(1)}, u32[]{:S(2)}, u32[]{:S(2)}) collective-permute-start(bf16[64,416]{1,0:T(8,128)(2,1)S(1)} %constant_dynamic-update-slice_fusion.refs_0_), channel_id=1, source_target_pairs={{0,6},{1,7},{2,4},{3,5},{4,2},{5,3},{6,0},{7,1},{8,14},{9,15},{10,... | collective-permute-start | bytes 159752 | tf_op jit(solution)/shard_map/ppermute | solution.py:325
  19.1 4.3 %collective-permute-start.4 = (bf16[64,416]{1,0:T(8,128)(2,1)S(1)}, bf16[64,416]{1,0:T(8,128)(2,1)S(1)}, u32[]{:S(2)}, u32[]{:S(2)}) collective-permute-start(bf16[64,416]{1,0:T(8,128)(2,1)S(1)} %constant_dynamic-update-slice_fusion.refs_0_), channel_id=1, source_target_pairs={{0,4},{1,5},{2,6},{3,7},{4,0},{5,1},{6,2},{7,3},{8,12},{9,13},{10,... | collective-permute-start | bytes 159752 | tf_op jit(solution)/shard_map/ppermute | solution.py:325
  19.6 4.3 %collective-permute-start.3 = (bf16[64,416]{1,0:T(8,128)(2,1)S(1)}, bf16[64,416]{1,0:T(8,128)(2,1)S(1)}, u32[]{:S(2)}, u32[]{:S(2)}) collective-permute-start(bf16[64,416]{1,0:T(8,128)(2,1)S(1)} %constant_dynamic-update-slice_fusion.refs_0_), channel_id=1, source_target_pairs={{0,2},{1,3},{2,0},{3,1},{4,6},{5,7},{6,4},{7,5},{8,10},{9,11},{10,... | collective-permute-start | bytes 159752 | tf_op jit(solution)/shard_map/ppermute | solution.py:325
  20.1 3.7 %collective-permute-start.6 = (bf16[64,416]{1,0:T(8,128)(2,1)S(1)}, bf16[64,416]{1,0:T(8,128)(2,1)S(1)}, u32[]{:S(2)}, u32[]{:S(2)}) collective-permute-start(bf16[64,416]{1,0:T(8,128)(2,1)S(1)} %constant_dynamic-update-slice_fusion.refs_0_), channel_id=1, source_target_pairs={{0,1},{1,0},{2,3},{3,2},{4,5},{5,4},{6,7},{7,6},{8,9},{9,8},{10,11... | collective-permute-start | bytes 159752 | tf_op jit(solution)/shard_map/ppermute | solution.py:325
  22.4 1.5 %collective-permute-start.9 = (bf16[64,416]{1,0:T(8,128)(2,1)S(1)}, bf16[64,416]{1,0:T(8,128)(2,1)S(1)}, u32[]{:S(2)}, u32[]{:S(2)}) collective-permute-start(bf16[64,416]{1,0:T(8,128)(2,1)S(1)} %collective-permute-done.5.refs_3_), channel_id=1, source_target_pairs={{0,1},{1,0},{2,3},{3,2},{4,5},{5,4},{6,7},{7,6},{8,9},{9,8},{10,11... | collective-permute-start | bytes 159752 | tf_op jit(solution)/shard_map/ppermute | solution.py:325
  23.3 1.3 %collective-permute-start.8 = (bf16[64,416]{1,0:T(8,128)(2,1)S(1)}, bf16[64,416]{1,0:T(8,128)(2,1)S(1)}, u32[]{:S(2)}, u32[]{:S(2)}) collective-permute-start(bf16[64,416]{1,0:T(8,128)(2,1)S(1)} %collective-permute-done.4.refs_2_), channel_id=1, source_target_pairs={{0,1},{1,0},{2,3},{3,2},{4,5},{5,4},{6,7},{7,6},{8,9},{9,8},{10,11... | collective-permute-start | bytes 159752 | tf_op jit(solution)/shard_map/ppermute | solution.py:325
  23.8 1.3 %collective-permute-start.7 = (bf16[64,416]{1,0:T(8,128)(2,1)S(1)}, bf16[64,416]{1,0:T(8,128)(2,1)S(1)}, u32[]{:S(2)}, u32[]{:S(2)}) collective-permute-start(bf16[64,416]{1,0:T(8,128)(2,1)S(1)} %collective-permute-done.3.refs_1_), channel_id=1, source_target_pairs={{0,1},{1,0},{2,3},{3,2},{4,5},{5,4},{6,7},{7,6},{8,9},{9,8},{10,11... | collective-permute-start | bytes 159752 | tf_op jit(solution)/shard_map/ppermute | solution.py:325

commit v6 on v5

--- a/solution.py
+++ b/solution.py
@@ -88,6 +88,7 @@
         at, strip = divide(source, n_strip)
         core, chip = divide(at, n_mr // 2)
         strip = strip.astype(jnp.int32) ^ lax.axis_index("strip")
+        _, chip = divide(n_mr // 2 - chip, n_mr // 2)
         mr = (2.0 * chip + core).astype(jnp.int32) ^ lax.axis_index("mr")
         return ((strip * n_mr + mr) * orders).astype(jnp.float32)
 
@@ -194,7 +195,7 @@
         copy.wait()
     mix(0)
     steps = [[0]] + [[m, m + 1] for m in range(1, orders - 1, 2)] + [[orders - 1]]
-    for step in steps:
+    for at, step in enumerate(steps):
         for m in step:
             big[m].wait()
         for m in step:
@@ -205,7 +206,7 @@
             for c in range(2):
                 total = jnp.sum(y[c * k_pad : (c + 1) * k_pad], axis=0, keepdims=True)
                 rows[c * orders + m : c * orders + m + 1, :] = total
-        for m in step:
+        for m in range(2 * at, min(2 * at + 2, orders)):
             here = slice(m * block, (m + 1) * block)
             slot_weights(
                 sizes,
@@ -272,46 +273,45 @@
     )
 
 
-def sample_kernel(re_ref, im_ref, tail_re_ref, tail_im_ref, *refs):
-    parts, out_ref, coef = refs[:-2], refs[-2], refs[-1]
+def sample_kernel(first, re_ref, im_ref, tail_re_ref, tail_im_ref, *refs):
+    *parts, before_ref, out_ref, coef = refs
     start = 0
     for part in parts:
         coef[start : start + part.shape[0], :] = part[...]
         start += part.shape[0]
-    both = jnp.concatenate([re_ref[...], im_ref[...]], axis=0)
-    both = jnp.dot(both, coef[...], preferred_element_type=jnp.float32)
-    slots = re_ref.shape[0]
-    terms = both[:slots] * tail_re_ref[...] + both[slots:] * tail_im_ref[...]
-    lanes = terms.shape[1]
-    whole = lanes // 128 * 128
-    total = jnp.zeros((1, terms.shape[0]), jnp.float32)
-    if whole:
-        tiles = [terms[:, i : i + 128] for i in range(0, whole, 128)]
-        total = total + jnp.sum(sum(tiles).T, axis=0, keepdims=True)
-    if whole < lanes:
-        total = total + jnp.sum(terms[:, whole:].T, axis=0, keepdims=True)
-    out_ref[...] = total
-
-
-def sample(phases, parts):
-    slots, width = phases[0].shape
-    lanes = phases[2].shape[1]
+    slots, lanes = tail_re_ref.shape
     block = min(slots, 256)
-    rows = lambda n: pl.BlockSpec((block, n), lambda i: (i, 0))
+    whole = lanes // LANES * LANES
+    for i in range(0, slots, block):
+        here = slice(i, i + block)
+        both = [ref[here, first : first + start] for ref in (re_ref, im_ref)]
+        both = jnp.concatenate(both, axis=0)
+        both = jnp.dot(both, coef[...], preferred_element_type=jnp.float32)
+        terms = both[:block] * tail_re_ref[here] + both[block:] * tail_im_ref[here]
+        total = before_ref[:, here]
+        if whole:
+            tiles = [terms[:, j : j + LANES] for j in range(0, whole, LANES)]
+            total = total + jnp.sum(sum(tiles).T, axis=0, keepdims=True)
+        if whole < lanes:
+            total = total + jnp.sum(terms[:, whole:].T, axis=0, keepdims=True)
+        out_ref[:, here] = total
+
+
+def sample(phases, first, parts, before):
+    slots, lanes = phases[2].shape
+    rows = sum(part.shape[0] for part in parts)
     return pl.pallas_call(
-        sample_kernel,
-        grid=(slots // block,),
+        functools.partial(sample_kernel, first),
         out_shape=jax.ShapeDtypeStruct((1, slots), jnp.float32),
-        in_specs=[rows(width), rows(width), rows(lanes), rows(lanes)]
-        + [pl.BlockSpec(part.shape, lambda i: (0, 0)) for part in parts],
-        out_specs=pl.BlockSpec((1, block), lambda i: (0, i)),
-        scratch_shapes=[pltpu.VMEM((width, lanes), jnp.bfloat16)],
+        in_specs=[VMEM] * (5 + len(parts)),
+        out_specs=VMEM,
+        scratch_shapes=[pltpu.VMEM((rows, lanes), jnp.bfloat16)],
         compiler_params=pltpu.CompilerParams(vmem_limit_bytes=32 << 20),
         cost_estimate=pl.CostEstimate(
-            flops=4 * slots * width * lanes, bytes_accessed=1 << 20, transcendentals=0
+            flops=4 * slots * rows * lanes, bytes_accessed=1 << 20, transcendentals=0
         ),
         name="sample",
-    )(*phases, *parts)
+    )(*phases, *parts, before)
 
 
 def on_device(alm, beam, wigner, base_index, interp_weights, live_counts):
@@ -326,9 +326,14 @@
 
     column = [swap(mine, "strip", d) for d in range(n_strip - 1, 0, -1)][::-1]
     column = jnp.concatenate([mine] + column, axis=0)
-    plane = [column] + [swap(column, "mr", d) for d in range(n_mr - 2, 0, -2)][::-1]
+    plane = [column] + [swap(column, "mr", d) for d in range(n_mr - 2, 0, -2)]
     other = [swap(part, "mr", 1) for part in plane]
-    return sample(phases, plane + other).reshape(-1)
+    parts = plane + other
+    early, late = parts[:-2], parts[-2:]
+    zero = jnp.zeros((1, base_index.shape[0]), jnp.float32)
+    result = sample(phases, 0, early, zero)
+    result = sample(phases, sum(part.shape[0] for part in early), late, result)
+    return result.reshape(-1)
 
 
 def solution(mesh):

time: 26.4 us -> 27.6 us (1.045)
  waiting for transfers between devices: 8.96 us -> 9.92 us
  Pallas kernels: 7.9 us -> 8.25 us
    ppermute x10, waiting for transfers between devices: 8.96 us -> 9.92 us  [swap(): lax.ppermute(x, axis, [(i, i ^ d) for i in range(lax.axis_size(axis))])]
    pallas_call x1 -> x2, Pallas kernels: 1.11 us -> 1.48 us  [sample(): pl.pallas_call(functools.partial(sample_kernel, first), out_shape=jax.Sha...]
  transfers between devices with their start and end apart: 10 -> 10, of which waited for: 7 -> 7; matrix products, arithmetic and copies ran while one was open for 0% -> 0% of each run, Pallas kernels for 0% -> 2%
where the time goes in v6:
time: 27.6 us; the launch traced here: 27.4 us
  waiting for transfers between devices  9.92 us (36%)
  starting transfers between devices  9.19 us (33%)
  Pallas kernels  8.25 us (30%)
    ppermute x10, waiting for transfers between devices, swap(): lax.ppermute(x, axis, [(i, i ^ d) for i in range(lax.axis_size(axis))])  9.92 us
    ppermute x10, starting transfers between devices, swap(): lax.ppermute(x, axis, [(i, i ^ d) for i in range(lax.axis_size(axis))])  9.19 us
    pallas_call x1, Pallas kernels, local_part(): pl.pallas_call(functools.partial(coef_kernel, sizes), out_shape=(jax.Shap...  6.77 us
    pallas_call x2, Pallas kernels, sample(): pl.pallas_call(functools.partial(sample_kernel, first), out_shape=jax.Sha...  1.48 us
  transfers between devices with their start and end apart: 10, of which 7 were waited for; matrix products, arithmetic and copies ran while one was open for 0% of the time, Pallas kernels for 2%

profile of v6, /device:TPU:0, one launch (start us, length us, event | category | flops | bytes accessed | tf_op | source)
XLA Modules:
  0.0 27.4 jit_solution(13352216570670213665)
XLA Ops:
  0.0 6.8 %coef.1 = (bf16[16,416]{1,0:T(8,128)(2,1)S(1)}, bf16[256,512]{1,0:T(8,128)(2,1)S(1)}, bf16[256,512]{1,0:T(8,128)(2,1)S(1)}, f32[256,416]{1,0:T(8,128)S(1)}, f32[256,416]{1,0:T(8,128)S(1)}) custom-call(bf16[2,8,2048]{2,1,0:T(8,128)(2,1)} %alm_hbm.1, f32[13,2048]{1,0:T(8,128)} %beam_hbm.1, bf16[8,416,2048]{2,1,0:T(8,128)(2,1)} %bitcast.3, ...), custom_call_target="tpu_custom_call" | custom-call | flops 27262976 | bytes 13631488 | tf_op jit(solution)/shard_map/coef/pallas_call | solution.py:233
  6.8 3.1 %collective-permute-start = (bf16[16,416]{1,0:T(8,128)(2,1)S(1)}, bf16[16,416]{1,0:T(8,128)(2,1)S(1)}, u32[]{:S(2)}, u32[]{:S(2)}) collective-permute-start(bf16[16,416]{1,0:T(8,128)(2,1)S(1)} %get-tuple-element.14), channel_id=1, source_target_pairs={{0,8},{8,0},{16,24},{24,16},{1,9},{9,1},{17,25},{25,17},{2,10},{10... | collective-permute-start | bytes 39944 | tf_op jit(solution)/shard_map/ppermute | solution.py:325
  9.9 2.6 %collective-permute-start.1 = (bf16[16,416]{1,0:T(8,128)(2,1)S(1)}, bf16[16,416]{1,0:T(8,128)(2,1)S(1)}, u32[]{:S(2)}, u32[]{:S(2)}) collective-permute-start(bf16[16,416]{1,0:T(8,128)(2,1)S(1)} %get-tuple-element.14), channel_id=1, source_target_pairs={{0,16},{8,24},{16,0},{24,8},{1,17},{9,25},{17,1},{25,9},{2,18},{10... | collective-permute-start | bytes 39944 | tf_op jit(solution)/shard_map/ppermute | solution.py:325
  12.5 0.0 collective-permute-start.2
  12.5 0.0 collective-permute-done
  12.5 2.1 %collective-permute-done.1 = bf16[16,416]{1,0:T(8,128)(2,1)S(1)} collective-permute-done((bf16[16,416]{1,0:T(8,128)(2,1)S(1)}, bf16[16,416]{1,0:T(8,128)(2,1)S(1)}, u32[]{:S(2)}, u32[]{:S(2)}) %collective-permute-start.1) | collective-permute-done | bytes 13344 | tf_op jit(solution)/shard_map/ppermute | solution.py:325
  14.6 3.4 %collective-permute-done.2 = bf16[16,416]{1,0:T(8,128)(2,1)S(1)} collective-permute-done((bf16[16,416]{1,0:T(8,128)(2,1)S(1)}, bf16[16,416]{1,0:T(8,128)(2,1)S(1)}, u32[]{:S(2)}, u32[]{:S(2)}) %collective-permute-start.2) | collective-permute-done | bytes 13344 | tf_op jit(solution)/shard_map/ppermute | solution.py:325
  18.0 2.4 %collective-permute-start.7 = (bf16[64,416]{1,0:T(8,128)(2,1)S(1)}, bf16[64,416]{1,0:T(8,128)(2,1)S(1)}, u32[]{:S(2)}, u32[]{:S(2)}) collective-permute-start(bf16[64,416]{1,0:T(8,128)(2,1)S(1)} %constant_dynamic-update-slice_fusion.refs_0_), channel_id=1, source_target_pairs={{0,6},{1,7},{2,4},{3,5},{4,2},{5,3},{6,0},{7,1},{8,14},{9,15},{10,... | collective-permute-start | bytes 159752 | tf_op jit(solution)/shard_map/ppermute | solution.py:325
  20.4 0.5 %collective-permute-start.3 = (bf16[64,416]{1,0:T(8,128)(2,1)S(1)}, bf16[64,416]{1,0:T(8,128)(2,1)S(1)}, u32[]{:S(2)}, u32[]{:S(2)}) collective-permute-start(bf16[64,416]{1,0:T(8,128)(2,1)S(1)} %constant_dynamic-update-slice_fusion.refs_0_), channel_id=1, source_target_pairs={{0,4},{1,5},{2,6},{3,7},{4,0},{5,1},{6,2},{7,3},{8,12},{9,13},{10,... | collective-permute-start | bytes 159752 | tf_op jit(solution)/shard_map/ppermute | solution.py:325
  21.0 0.5 %collective-permute-start.5 = (bf16[64,416]{1,0:T(8,128)(2,1)S(1)}, bf16[64,416]{1,0:T(8,128)(2,1)S(1)}, u32[]{:S(2)}, u32[]{:S(2)}) collective-permute-start(bf16[64,416]{1,0:T(8,128)(2,1)S(1)} %constant_dynamic-update-slice_fusion.refs_0_), channel_id=1, source_target_pairs={{0,2},{1,3},{2,0},{3,1},{4,6},{5,7},{6,4},{7,5},{8,10},{9,11},{10,... | collective-permute-start | bytes 159752 | tf_op jit(solution)/shard_map/ppermute | solution.py:325
  21.5 0.0 collective-permute-start.8
  21.5 2.0 %collective-permute-done.7.refs_1_ = bf16[64,416]{1,0:T(8,128)(2,1)S(1)} collective-permute-done((bf16[64,416]{1,0:T(8,128)(2,1)S(1)}, bf16[64,416]{1,0:T(8,128)(2,1)S(1)}, u32[]{:S(2)}, u32[]{:S(2)}) %collective-permute-start.7) | collective-permute-done | bytes 53280 | tf_op jit(solution)/shard_map/ppermute | solution.py:325
  23.5 0.0 collective-permute-start.9
  23.5 1.2 %collective-permute-done.3.refs_2_ = bf16[64,416]{1,0:T(8,128)(2,1)S(1)} collective-permute-done((bf16[64,416]{1,0:T(8,128)(2,1)S(1)}, bf16[64,416]{1,0:T(8,128)(2,1)S(1)}, u32[]{:S(2)}, u32[]{:S(2)}) %collective-permute-start.3) | collective-permute-done | bytes 53280 | tf_op jit(solution)/shard_map/ppermute | solution.py:325
  24.7 0.0 collective-permute-start.4
  24.7 0.5 %collective-permute-done.5.refs_3_ = bf16[64,416]{1,0:T(8,128)(2,1)S(1)} collective-permute-done((bf16[64,416]{1,0:T(8,128)(2,1)S(1)}, bf16[64,416]{1,0:T(8,128)(2,1)S(1)}, u32[]{:S(2)}, u32[]{:S(2)}) %collective-permute-start.5) | collective-permute-done | bytes 53280 | tf_op jit(solution)/shard_map/ppermute | solution.py:325
  25.2 0.0 collective-permute-start.6
  25.2 0.0 collective-permute-done.8.refs_4_
  25.2 0.0 collective-permute-done.9.refs_5_
  25.2 0.5 %sample.2.refs_2_ = f32[1,256]{1,0:T(1,128)S(1)} custom-call(bf16[256,512]{1,0:T(8,128)(2,1)S(1)} %get-tuple-element.10.re_ref, bf16[256,512]{1,0:T(8,128)(2,1)S(1)} %get-tuple-element.11.im_ref, f32[256,416]{1,0:T(8,128)S(1)} %get-tuple-element.12.tail_re_ref, f32[256,416]{1,0:T(8,128)S(1)} %get-tuple-element.13.tail_im_ref, ...), custom_call_target="tpu_custom_call" | custom-call | flops 163577856 | bytes 1048576 | tf_op jit(solution)/shard_map/sample/pallas_call | solution.py:303
  25.8 0.2 collective-permute-done.4.refs_0_
  26.0 0.5 %collective-permute-done.6.refs_1_ = bf16[64,416]{1,0:T(8,128)(2,1)S(1)} collective-permute-done((bf16[64,416]{1,0:T(8,128)(2,1)S(1)}, bf16[64,416]{1,0:T(8,128)(2,1)S(1)}, u32[]{:S(2)}, u32[]{:S(2)}) %collective-permute-start.6) | collective-permute-done | bytes 53280 | tf_op jit(solution)/shard_map/ppermute | solution.py:325
  26.5 0.9 %sample.3 = f32[1,256]{1,0:T(1,128)} custom-call(bf16[256,512]{1,0:T(8,128)(2,1)S(1)} %get-tuple-element.10.re_ref, bf16[256,512]{1,0:T(8,128)(2,1)S(1)} %get-tuple-element.11.im_ref, f32[256,416]{1,0:T(8,128)S(1)} %get-tuple-element.12.tail_re_ref, f32[256,416]{1,0:T(8,128)S(1)} %get-tuple-element.13.tail_im_ref, ...), custom_call_target="tpu_custom_call" | custom-call | flops 54525952 | bytes 1048576 | tf_op jit(solution)/shard_map/sample/pallas_call | solution.py:303
  (5 shorter events, 0.0 us)
Async XLA Ops:
  6.8 5.7 %collective-permute-start = (bf16[16,416]{1,0:T(8,128)(2,1)S(1)}, bf16[16,416]{1,0:T(8,128)(2,1)S(1)}, u32[]{:S(2)}, u32[]{:S(2)}) collective-permute-start(bf16[16,416]{1,0:T(8,128)(2,1)S(1)} %get-tuple-element.14), channel_id=1, source_target_pairs={{0,8},{8,0},{16,24},{24,16},{1,9},{9,1},{17,25},{25,17},{2,10},{10... | collective-permute-start | bytes 39944 | tf_op jit(solution)/shard_map/ppermute | solution.py:325
  9.9 4.7 %collective-permute-start.1 = (bf16[16,416]{1,0:T(8,128)(2,1)S(1)}, bf16[16,416]{1,0:T(8,128)(2,1)S(1)}, u32[]{:S(2)}, u32[]{:S(2)}) collective-permute-start(bf16[16,416]{1,0:T(8,128)(2,1)S(1)} %get-tuple-element.14), channel_id=1, source_target_pairs={{0,16},{8,24},{16,0},{24,8},{1,17},{9,25},{17,1},{25,9},{2,18},{10... | collective-permute-start | bytes 39944 | tf_op jit(solution)/shard_map/ppermute | solution.py:325
  12.5 5.5 %collective-permute-start.2 = (bf16[16,416]{1,0:T(8,128)(2,1)S(1)}, bf16[16,416]{1,0:T(8,128)(2,1)S(1)}, u32[]{:S(2)}, u32[]{:S(2)}) collective-permute-start(bf16[16,416]{1,0:T(8,128)(2,1)S(1)} %get-tuple-element.14), channel_id=1, source_target_pairs={{0,24},{8,16},{16,8},{24,0},{1,25},{9,17},{17,9},{25,1},{2,26},{10... | collective-permute-start | bytes 39944 | tf_op jit(solution)/shard_map/ppermute | solution.py:325
  18.0 5.5 %collective-permute-start.7 = (bf16[64,416]{1,0:T(8,128)(2,1)S(1)}, bf16[64,416]{1,0:T(8,128)(2,1)S(1)}, u32[]{:S(2)}, u32[]{:S(2)}) collective-permute-start(bf16[64,416]{1,0:T(8,128)(2,1)S(1)} %constant_dynamic-update-slice_fusion.refs_0_), channel_id=1, source_target_pairs={{0,6},{1,7},{2,4},{3,5},{4,2},{5,3},{6,0},{7,1},{8,14},{9,15},{10,... | collective-permute-start | bytes 159752 | tf_op jit(solution)/shard_map/ppermute | solution.py:325
  20.4 4.3 %collective-permute-start.3 = (bf16[64,416]{1,0:T(8,128)(2,1)S(1)}, bf16[64,416]{1,0:T(8,128)(2,1)S(1)}, u32[]{:S(2)}, u32[]{:S(2)}) collective-permute-start(bf16[64,416]{1,0:T(8,128)(2,1)S(1)} %constant_dynamic-update-slice_fusion.refs_0_), channel_id=1, source_target_pairs={{0,4},{1,5},{2,6},{3,7},{4,0},{5,1},{6,2},{7,3},{8,12},{9,13},{10,... | collective-permute-start | bytes 159752 | tf_op jit(solution)/shard_map/ppermute | solution.py:325
  21.0 4.3 %collective-permute-start.5 = (bf16[64,416]{1,0:T(8,128)(2,1)S(1)}, bf16[64,416]{1,0:T(8,128)(2,1)S(1)}, u32[]{:S(2)}, u32[]{:S(2)}) collective-permute-start(bf16[64,416]{1,0:T(8,128)(2,1)S(1)} %constant_dynamic-update-slice_fusion.refs_0_), channel_id=1, source_target_pairs={{0,2},{1,3},{2,0},{3,1},{4,6},{5,7},{6,4},{7,5},{8,10},{9,11},{10,... | collective-permute-start | bytes 159752 | tf_op jit(solution)/shard_map/ppermute | solution.py:325
  21.5 3.7 %collective-permute-start.8 = (bf16[64,416]{1,0:T(8,128)(2,1)S(1)}, bf16[64,416]{1,0:T(8,128)(2,1)S(1)}, u32[]{:S(2)}, u32[]{:S(2)}) collective-permute-start(bf16[64,416]{1,0:T(8,128)(2,1)S(1)} %constant_dynamic-update-slice_fusion.refs_0_), channel_id=1, source_target_pairs={{0,1},{1,0},{2,3},{3,2},{4,5},{5,4},{6,7},{7,6},{8,9},{9,8},{10,11... | collective-permute-start | bytes 159752 | tf_op jit(solution)/shard_map/ppermute | solution.py:325
  23.5 1.8 %collective-permute-start.9 = (bf16[64,416]{1,0:T(8,128)(2,1)S(1)}, bf16[64,416]{1,0:T(8,128)(2,1)S(1)}, u32[]{:S(2)}, u32[]{:S(2)}) collective-permute-start(bf16[64,416]{1,0:T(8,128)(2,1)S(1)} %collective-permute-done.7.refs_1_), channel_id=1, source_target_pairs={{0,1},{1,0},{2,3},{3,2},{4,5},{5,4},{6,7},{7,6},{8,9},{9,8},{10,11... | collective-permute-start | bytes 159752 | tf_op jit(solution)/shard_map/ppermute | solution.py:325
  24.7 1.3 %collective-permute-start.4 = (bf16[64,416]{1,0:T(8,128)(2,1)S(1)}, bf16[64,416]{1,0:T(8,128)(2,1)S(1)}, u32[]{:S(2)}, u32[]{:S(2)}) collective-permute-start(bf16[64,416]{1,0:T(8,128)(2,1)S(1)} %collective-permute-done.3.refs_2_), channel_id=1, source_target_pairs={{0,1},{1,0},{2,3},{3,2},{4,5},{5,4},{6,7},{7,6},{8,9},{9,8},{10,11... | collective-permute-start | bytes 159752 | tf_op jit(solution)/shard_map/ppermute | solution.py:325
  25.2 1.3 %collective-permute-start.6 = (bf16[64,416]{1,0:T(8,128)(2,1)S(1)}, bf16[64,416]{1,0:T(8,128)(2,1)S(1)}, u32[]{:S(2)}, u32[]{:S(2)}) collective-permute-start(bf16[64,416]{1,0:T(8,128)(2,1)S(1)} %collective-permute-done.5.refs_3_), channel_id=1, source_target_pairs={{0,1},{1,0},{2,3},{3,2},{4,5},{5,4},{6,7},{7,6},{8,9},{9,8},{10,11... | collective-permute-start | bytes 159752 | tf_op jit(solution)/shard_map/ppermute | solution.py:325

commit v7 on v6

--- a/solution.py
+++ b/solution.py
@@ -87,6 +87,7 @@
     def first_order(source):
         at, strip = divide(source, n_strip)
         core, chip = divide(at, n_mr // 2)
+        _, strip = divide(n_strip - strip, n_strip)
         strip = strip.astype(jnp.int32) ^ lax.axis_index("strip")
         _, chip = divide(n_mr // 2 - chip, n_mr // 2)
         mr = (2.0 * chip + core).astype(jnp.int32) ^ lax.axis_index("mr")
@@ -324,7 +325,7 @@
     def swap(x, axis, d):
         return lax.ppermute(x, axis, [(i, i ^ d) for i in range(lax.axis_size(axis))])
 
-    column = [swap(mine, "strip", d) for d in range(n_strip - 1, 0, -1)][::-1]
+    column = [swap(mine, "strip", d) for d in range(n_strip - 1, 0, -1)]
     column = jnp.concatenate([mine] + column, axis=0)
     plane = [column] + [swap(column, "mr", d) for d in range(n_mr - 2, 0, -2)]
     other = [swap(part, "mr", 1) for part in plane]

time: 27.6 us -> 26.2 us (0.949)
  waiting for transfers between devices: 9.92 us -> 8.4 us
    ppermute x10, waiting for transfers between devices: 9.92 us -> 8.4 us  [swap(): lax.ppermute(x, axis, [(i, i ^ d) for i in range(lax.axis_size(axis))])]
where the time goes in v7:
time: 26.2 us; the launch traced here: 26 us
  starting transfers between devices  9.33 us (36%)
  waiting for transfers between devices  8.4 us (32%)
  Pallas kernels  8.25 us (31%)
    ppermute x10, starting transfers between devices, swap(): lax.ppermute(x, axis, [(i, i ^ d) for i in range(lax.axis_size(axis))])  9.33 us
    ppermute x10, waiting for transfers between devices, swap(): lax.ppermute(x, axis, [(i, i ^ d) for i in range(lax.axis_size(axis))])  8.4 us
    pallas_call x1, Pallas kernels, local_part(): pl.pallas_call(functools.partial(coef_kernel, sizes), out_shape=(jax.Shap...  6.77 us
    pallas_call x2, Pallas kernels, sample(): pl.pallas_call(functools.partial(sample_kernel, first), out_shape=jax.Sha...  1.48 us
  transfers between devices with their start and end apart: 10, of which 7 were waited for; matrix products, arithmetic and copies ran while one was open for 0% of the time, Pallas kernels for 2%

profile of v7, /device:TPU:0, one launch (start us, length us, event | category | flops | bytes accessed | tf_op | source)
XLA Modules:
  0.0 26.0 jit_solution(11276849112140289753)
XLA Ops:
  0.0 6.8 %coef.1 = (bf16[16,416]{1,0:T(8,128)(2,1)S(1)}, bf16[256,512]{1,0:T(8,128)(2,1)S(1)}, bf16[256,512]{1,0:T(8,128)(2,1)S(1)}, f32[256,416]{1,0:T(8,128)S(1)}, f32[256,416]{1,0:T(8,128)S(1)}) custom-call(bf16[2,8,2048]{2,1,0:T(8,128)(2,1)} %alm_hbm.1, f32[13,2048]{1,0:T(8,128)} %beam_hbm.1, bf16[8,416,2048]{2,1,0:T(8,128)(2,1)} %bitcast.3, ...), custom_call_target="tpu_custom_call" | custom-call | flops 27262976 | bytes 13631488 | tf_op jit(solution)/shard_map/coef/pallas_call | solution.py:234
  6.8 5.1 %collective-permute-start = (bf16[16,416]{1,0:T(8,128)(2,1)S(1)}, bf16[16,416]{1,0:T(8,128)(2,1)S(1)}, u32[]{:S(2)}, u32[]{:S(2)}) collective-permute-start(bf16[16,416]{1,0:T(8,128)(2,1)S(1)} %get-tuple-element.14), channel_id=1, source_target_pairs={{0,24},{8,16},{16,8},{24,0},{1,25},{9,17},{17,9},{25,1},{2,26},{10... | collective-permute-start | bytes 39944 | tf_op jit(solution)/shard_map/ppermute | solution.py:326
  11.9 0.0 collective-permute-start.1
  11.9 0.6 %collective-permute-start.2 = (bf16[16,416]{1,0:T(8,128)(2,1)S(1)}, bf16[16,416]{1,0:T(8,128)(2,1)S(1)}, u32[]{:S(2)}, u32[]{:S(2)}) collective-permute-start(bf16[16,416]{1,0:T(8,128)(2,1)S(1)} %get-tuple-element.14), channel_id=1, source_target_pairs={{0,8},{8,0},{16,24},{24,16},{1,9},{9,1},{17,25},{25,17},{2,10},{10... | collective-permute-start | bytes 39944 | tf_op jit(solution)/shard_map/ppermute | solution.py:326
  12.5 1.1 %collective-permute-done = bf16[16,416]{1,0:T(8,128)(2,1)S(1)} collective-permute-done((bf16[16,416]{1,0:T(8,128)(2,1)S(1)}, bf16[16,416]{1,0:T(8,128)(2,1)S(1)}, u32[]{:S(2)}, u32[]{:S(2)}) %collective-permute-start) | collective-permute-done | bytes 13344 | tf_op jit(solution)/shard_map/ppermute | solution.py:326
  13.6 2.9 %collective-permute-done.1 = bf16[16,416]{1,0:T(8,128)(2,1)S(1)} collective-permute-done((bf16[16,416]{1,0:T(8,128)(2,1)S(1)}, bf16[16,416]{1,0:T(8,128)(2,1)S(1)}, u32[]{:S(2)}, u32[]{:S(2)}) %collective-permute-start.1) | collective-permute-done | bytes 13344 | tf_op jit(solution)/shard_map/ppermute | solution.py:326
  16.5 0.0 collective-permute-done.2
  16.5 2.5 %collective-permute-start.7 = (bf16[64,416]{1,0:T(8,128)(2,1)S(1)}, bf16[64,416]{1,0:T(8,128)(2,1)S(1)}, u32[]{:S(2)}, u32[]{:S(2)}) collective-permute-start(bf16[64,416]{1,0:T(8,128)(2,1)S(1)} %constant_dynamic-update-slice_fusion.refs_0_), channel_id=1, source_target_pairs={{0,6},{1,7},{2,4},{3,5},{4,2},{5,3},{6,0},{7,1},{8,14},{9,15},{10,... | collective-permute-start | bytes 159752 | tf_op jit(solution)/shard_map/ppermute | solution.py:326
  19.1 0.5 %collective-permute-start.3 = (bf16[64,416]{1,0:T(8,128)(2,1)S(1)}, bf16[64,416]{1,0:T(8,128)(2,1)S(1)}, u32[]{:S(2)}, u32[]{:S(2)}) collective-permute-start(bf16[64,416]{1,0:T(8,128)(2,1)S(1)} %constant_dynamic-update-slice_fusion.refs_0_), channel_id=1, source_target_pairs={{0,4},{1,5},{2,6},{3,7},{4,0},{5,1},{6,2},{7,3},{8,12},{9,13},{10,... | collective-permute-start | bytes 159752 | tf_op jit(solution)/shard_map/ppermute | solution.py:326
  19.6 0.5 %collective-permute-start.5 = (bf16[64,416]{1,0:T(8,128)(2,1)S(1)}, bf16[64,416]{1,0:T(8,128)(2,1)S(1)}, u32[]{:S(2)}, u32[]{:S(2)}) collective-permute-start(bf16[64,416]{1,0:T(8,128)(2,1)S(1)} %constant_dynamic-update-slice_fusion.refs_0_), channel_id=1, source_target_pairs={{0,2},{1,3},{2,0},{3,1},{4,6},{5,7},{6,4},{7,5},{8,10},{9,11},{10,... | collective-permute-start | bytes 159752 | tf_op jit(solution)/shard_map/ppermute | solution.py:326
  20.1 0.0 collective-permute-start.8
  20.1 2.3 %collective-permute-done.7.refs_1_ = bf16[64,416]{1,0:T(8,128)(2,1)S(1)} collective-permute-done((bf16[64,416]{1,0:T(8,128)(2,1)S(1)}, bf16[64,416]{1,0:T(8,128)(2,1)S(1)}, u32[]{:S(2)}, u32[]{:S(2)}) %collective-permute-start.7) | collective-permute-done | bytes 53280 | tf_op jit(solution)/shard_map/ppermute | solution.py:326
  22.4 0.0 collective-permute-start.9
  22.4 1.0 %collective-permute-done.3.refs_2_ = bf16[64,416]{1,0:T(8,128)(2,1)S(1)} collective-permute-done((bf16[64,416]{1,0:T(8,128)(2,1)S(1)}, bf16[64,416]{1,0:T(8,128)(2,1)S(1)}, u32[]{:S(2)}, u32[]{:S(2)}) %collective-permute-start.3) | collective-permute-done | bytes 53280 | tf_op jit(solution)/shard_map/ppermute | solution.py:326
  23.3 0.0 collective-permute-start.4
  23.3 0.5 %collective-permute-done.5.refs_3_ = bf16[64,416]{1,0:T(8,128)(2,1)S(1)} collective-permute-done((bf16[64,416]{1,0:T(8,128)(2,1)S(1)}, bf16[64,416]{1,0:T(8,128)(2,1)S(1)}, u32[]{:S(2)}, u32[]{:S(2)}) %collective-permute-start.5) | collective-permute-done | bytes 53280 | tf_op jit(solution)/shard_map/ppermute | solution.py:326
  23.8 0.0 collective-permute-start.6
  23.8 0.0 collective-permute-done.8.refs_4_
  23.8 0.0 collective-permute-done.9.refs_5_
  23.9 0.5 %sample.2.refs_2_ = f32[1,256]{1,0:T(1,128)S(1)} custom-call(bf16[256,512]{1,0:T(8,128)(2,1)S(1)} %get-tuple-element.10.re_ref, bf16[256,512]{1,0:T(8,128)(2,1)S(1)} %get-tuple-element.11.im_ref, f32[256,416]{1,0:T(8,128)S(1)} %get-tuple-element.12.tail_re_ref, f32[256,416]{1,0:T(8,128)S(1)} %get-tuple-element.13.tail_im_ref, ...), custom_call_target="tpu_custom_call" | custom-call | flops 163577856 | bytes 1048576 | tf_op jit(solution)/shard_map/sample/pallas_call | solution.py:304
  24.4 0.2 collective-permute-done.4.refs_0_
  24.6 0.5 %collective-permute-done.6.refs_1_ = bf16[64,416]{1,0:T(8,128)(2,1)S(1)} collective-permute-done((bf16[64,416]{1,0:T(8,128)(2,1)S(1)}, bf16[64,416]{1,0:T(8,128)(2,1)S(1)}, u32[]{:S(2)}, u32[]{:S(2)}) %collective-permute-start.6) | collective-permute-done | bytes 53280 | tf_op jit(solution)/shard_map/ppermute | solution.py:326
  25.1 0.9 %sample.3 = f32[1,256]{1,0:T(1,128)} custom-call(bf16[256,512]{1,0:T(8,128)(2,1)S(1)} %get-tuple-element.10.re_ref, bf16[256,512]{1,0:T(8,128)(2,1)S(1)} %get-tuple-element.11.im_ref, f32[256,416]{1,0:T(8,128)S(1)} %get-tuple-element.12.tail_re_ref, f32[256,416]{1,0:T(8,128)S(1)} %get-tuple-element.13.tail_im_ref, ...), custom_call_target="tpu_custom_call" | custom-call | flops 54525952 | bytes 1048576 | tf_op jit(solution)/shard_map/sample/pallas_call | solution.py:304
  (5 shorter events, 0.0 us)
Async XLA Ops:
  6.8 6.8 %collective-permute-start = (bf16[16,416]{1,0:T(8,128)(2,1)S(1)}, bf16[16,416]{1,0:T(8,128)(2,1)S(1)}, u32[]{:S(2)}, u32[]{:S(2)}) collective-permute-start(bf16[16,416]{1,0:T(8,128)(2,1)S(1)} %get-tuple-element.14), channel_id=1, source_target_pairs={{0,24},{8,16},{16,8},{24,0},{1,25},{9,17},{17,9},{25,1},{2,26},{10... | collective-permute-start | bytes 39944 | tf_op jit(solution)/shard_map/ppermute | solution.py:326
  11.9 4.6 %collective-permute-start.1 = (bf16[16,416]{1,0:T(8,128)(2,1)S(1)}, bf16[16,416]{1,0:T(8,128)(2,1)S(1)}, u32[]{:S(2)}, u32[]{:S(2)}) collective-permute-start(bf16[16,416]{1,0:T(8,128)(2,1)S(1)} %get-tuple-element.14), channel_id=1, source_target_pairs={{0,16},{8,24},{16,0},{24,8},{1,17},{9,25},{17,1},{25,9},{2,18},{10... | collective-permute-start | bytes 39944 | tf_op jit(solution)/shard_map/ppermute | solution.py:326
  11.9 4.6 %collective-permute-start.2 = (bf16[16,416]{1,0:T(8,128)(2,1)S(1)}, bf16[16,416]{1,0:T(8,128)(2,1)S(1)}, u32[]{:S(2)}, u32[]{:S(2)}) collective-permute-start(bf16[16,416]{1,0:T(8,128)(2,1)S(1)} %get-tuple-element.14), channel_id=1, source_target_pairs={{0,8},{8,0},{16,24},{24,16},{1,9},{9,1},{17,25},{25,17},{2,10},{10... | collective-permute-start | bytes 39944 | tf_op jit(solution)/shard_map/ppermute | solution.py:326
  16.5 5.8 %collective-permute-start.7 = (bf16[64,416]{1,0:T(8,128)(2,1)S(1)}, bf16[64,416]{1,0:T(8,128)(2,1)S(1)}, u32[]{:S(2)}, u32[]{:S(2)}) collective-permute-start(bf16[64,416]{1,0:T(8,128)(2,1)S(1)} %constant_dynamic-update-slice_fusion.refs_0_), channel_id=1, source_target_pairs={{0,6},{1,7},{2,4},{3,5},{4,2},{5,3},{6,0},{7,1},{8,14},{9,15},{10,... | collective-permute-start | bytes 159752 | tf_op jit(solution)/shard_map/ppermute | solution.py:326
  19.1 4.3 %collective-permute-start.3 = (bf16[64,416]{1,0:T(8,128)(2,1)S(1)}, bf16[64,416]{1,0:T(8,128)(2,1)S(1)}, u32[]{:S(2)}, u32[]{:S(2)}) collective-permute-start(bf16[64,416]{1,0:T(8,128)(2,1)S(1)} %constant_dynamic-update-slice_fusion.refs_0_), channel_id=1, source_target_pairs={{0,4},{1,5},{2,6},{3,7},{4,0},{5,1},{6,2},{7,3},{8,12},{9,13},{10,... | collective-permute-start | bytes 159752 | tf_op jit(solution)/shard_map/ppermute | solution.py:326
  19.6 4.3 %collective-permute-start.5 = (bf16[64,416]{1,0:T(8,128)(2,1)S(1)}, bf16[64,416]{1,0:T(8,128)(2,1)S(1)}, u32[]{:S(2)}, u32[]{:S(2)}) collective-permute-start(bf16[64,416]{1,0:T(8,128)(2,1)S(1)} %constant_dynamic-update-slice_fusion.refs_0_), channel_id=1, source_target_pairs={{0,2},{1,3},{2,0},{3,1},{4,6},{5,7},{6,4},{7,5},{8,10},{9,11},{10,... | collective-permute-start | bytes 159752 | tf_op jit(solution)/shard_map/ppermute | solution.py:326
  20.1 3.7 %collective-permute-start.8 = (bf16[64,416]{1,0:T(8,128)(2,1)S(1)}, bf16[64,416]{1,0:T(8,128)(2,1)S(1)}, u32[]{:S(2)}, u32[]{:S(2)}) collective-permute-start(bf16[64,416]{1,0:T(8,128)(2,1)S(1)} %constant_dynamic-update-slice_fusion.refs_0_), channel_id=1, source_target_pairs={{0,1},{1,0},{2,3},{3,2},{4,5},{5,4},{6,7},{7,6},{8,9},{9,8},{10,11... | collective-permute-start | bytes 159752 | tf_op jit(solution)/shard_map/ppermute | solution.py:326
  22.4 1.5 %collective-permute-start.9 = (bf16[64,416]{1,0:T(8,128)(2,1)S(1)}, bf16[64,416]{1,0:T(8,128)(2,1)S(1)}, u32[]{:S(2)}, u32[]{:S(2)}) collective-permute-start(bf16[64,416]{1,0:T(8,128)(2,1)S(1)} %collective-permute-done.7.refs_1_), channel_id=1, source_target_pairs={{0,1},{1,0},{2,3},{3,2},{4,5},{5,4},{6,7},{7,6},{8,9},{9,8},{10,11... | collective-permute-start | bytes 159752 | tf_op jit(solution)/shard_map/ppermute | solution.py:326
  23.3 1.3 %collective-permute-start.4 = (bf16[64,416]{1,0:T(8,128)(2,1)S(1)}, bf16[64,416]{1,0:T(8,128)(2,1)S(1)}, u32[]{:S(2)}, u32[]{:S(2)}) collective-permute-start(bf16[64,416]{1,0:T(8,128)(2,1)S(1)} %collective-permute-done.3.refs_2_), channel_id=1, source_target_pairs={{0,1},{1,0},{2,3},{3,2},{4,5},{5,4},{6,7},{7,6},{8,9},{9,8},{10,11... | collective-permute-start | bytes 159752 | tf_op jit(solution)/shard_map/ppermute | solution.py:326
  23.8 1.3 %collective-permute-start.6 = (bf16[64,416]{1,0:T(8,128)(2,1)S(1)}, bf16[64,416]{1,0:T(8,128)(2,1)S(1)}, u32[]{:S(2)}, u32[]{:S(2)}) collective-permute-start(bf16[64,416]{1,0:T(8,128)(2,1)S(1)} %collective-permute-done.5.refs_3_), channel_id=1, source_target_pairs={{0,1},{1,0},{2,3},{3,2},{4,5},{5,4},{6,7},{7,6},{8,9},{9,8},{10,11... | collective-permute-start | bytes 159752 | tf_op jit(solution)/shard_map/ppermute | solution.py:326

commit v8 on v7

--- a/solution.py
+++ b/solution.py
@@ -88,8 +88,10 @@
         at, strip = divide(source, n_strip)
         core, chip = divide(at, n_mr // 2)
         _, strip = divide(n_strip - strip, n_strip)
+        _, chip = divide(n_mr // 2 - chip, n_mr // 2)
+        crossed = (strip > 0.0).astype(jnp.float32) + (chip > 0.0).astype(jnp.float32)
+        _, core = divide(core + crossed, 2)
         strip = strip.astype(jnp.int32) ^ lax.axis_index("strip")
-        _, chip = divide(n_mr // 2 - chip, n_mr // 2)
         mr = (2.0 * chip + core).astype(jnp.int32) ^ lax.axis_index("mr")
         return ((strip * n_mr + mr) * orders).astype(jnp.float32)
 
@@ -322,13 +324,14 @@
         alm, beam, wigner, base_index, interp_weights, live_counts, n_strip, n_mr
     )
 
-    def swap(x, axis, d):
-        return lax.ppermute(x, axis, [(i, i ^ d) for i in range(lax.axis_size(axis))])
-
-    column = [swap(mine, "strip", d) for d in range(n_strip - 1, 0, -1)]
-    column = jnp.concatenate([mine] + column, axis=0)
-    plane = [column] + [swap(column, "mr", d) for d in range(n_mr - 2, 0, -2)]
-    other = [swap(part, "mr", 1) for part in plane]
+    def swap(x, strip, mr):
+        d = strip * n_mr + mr
+        return lax.ppermute(x, ("strip", "mr"), [(i, i ^ d) for i in range(n_strip * n_mr)])
+
+    column = [mine] + [swap(mine, strip, 1) for strip in range(n_strip - 1, 0, -1)]
+    column = jnp.concatenate(column, axis=0)
+    plane = [column] + [swap(column, 0, mr + 1) for mr in range(n_mr - 2, 0, -2)]
+    other = [swap(part, 0, 1) for part in plane]
     parts = plane + other
     early, late = parts[:-2], parts[-2:]
     zero = jnp.zeros((1, base_index.shape[0]), jnp.float32)

time: 26.2 us -> 25 us (0.954)
  waiting for transfers between devices: 8.4 us -> 6.97 us
    ppermute x10, waiting for transfers between devices: 8.4 us -> 6.97 us  [swap(): lax.ppermute(x, ('strip', 'mr'), [(i, i ^ d) for i in range(n_strip * n_m...]
  transfers between devices with their start and end apart: 10 -> 10, of which waited for: 7 -> 6; matrix products, arithmetic and copies ran while one was open for 0% -> 0% of each run, Pallas kernels for 2% -> 2%
where the time goes in v8:
time: 25 us; the launch traced here: 24.8 us
  starting transfers between devices  9.55 us (38%)
  Pallas kernels  8.25 us (33%)
  waiting for transfers between devices  6.97 us (28%)
    ppermute x10, starting transfers between devices, swap(): lax.ppermute(x, ('strip', 'mr'), [(i, i ^ d) for i in range(n_strip * n_m...  9.55 us
    ppermute x10, waiting for transfers between devices, swap(): lax.ppermute(x, ('strip', 'mr'), [(i, i ^ d) for i in range(n_strip * n_m...  6.97 us
    pallas_call x1, Pallas kernels, local_part(): pl.pallas_call(functools.partial(coef_kernel, sizes), out_shape=(jax.Shap...  6.77 us
    pallas_call x2, Pallas kernels, sample(): pl.pallas_call(functools.partial(sample_kernel, first), out_shape=jax.Sha...  1.48 us
  transfers between devices with their start and end apart: 10, of which 6 were waited for; matrix products, arithmetic and copies ran while one was open for 0% of the time, Pallas kernels for 2%

profile of v8, /device:TPU:0, one launch (start us, length us, event | category | flops | bytes accessed | tf_op | source)
XLA Modules:
  0.0 24.8 jit_solution(13796747473113895265)
XLA Ops:
  0.0 6.8 %coef.1 = (bf16[16,416]{1,0:T(8,128)(2,1)S(1)}, bf16[256,512]{1,0:T(8,128)(2,1)S(1)}, bf16[256,512]{1,0:T(8,128)(2,1)S(1)}, f32[256,416]{1,0:T(8,128)S(1)}, f32[256,416]{1,0:T(8,128)S(1)}) custom-call(bf16[2,8,2048]{2,1,0:T(8,128)(2,1)} %alm_hbm.1, f32[13,2048]{1,0:T(8,128)} %beam_hbm.1, bf16[8,416,2048]{2,1,0:T(8,128)(2,1)} %bitcast.3, ...), custom_call_target="tpu_custom_call" | custom-call | flops 27262976 | bytes 13631488 | tf_op jit(solution)/shard_map/coef/pallas_call | solution.py:236
  6.8 4.6 %collective-permute-start = (bf16[16,416]{1,0:T(8,128)(2,1)S(1)}, bf16[16,416]{1,0:T(8,128)(2,1)S(1)}, u32[]{:S(2)}, u32[]{:S(2)}) collective-permute-start(bf16[16,416]{1,0:T(8,128)(2,1)S(1)} %get-tuple-element.14), channel_id=1, source_target_pairs={{0,25},{1,24},{2,27},{3,26},{4,29},{5,28},{6,31},{7,30},{8,17},{9,... | collective-permute-start | bytes 39944 | tf_op jit(solution)/shard_map/ppermute | solution.py:329
  11.3 0.0 collective-permute-start.1
  11.3 0.9 %collective-permute-start.2 = (bf16[16,416]{1,0:T(8,128)(2,1)S(1)}, bf16[16,416]{1,0:T(8,128)(2,1)S(1)}, u32[]{:S(2)}, u32[]{:S(2)}) collective-permute-start(bf16[16,416]{1,0:T(8,128)(2,1)S(1)} %get-tuple-element.14), channel_id=1, source_target_pairs={{0,9},{1,8},{2,11},{3,10},{4,13},{5,12},{6,15},{7,14},{8,1},{9,0},... | collective-permute-start | bytes 39944 | tf_op jit(solution)/shard_map/ppermute | solution.py:329
  12.3 0.6 %collective-permute-done = bf16[16,416]{1,0:T(8,128)(2,1)S(1)} collective-permute-done((bf16[16,416]{1,0:T(8,128)(2,1)S(1)}, bf16[16,416]{1,0:T(8,128)(2,1)S(1)}, u32[]{:S(2)}, u32[]{:S(2)}) %collective-permute-start) | collective-permute-done | bytes 13344 | tf_op jit(solution)/shard_map/ppermute | solution.py:329
  12.8 2.7 %collective-permute-done.1 = bf16[16,416]{1,0:T(8,128)(2,1)S(1)} collective-permute-done((bf16[16,416]{1,0:T(8,128)(2,1)S(1)}, bf16[16,416]{1,0:T(8,128)(2,1)S(1)}, u32[]{:S(2)}, u32[]{:S(2)}) %collective-permute-start.1) | collective-permute-done | bytes 13344 | tf_op jit(solution)/shard_map/ppermute | solution.py:329
  15.5 0.0 collective-permute-done.2
  15.5 2.7 %collective-permute-start.7 = (bf16[64,416]{1,0:T(8,128)(2,1)S(1)}, bf16[64,416]{1,0:T(8,128)(2,1)S(1)}, u32[]{:S(2)}, u32[]{:S(2)}) collective-permute-start(bf16[64,416]{1,0:T(8,128)(2,1)S(1)} %constant_dynamic-update-slice_fusion.refs_0_), channel_id=1, source_target_pairs={{0,7},{1,6},{2,5},{3,4},{4,3},{5,2},{6,1},{7,0},{8,15},{9,14},{10,... | collective-permute-start | bytes 159752 | tf_op jit(solution)/shard_map/ppermute | solution.py:329
  18.2 0.1 collective-permute-start.3
  18.3 0.7 %collective-permute-start.5 = (bf16[64,416]{1,0:T(8,128)(2,1)S(1)}, bf16[64,416]{1,0:T(8,128)(2,1)S(1)}, u32[]{:S(2)}, u32[]{:S(2)}) collective-permute-start(bf16[64,416]{1,0:T(8,128)(2,1)S(1)} %constant_dynamic-update-slice_fusion.refs_0_), channel_id=1, source_target_pairs={{0,3},{1,2},{2,1},{3,0},{4,7},{5,6},{6,5},{7,4},{8,11},{9,10},{10,... | collective-permute-start | bytes 159752 | tf_op jit(solution)/shard_map/ppermute | solution.py:329
  19.0 0.0 collective-permute-start.8
  19.0 1.6 %collective-permute-done.7.refs_1_ = bf16[64,416]{1,0:T(8,128)(2,1)S(1)} collective-permute-done((bf16[64,416]{1,0:T(8,128)(2,1)S(1)}, bf16[64,416]{1,0:T(8,128)(2,1)S(1)}, u32[]{:S(2)}, u32[]{:S(2)}) %collective-permute-start.7) | collective-permute-done | bytes 53280 | tf_op jit(solution)/shard_map/ppermute | solution.py:329
  20.6 0.1 collective-permute-start.9
  20.7 1.7 %collective-permute-done.3.refs_2_ = bf16[64,416]{1,0:T(8,128)(2,1)S(1)} collective-permute-done((bf16[64,416]{1,0:T(8,128)(2,1)S(1)}, bf16[64,416]{1,0:T(8,128)(2,1)S(1)}, u32[]{:S(2)}, u32[]{:S(2)}) %collective-permute-start.3) | collective-permute-done | bytes 53280 | tf_op jit(solution)/shard_map/ppermute | solution.py:329
  22.5 0.1 collective-permute-start.4
  22.6 0.0 collective-permute-done.5.refs_3_
  22.6 0.4 %collective-permute-start.6 = (bf16[64,416]{1,0:T(8,128)(2,1)S(1)}, bf16[64,416]{1,0:T(8,128)(2,1)S(1)}, u32[]{:S(2)}, u32[]{:S(2)}) collective-permute-start(bf16[64,416]{1,0:T(8,128)(2,1)S(1)} %collective-permute-done.5.refs_3_), channel_id=1, source_target_pairs={{0,1},{1,0},{2,3},{3,2},{4,5},{5,4},{6,7},{7,6},{8,9},{9,8},{10,11... | collective-permute-start | bytes 159752 | tf_op jit(solution)/shard_map/ppermute | solution.py:329
  23.0 0.0 collective-permute-done.8.refs_4_
  23.0 0.0 collective-permute-done.9.refs_5_
  23.0 0.5 %sample.2.refs_2_ = f32[1,256]{1,0:T(1,128)S(1)} custom-call(bf16[256,512]{1,0:T(8,128)(2,1)S(1)} %get-tuple-element.10.re_ref, bf16[256,512]{1,0:T(8,128)(2,1)S(1)} %get-tuple-element.11.im_ref, f32[256,416]{1,0:T(8,128)S(1)} %get-tuple-element.12.tail_re_ref, f32[256,416]{1,0:T(8,128)S(1)} %get-tuple-element.13.tail_im_ref, ...), custom_call_target="tpu_custom_call" | custom-call | flops 163577856 | bytes 1048576 | tf_op jit(solution)/shard_map/sample/pallas_call | solution.py:306
  23.5 0.2 collective-permute-done.4.refs_0_
  23.7 0.2 collective-permute-done.6.refs_1_
  23.9 0.9 %sample.3 = f32[1,256]{1,0:T(1,128)} custom-call(bf16[256,512]{1,0:T(8,128)(2,1)S(1)} %get-tuple-element.10.re_ref, bf16[256,512]{1,0:T(8,128)(2,1)S(1)} %get-tuple-element.11.im_ref, f32[256,416]{1,0:T(8,128)S(1)} %get-tuple-element.12.tail_re_ref, f32[256,416]{1,0:T(8,128)S(1)} %get-tuple-element.13.tail_im_ref, ...), custom_call_target="tpu_custom_call" | custom-call | flops 54525952 | bytes 1048576 | tf_op jit(solution)/shard_map/sample/pallas_call | solution.py:306
  (5 shorter events, 0.0 us)
Async XLA Ops:
  6.8 6.0 %collective-permute-start = (bf16[16,416]{1,0:T(8,128)(2,1)S(1)}, bf16[16,416]{1,0:T(8,128)(2,1)S(1)}, u32[]{:S(2)}, u32[]{:S(2)}) collective-permute-start(bf16[16,416]{1,0:T(8,128)(2,1)S(1)} %get-tuple-element.14), channel_id=1, source_target_pairs={{0,25},{1,24},{2,27},{3,26},{4,29},{5,28},{6,31},{7,30},{8,17},{9,... | collective-permute-start | bytes 39944 | tf_op jit(solution)/shard_map/ppermute | solution.py:329
  11.3 4.2 %collective-permute-start.1 = (bf16[16,416]{1,0:T(8,128)(2,1)S(1)}, bf16[16,416]{1,0:T(8,128)(2,1)S(1)}, u32[]{:S(2)}, u32[]{:S(2)}) collective-permute-start(bf16[16,416]{1,0:T(8,128)(2,1)S(1)} %get-tuple-element.14), channel_id=1, source_target_pairs={{0,17},{1,16},{2,19},{3,18},{4,21},{5,20},{6,23},{7,22},{8,25},{9,... | collective-permute-start | bytes 39944 | tf_op jit(solution)/shard_map/ppermute | solution.py:329
  11.3 4.2 %collective-permute-start.2 = (bf16[16,416]{1,0:T(8,128)(2,1)S(1)}, bf16[16,416]{1,0:T(8,128)(2,1)S(1)}, u32[]{:S(2)}, u32[]{:S(2)}) collective-permute-start(bf16[16,416]{1,0:T(8,128)(2,1)S(1)} %get-tuple-element.14), channel_id=1, source_target_pairs={{0,9},{1,8},{2,11},{3,10},{4,13},{5,12},{6,15},{7,14},{8,1},{9,0},... | collective-permute-start | bytes 39944 | tf_op jit(solution)/shard_map/ppermute | solution.py:329
  15.5 5.1 %collective-permute-start.7 = (bf16[64,416]{1,0:T(8,128)(2,1)S(1)}, bf16[64,416]{1,0:T(8,128)(2,1)S(1)}, u32[]{:S(2)}, u32[]{:S(2)}) collective-permute-start(bf16[64,416]{1,0:T(8,128)(2,1)S(1)} %constant_dynamic-update-slice_fusion.refs_0_), channel_id=1, source_target_pairs={{0,7},{1,6},{2,5},{3,4},{4,3},{5,2},{6,1},{7,0},{8,15},{9,14},{10,... | collective-permute-start | bytes 159752 | tf_op jit(solution)/shard_map/ppermute | solution.py:329
  18.2 4.3 %collective-permute-start.3 = (bf16[64,416]{1,0:T(8,128)(2,1)S(1)}, bf16[64,416]{1,0:T(8,128)(2,1)S(1)}, u32[]{:S(2)}, u32[]{:S(2)}) collective-permute-start(bf16[64,416]{1,0:T(8,128)(2,1)S(1)} %constant_dynamic-update-slice_fusion.refs_0_), channel_id=1, source_target_pairs={{0,5},{1,4},{2,7},{3,6},{4,1},{5,0},{6,3},{7,2},{8,13},{9,12},{10,... | collective-permute-start | bytes 159752 | tf_op jit(solution)/shard_map/ppermute | solution.py:329
  18.3 4.3 %collective-permute-start.5 = (bf16[64,416]{1,0:T(8,128)(2,1)S(1)}, bf16[64,416]{1,0:T(8,128)(2,1)S(1)}, u32[]{:S(2)}, u32[]{:S(2)}) collective-permute-start(bf16[64,416]{1,0:T(8,128)(2,1)S(1)} %constant_dynamic-update-slice_fusion.refs_0_), channel_id=1, source_target_pairs={{0,3},{1,2},{2,1},{3,0},{4,7},{5,6},{6,5},{7,4},{8,11},{9,10},{10,... | collective-permute-start | bytes 159752 | tf_op jit(solution)/shard_map/ppermute | solution.py:329
  19.0 4.0 %collective-permute-start.8 = (bf16[64,416]{1,0:T(8,128)(2,1)S(1)}, bf16[64,416]{1,0:T(8,128)(2,1)S(1)}, u32[]{:S(2)}, u32[]{:S(2)}) collective-permute-start(bf16[64,416]{1,0:T(8,128)(2,1)S(1)} %constant_dynamic-update-slice_fusion.refs_0_), channel_id=1, source_target_pairs={{0,1},{1,0},{2,3},{3,2},{4,5},{5,4},{6,7},{7,6},{8,9},{9,8},{10,11... | collective-permute-start | bytes 159752 | tf_op jit(solution)/shard_map/ppermute | solution.py:329
  20.6 2.4 %collective-permute-start.9 = (bf16[64,416]{1,0:T(8,128)(2,1)S(1)}, bf16[64,416]{1,0:T(8,128)(2,1)S(1)}, u32[]{:S(2)}, u32[]{:S(2)}) collective-permute-start(bf16[64,416]{1,0:T(8,128)(2,1)S(1)} %collective-permute-done.7.refs_1_), channel_id=1, source_target_pairs={{0,1},{1,0},{2,3},{3,2},{4,5},{5,4},{6,7},{7,6},{8,9},{9,8},{10,11... | collective-permute-start | bytes 159752 | tf_op jit(solution)/shard_map/ppermute | solution.py:329
  22.5 1.3 %collective-permute-start.4 = (bf16[64,416]{1,0:T(8,128)(2,1)S(1)}, bf16[64,416]{1,0:T(8,128)(2,1)S(1)}, u32[]{:S(2)}, u32[]{:S(2)}) collective-permute-start(bf16[64,416]{1,0:T(8,128)(2,1)S(1)} %collective-permute-done.3.refs_2_), channel_id=1, source_target_pairs={{0,1},{1,0},{2,3},{3,2},{4,5},{5,4},{6,7},{7,6},{8,9},{9,8},{10,11... | collective-permute-start | bytes 159752 | tf_op jit(solution)/shard_map/ppermute | solution.py:329
  22.6 1.3 %collective-permute-start.6 = (bf16[64,416]{1,0:T(8,128)(2,1)S(1)}, bf16[64,416]{1,0:T(8,128)(2,1)S(1)}, u32[]{:S(2)}, u32[]{:S(2)}) collective-permute-start(bf16[64,416]{1,0:T(8,128)(2,1)S(1)} %collective-permute-done.5.refs_3_), channel_id=1, source_target_pairs={{0,1},{1,0},{2,3},{3,2},{4,5},{5,4},{6,7},{7,6},{8,9},{9,8},{10,11... | collective-permute-start | bytes 159752 | tf_op jit(solution)/shard_map/ppermute | solution.py:329

commit v9 on v6

--- a/solution.py
+++ b/solution.py
@@ -85,10 +85,17 @@
     phi_total, _, psi_count, _ = sizes
 
     def first_order(source):
-        at, strip = divide(source, n_strip)
+        half = n_strip // 2
+        at, block = divide(source, n_strip)
         core, chip = divide(at, n_mr // 2)
+        _, chip = divide(n_mr // 2 - chip, n_mr // 2)
+        core = core + (chip > 0.0).astype(jnp.float32)
+        own = (lax.axis_index("mr") % 2).astype(jnp.float32)
+        _, sender = divide(core + own, 2)
+        pair, second = divide(block - 2.0, 2)
+        strip = jnp.where(block < 2.0, block * half, pair + 1.0 + sender * half)
+        _, core = divide(core + jnp.where(block < 2.0, 0.0, second), 2)
         strip = strip.astype(jnp.int32) ^ lax.axis_index("strip")
-        _, chip = divide(n_mr // 2 - chip, n_mr // 2)
         mr = (2.0 * chip + core).astype(jnp.int32) ^ lax.axis_index("mr")
         return ((strip * n_mr + mr) * orders).astype(jnp.float32)
 
@@ -321,13 +328,18 @@
         alm, beam, wigner, base_index, interp_weights, live_counts, n_strip, n_mr
     )
 
-    def swap(x, axis, d):
-        return lax.ppermute(x, axis, [(i, i ^ d) for i in range(lax.axis_size(axis))])
-
-    column = [swap(mine, "strip", d) for d in range(n_strip - 1, 0, -1)][::-1]
-    column = jnp.concatenate([mine] + column, axis=0)
-    plane = [column] + [swap(column, "mr", d) for d in range(n_mr - 2, 0, -2)]
-    other = [swap(part, "mr", 1) for part in plane]
+    def swap(x, even, odd=None):
+        masks = (even, even if odd is None else odd)
+        pairs = [(i, i ^ masks[i % 2]) for i in range(n_strip * n_mr)]
+        return lax.ppermute(x, ("strip", "mr"), pairs)
+
+    half = n_strip // 2
+    opposite = swap(mine, half * n_mr)
+    pair = jnp.concatenate([mine, swap(mine, 1)], axis=0)
+    column = [swap(pair, d * n_mr, (d + half) * n_mr) for d in range(1, half)]
+    column = jnp.concatenate([mine, opposite] + column, axis=0)
+    plane = [column] + [swap(column, mr + 1) for mr in range(n_mr - 2, 0, -2)]
+    other = [swap(part, 1) for part in plane]
     parts = plane + other
     early, late = parts[:-2], parts[-2:]
     zero = jnp.zeros((1, base_index.shape[0]), jnp.float32)

time: 27.6 us -> 24.6 us (0.89)
  waiting for transfers between devices: 9.92 us -> 6.14 us
  starting transfers between devices: 9.19 us -> 10 us
    ppermute x10, waiting for transfers between devices: 9.92 us -> 6.14 us  [swap(): return lax.ppermute(x, ('strip', 'mr'), pairs)]
    ppermute x10, starting transfers between devices: 9.19 us -> 10 us  [swap(): return lax.ppermute(x, ('strip', 'mr'), pairs)]
  transfers between devices with their start and end apart: 10 -> 10, of which waited for: 7 -> 6; matrix products, arithmetic and copies ran while one was open for 0% -> 0% of each run, Pallas kernels for 2% -> 2%
where the time goes in v9:
time: 24.6 us; the launch traced here: 24.5 us
  starting transfers between devices  10 us (41%)
  Pallas kernels  8.25 us (34%)
  waiting for transfers between devices  6.14 us (25%)
    ppermute x10, starting transfers between devices, swap(): return lax.ppermute(x, ('strip', 'mr'), pairs)  10 us
    pallas_call x1, Pallas kernels, local_part(): pl.pallas_call(functools.partial(coef_kernel, sizes), out_shape=(jax.Shap...  6.77 us
    ppermute x10, waiting for transfers between devices, swap(): return lax.ppermute(x, ('strip', 'mr'), pairs)  6.14 us
    pallas_call x2, Pallas kernels, sample(): pl.pallas_call(functools.partial(sample_kernel, first), out_shape=jax.Sha...  1.48 us
  transfers between devices with their start and end apart: 10, of which 6 were waited for; matrix products, arithmetic and copies ran while one was open for 0% of the time, Pallas kernels for 2%

profile of v9, /device:TPU:0, one launch (start us, length us, event | category | flops | bytes accessed | tf_op | source)
XLA Modules:
  0.0 24.5 jit_solution(6088553764036498453)
XLA Ops:
  0.0 6.8 %coef.1 = (bf16[16,416]{1,0:T(8,128)(2,1)S(1)}, bf16[256,512]{1,0:T(8,128)(2,1)S(1)}, bf16[256,512]{1,0:T(8,128)(2,1)S(1)}, f32[256,416]{1,0:T(8,128)S(1)}, f32[256,416]{1,0:T(8,128)S(1)}) custom-call(bf16[2,8,2048]{2,1,0:T(8,128)(2,1)} %alm_hbm.1, f32[13,2048]{1,0:T(8,128)} %beam_hbm.1, bf16[8,416,2048]{2,1,0:T(8,128)(2,1)} %bitcast.3, ...), custom_call_target="tpu_custom_call" | custom-call | flops 27262976 | bytes 13631488 | tf_op jit(solution)/shard_map/coef/pallas_call | solution.py:240
  6.8 0.5 %collective-permute-start.1 = (bf16[16,416]{1,0:T(8,128)(2,1)S(1)}, bf16[16,416]{1,0:T(8,128)(2,1)S(1)}, u32[]{:S(2)}, u32[]{:S(2)}) collective-permute-start(bf16[16,416]{1,0:T(8,128)(2,1)S(1)} %get-tuple-element.14), channel_id=1, source_target_pairs={{0,1},{1,0},{2,3},{3,2},{4,5},{5,4},{6,7},{7,6},{8,9},{9,8},{10,11... | collective-permute-start | bytes 39944 | tf_op jit(solution)/shard_map/ppermute | solution.py:334
  7.3 3.7 %collective-permute-start = (bf16[16,416]{1,0:T(8,128)(2,1)S(1)}, bf16[16,416]{1,0:T(8,128)(2,1)S(1)}, u32[]{:S(2)}, u32[]{:S(2)}) collective-permute-start(bf16[16,416]{1,0:T(8,128)(2,1)S(1)} %get-tuple-element.14), channel_id=1, source_target_pairs={{0,16},{1,17},{2,18},{3,19},{4,20},{5,21},{6,22},{7,23},{8,24},{9,... | collective-permute-start | bytes 39944 | tf_op jit(solution)/shard_map/ppermute | solution.py:334
  11.0 0.0 collective-permute-done.1
  11.0 1.6 %collective-permute-start.2 = (bf16[32,416]{1,0:T(8,128)(2,1)S(1)}, bf16[32,416]{1,0:T(8,128)(2,1)S(1)}, u32[]{:S(2)}, u32[]{:S(2)}) collective-permute-start(bf16[32,416]{1,0:T(8,128)(2,1)S(1)} %pad_maximum_fusion), channel_id=1, source_target_pairs={{0,8},{1,25},{2,10},{3,27},{4,12},{5,29},{6,14},{7,31},{8,0},{9,17... | collective-permute-start | bytes 79880 | tf_op jit(solution)/shard_map/ppermute | solution.py:334
  12.6 0.1 collective-permute-done
  12.7 2.3 %collective-permute-done.2 = bf16[32,416]{1,0:T(8,128)(2,1)S(1)} collective-permute-done((bf16[32,416]{1,0:T(8,128)(2,1)S(1)}, bf16[32,416]{1,0:T(8,128)(2,1)S(1)}, u32[]{:S(2)}, u32[]{:S(2)}) %collective-permute-start.2) | collective-permute-done | bytes 26656 | tf_op jit(solution)/shard_map/ppermute | solution.py:334
  15.0 2.9 %collective-permute-start.7 = (bf16[64,416]{1,0:T(8,128)(2,1)S(1)}, bf16[64,416]{1,0:T(8,128)(2,1)S(1)}, u32[]{:S(2)}, u32[]{:S(2)}) collective-permute-start(bf16[64,416]{1,0:T(8,128)(2,1)S(1)} %constant_dynamic-update-slice_fusion.refs_0_), channel_id=1, source_target_pairs={{0,7},{1,6},{2,5},{3,4},{4,3},{5,2},{6,1},{7,0},{8,15},{9,14},{10,... | collective-permute-start | bytes 159752 | tf_op jit(solution)/shard_map/ppermute | solution.py:334
  17.8 0.0 collective-permute-start.3
  17.8 0.8 %collective-permute-start.5 = (bf16[64,416]{1,0:T(8,128)(2,1)S(1)}, bf16[64,416]{1,0:T(8,128)(2,1)S(1)}, u32[]{:S(2)}, u32[]{:S(2)}) collective-permute-start(bf16[64,416]{1,0:T(8,128)(2,1)S(1)} %constant_dynamic-update-slice_fusion.refs_0_), channel_id=1, source_target_pairs={{0,3},{1,2},{2,1},{3,0},{4,7},{5,6},{6,5},{7,4},{8,11},{9,10},{10,... | collective-permute-start | bytes 159752 | tf_op jit(solution)/shard_map/ppermute | solution.py:334
  18.6 0.0 collective-permute-start.8
  18.6 1.7 %collective-permute-done.7.refs_1_ = bf16[64,416]{1,0:T(8,128)(2,1)S(1)} collective-permute-done((bf16[64,416]{1,0:T(8,128)(2,1)S(1)}, bf16[64,416]{1,0:T(8,128)(2,1)S(1)}, u32[]{:S(2)}, u32[]{:S(2)}) %collective-permute-start.7) | collective-permute-done | bytes 53280 | tf_op jit(solution)/shard_map/ppermute | solution.py:334
  20.3 0.1 collective-permute-start.9
  20.4 1.7 %collective-permute-done.3.refs_2_ = bf16[64,416]{1,0:T(8,128)(2,1)S(1)} collective-permute-done((bf16[64,416]{1,0:T(8,128)(2,1)S(1)}, bf16[64,416]{1,0:T(8,128)(2,1)S(1)}, u32[]{:S(2)}, u32[]{:S(2)}) %collective-permute-start.3) | collective-permute-done | bytes 53280 | tf_op jit(solution)/shard_map/ppermute | solution.py:334
  22.1 0.0 collective-permute-start.4
  22.1 0.0 collective-permute-done.5.refs_3_
  22.1 0.5 %collective-permute-start.6 = (bf16[64,416]{1,0:T(8,128)(2,1)S(1)}, bf16[64,416]{1,0:T(8,128)(2,1)S(1)}, u32[]{:S(2)}, u32[]{:S(2)}) collective-permute-start(bf16[64,416]{1,0:T(8,128)(2,1)S(1)} %collective-permute-done.5.refs_3_), channel_id=1, source_target_pairs={{0,1},{1,0},{2,3},{3,2},{4,5},{5,4},{6,7},{7,6},{8,9},{9,8},{10,11... | collective-permute-start | bytes 159752 | tf_op jit(solution)/shard_map/ppermute | solution.py:334
  22.6 0.0 collective-permute-done.8.refs_4_
  22.6 0.0 collective-permute-done.9.refs_5_
  22.6 0.5 %sample.2.refs_2_ = f32[1,256]{1,0:T(1,128)S(1)} custom-call(bf16[256,512]{1,0:T(8,128)(2,1)S(1)} %get-tuple-element.10.re_ref, bf16[256,512]{1,0:T(8,128)(2,1)S(1)} %get-tuple-element.11.im_ref, f32[256,416]{1,0:T(8,128)S(1)} %get-tuple-element.12.tail_re_ref, f32[256,416]{1,0:T(8,128)S(1)} %get-tuple-element.13.tail_im_ref, ...), custom_call_target="tpu_custom_call" | custom-call | flops 163577856 | bytes 1048576 | tf_op jit(solution)/shard_map/sample/pallas_call | solution.py:310
  23.2 0.2 collective-permute-done.4.refs_0_
  23.4 0.2 collective-permute-done.6.refs_1_
  23.5 0.9 %sample.3 = f32[1,256]{1,0:T(1,128)} custom-call(bf16[256,512]{1,0:T(8,128)(2,1)S(1)} %get-tuple-element.10.re_ref, bf16[256,512]{1,0:T(8,128)(2,1)S(1)} %get-tuple-element.11.im_ref, f32[256,416]{1,0:T(8,128)S(1)} %get-tuple-element.12.tail_re_ref, f32[256,416]{1,0:T(8,128)S(1)} %get-tuple-element.13.tail_im_ref, ...), custom_call_target="tpu_custom_call" | custom-call | flops 54525952 | bytes 1048576 | tf_op jit(solution)/shard_map/sample/pallas_call | solution.py:310
  (5 shorter events, 0.0 us)
Async XLA Ops:
  6.8 4.2 %collective-permute-start.1 = (bf16[16,416]{1,0:T(8,128)(2,1)S(1)}, bf16[16,416]{1,0:T(8,128)(2,1)S(1)}, u32[]{:S(2)}, u32[]{:S(2)}) collective-permute-start(bf16[16,416]{1,0:T(8,128)(2,1)S(1)} %get-tuple-element.14), channel_id=1, source_target_pairs={{0,1},{1,0},{2,3},{3,2},{4,5},{5,4},{6,7},{7,6},{8,9},{9,8},{10,11... | collective-permute-start | bytes 39944 | tf_op jit(solution)/shard_map/ppermute | solution.py:334
  7.3 5.4 %collective-permute-start = (bf16[16,416]{1,0:T(8,128)(2,1)S(1)}, bf16[16,416]{1,0:T(8,128)(2,1)S(1)}, u32[]{:S(2)}, u32[]{:S(2)}) collective-permute-start(bf16[16,416]{1,0:T(8,128)(2,1)S(1)} %get-tuple-element.14), channel_id=1, source_target_pairs={{0,16},{1,17},{2,18},{3,19},{4,20},{5,21},{6,22},{7,23},{8,24},{9,... | collective-permute-start | bytes 39944 | tf_op jit(solution)/shard_map/ppermute | solution.py:334
  11.0 4.0 %collective-permute-start.2 = (bf16[32,416]{1,0:T(8,128)(2,1)S(1)}, bf16[32,416]{1,0:T(8,128)(2,1)S(1)}, u32[]{:S(2)}, u32[]{:S(2)}) collective-permute-start(bf16[32,416]{1,0:T(8,128)(2,1)S(1)} %pad_maximum_fusion), channel_id=1, source_target_pairs={{0,8},{1,25},{2,10},{3,27},{4,12},{5,29},{6,14},{7,31},{8,0},{9,17... | collective-permute-start | bytes 79880 | tf_op jit(solution)/shard_map/ppermute | solution.py:334
  15.0 5.3 %collective-permute-start.7 = (bf16[64,416]{1,0:T(8,128)(2,1)S(1)}, bf16[64,416]{1,0:T(8,128)(2,1)S(1)}, u32[]{:S(2)}, u32[]{:S(2)}) collective-permute-start(bf16[64,416]{1,0:T(8,128)(2,1)S(1)} %constant_dynamic-update-slice_fusion.refs_0_), channel_id=1, source_target_pairs={{0,7},{1,6},{2,5},{3,4},{4,3},{5,2},{6,1},{7,0},{8,15},{9,14},{10,... | collective-permute-start | bytes 159752 | tf_op jit(solution)/shard_map/ppermute | solution.py:334
  17.8 4.3 %collective-permute-start.3 = (bf16[64,416]{1,0:T(8,128)(2,1)S(1)}, bf16[64,416]{1,0:T(8,128)(2,1)S(1)}, u32[]{:S(2)}, u32[]{:S(2)}) collective-permute-start(bf16[64,416]{1,0:T(8,128)(2,1)S(1)} %constant_dynamic-update-slice_fusion.refs_0_), channel_id=1, source_target_pairs={{0,5},{1,4},{2,7},{3,6},{4,1},{5,0},{6,3},{7,2},{8,13},{9,12},{10,... | collective-permute-start | bytes 159752 | tf_op jit(solution)/shard_map/ppermute | solution.py:334
  17.8 4.3 %collective-permute-start.5 = (bf16[64,416]{1,0:T(8,128)(2,1)S(1)}, bf16[64,416]{1,0:T(8,128)(2,1)S(1)}, u32[]{:S(2)}, u32[]{:S(2)}) collective-permute-start(bf16[64,416]{1,0:T(8,128)(2,1)S(1)} %constant_dynamic-update-slice_fusion.refs_0_), channel_id=1, source_target_pairs={{0,3},{1,2},{2,1},{3,0},{4,7},{5,6},{6,5},{7,4},{8,11},{9,10},{10,... | collective-permute-start | bytes 159752 | tf_op jit(solution)/shard_map/ppermute | solution.py:334
  18.6 4.0 %collective-permute-start.8 = (bf16[64,416]{1,0:T(8,128)(2,1)S(1)}, bf16[64,416]{1,0:T(8,128)(2,1)S(1)}, u32[]{:S(2)}, u32[]{:S(2)}) collective-permute-start(bf16[64,416]{1,0:T(8,128)(2,1)S(1)} %constant_dynamic-update-slice_fusion.refs_0_), channel_id=1, source_target_pairs={{0,1},{1,0},{2,3},{3,2},{4,5},{5,4},{6,7},{7,6},{8,9},{9,8},{10,11... | collective-permute-start | bytes 159752 | tf_op jit(solution)/shard_map/ppermute | solution.py:334
  20.3 2.3 %collective-permute-start.9 = (bf16[64,416]{1,0:T(8,128)(2,1)S(1)}, bf16[64,416]{1,0:T(8,128)(2,1)S(1)}, u32[]{:S(2)}, u32[]{:S(2)}) collective-permute-start(bf16[64,416]{1,0:T(8,128)(2,1)S(1)} %collective-permute-done.7.refs_1_), channel_id=1, source_target_pairs={{0,1},{1,0},{2,3},{3,2},{4,5},{5,4},{6,7},{7,6},{8,9},{9,8},{10,11... | collective-permute-start | bytes 159752 | tf_op jit(solution)/shard_map/ppermute | solution.py:334
  22.1 1.3 %collective-permute-start.4 = (bf16[64,416]{1,0:T(8,128)(2,1)S(1)}, bf16[64,416]{1,0:T(8,128)(2,1)S(1)}, u32[]{:S(2)}, u32[]{:S(2)}) collective-permute-start(bf16[64,416]{1,0:T(8,128)(2,1)S(1)} %collective-permute-done.3.refs_2_), channel_id=1, source_target_pairs={{0,1},{1,0},{2,3},{3,2},{4,5},{5,4},{6,7},{7,6},{8,9},{9,8},{10,11... | collective-permute-start | bytes 159752 | tf_op jit(solution)/shard_map/ppermute | solution.py:334
  22.1 1.4 %collective-permute-start.6 = (bf16[64,416]{1,0:T(8,128)(2,1)S(1)}, bf16[64,416]{1,0:T(8,128)(2,1)S(1)}, u32[]{:S(2)}, u32[]{:S(2)}) collective-permute-start(bf16[64,416]{1,0:T(8,128)(2,1)S(1)} %collective-permute-done.5.refs_3_), channel_id=1, source_target_pairs={{0,1},{1,0},{2,3},{3,2},{4,5},{5,4},{6,7},{7,6},{8,9},{9,8},{10,11... | collective-permute-start | bytes 159752 | tf_op jit(solution)/shard_map/ppermute | solution.py:334

commit v10 on v9

--- a/solution.py
+++ b/solution.py
@@ -183,9 +183,14 @@
         for i, (source, target) in enumerate(pairs)
     ]
     small, slot, big = copies[:2], copies[2:5], copies[5:]
-    for copy in copies:
+    for copy in big[:1] + small + slot + big[1:]:
         copy.start()
-    mixed[...] = jnp.zeros_like(mixed)
+    whole = k_count // 8 * 8
+    if whole < k_pad:
+        for m in range(orders):
+            for c in range(2):
+                padded = slice(c * k_pad + whole, (c + 1) * k_pad)
+                mixed[m, padded, :] = jnp.zeros((k_pad - whole, ells), jnp.bfloat16)
 
     fixed = fixed_rows(sizes, n_strip, n_mr, orders, re_ref.shape[1])
     for copy in slot:

time: 24.6 us -> 24.5 us (level)
  no operation moved by 1% of the time
where the time goes in v10:
time: 24.5 us; the launch traced here: 24.4 us
  starting transfers between devices  10 us (41%)
  Pallas kernels  8.2 us (33%)
  waiting for transfers between devices  6.15 us (25%)
    ppermute x10, starting transfers between devices, swap(): return lax.ppermute(x, ('strip', 'mr'), pairs)  10 us
    pallas_call x1, Pallas kernels, local_part(): pl.pallas_call(functools.partial(coef_kernel, sizes), out_shape=(jax.Shap...  6.72 us
    ppermute x10, waiting for transfers between devices, swap(): return lax.ppermute(x, ('strip', 'mr'), pairs)  6.15 us
    pallas_call x2, Pallas kernels, sample(): pl.pallas_call(functools.partial(sample_kernel, first), out_shape=jax.Sha...  1.48 us
  transfers between devices with their start and end apart: 10, of which 6 were waited for; matrix products, arithmetic and copies ran while one was open for 0% of the time, Pallas kernels for 2%

profile of v10, /device:TPU:0, one launch (start us, length us, event | category | flops | bytes accessed | tf_op | source)
XLA Modules:
  0.0 24.4 jit_solution(11698070166175211831)
XLA Ops:
  0.0 6.7 %coef.1 = (bf16[16,416]{1,0:T(8,128)(2,1)S(1)}, bf16[256,512]{1,0:T(8,128)(2,1)S(1)}, bf16[256,512]{1,0:T(8,128)(2,1)S(1)}, f32[256,416]{1,0:T(8,128)S(1)}, f32[256,416]{1,0:T(8,128)S(1)}) custom-call(bf16[2,8,2048]{2,1,0:T(8,128)(2,1)} %alm_hbm.1, f32[13,2048]{1,0:T(8,128)} %beam_hbm.1, bf16[8,416,2048]{2,1,0:T(8,128)(2,1)} %bitcast.3, ...), custom_call_target="tpu_custom_call" | custom-call | flops 27262976 | bytes 13631488 | tf_op jit(solution)/shard_map/coef/pallas_call | solution.py:245
  6.7 0.5 %collective-permute-start.1 = (bf16[16,416]{1,0:T(8,128)(2,1)S(1)}, bf16[16,416]{1,0:T(8,128)(2,1)S(1)}, u32[]{:S(2)}, u32[]{:S(2)}) collective-permute-start(bf16[16,416]{1,0:T(8,128)(2,1)S(1)} %get-tuple-element.14), channel_id=1, source_target_pairs={{0,1},{1,0},{2,3},{3,2},{4,5},{5,4},{6,7},{7,6},{8,9},{9,8},{10,11... | collective-permute-start | bytes 39944 | tf_op jit(solution)/shard_map/ppermute | solution.py:339
  7.2 3.7 %collective-permute-start = (bf16[16,416]{1,0:T(8,128)(2,1)S(1)}, bf16[16,416]{1,0:T(8,128)(2,1)S(1)}, u32[]{:S(2)}, u32[]{:S(2)}) collective-permute-start(bf16[16,416]{1,0:T(8,128)(2,1)S(1)} %get-tuple-element.14), channel_id=1, source_target_pairs={{0,16},{1,17},{2,18},{3,19},{4,20},{5,21},{6,22},{7,23},{8,24},{9,... | collective-permute-start | bytes 39944 | tf_op jit(solution)/shard_map/ppermute | solution.py:339
  10.9 0.0 collective-permute-done.1
  10.9 1.6 %collective-permute-start.2 = (bf16[32,416]{1,0:T(8,128)(2,1)S(1)}, bf16[32,416]{1,0:T(8,128)(2,1)S(1)}, u32[]{:S(2)}, u32[]{:S(2)}) collective-permute-start(bf16[32,416]{1,0:T(8,128)(2,1)S(1)} %pad_maximum_fusion), channel_id=1, source_target_pairs={{0,8},{1,25},{2,10},{3,27},{4,12},{5,29},{6,14},{7,31},{8,0},{9,17... | collective-permute-start | bytes 79880 | tf_op jit(solution)/shard_map/ppermute | solution.py:339
  12.6 0.1 collective-permute-done
  12.6 2.3 %collective-permute-done.2 = bf16[32,416]{1,0:T(8,128)(2,1)S(1)} collective-permute-done((bf16[32,416]{1,0:T(8,128)(2,1)S(1)}, bf16[32,416]{1,0:T(8,128)(2,1)S(1)}, u32[]{:S(2)}, u32[]{:S(2)}) %collective-permute-start.2) | collective-permute-done | bytes 26656 | tf_op jit(solution)/shard_map/ppermute | solution.py:339
  14.9 2.9 %collective-permute-start.7 = (bf16[64,416]{1,0:T(8,128)(2,1)S(1)}, bf16[64,416]{1,0:T(8,128)(2,1)S(1)}, u32[]{:S(2)}, u32[]{:S(2)}) collective-permute-start(bf16[64,416]{1,0:T(8,128)(2,1)S(1)} %constant_dynamic-update-slice_fusion.refs_0_), channel_id=1, source_target_pairs={{0,7},{1,6},{2,5},{3,4},{4,3},{5,2},{6,1},{7,0},{8,15},{9,14},{10,... | collective-permute-start | bytes 159752 | tf_op jit(solution)/shard_map/ppermute | solution.py:339
  17.8 0.0 collective-permute-start.3
  17.8 0.8 %collective-permute-start.5 = (bf16[64,416]{1,0:T(8,128)(2,1)S(1)}, bf16[64,416]{1,0:T(8,128)(2,1)S(1)}, u32[]{:S(2)}, u32[]{:S(2)}) collective-permute-start(bf16[64,416]{1,0:T(8,128)(2,1)S(1)} %constant_dynamic-update-slice_fusion.refs_0_), channel_id=1, source_target_pairs={{0,3},{1,2},{2,1},{3,0},{4,7},{5,6},{6,5},{7,4},{8,11},{9,10},{10,... | collective-permute-start | bytes 159752 | tf_op jit(solution)/shard_map/ppermute | solution.py:339
  18.5 0.0 collective-permute-start.8
  18.5 1.7 %collective-permute-done.7.refs_1_ = bf16[64,416]{1,0:T(8,128)(2,1)S(1)} collective-permute-done((bf16[64,416]{1,0:T(8,128)(2,1)S(1)}, bf16[64,416]{1,0:T(8,128)(2,1)S(1)}, u32[]{:S(2)}, u32[]{:S(2)}) %collective-permute-start.7) | collective-permute-done | bytes 53280 | tf_op jit(solution)/shard_map/ppermute | solution.py:339
  20.3 0.1 collective-permute-start.9
  20.3 1.7 %collective-permute-done.3.refs_2_ = bf16[64,416]{1,0:T(8,128)(2,1)S(1)} collective-permute-done((bf16[64,416]{1,0:T(8,128)(2,1)S(1)}, bf16[64,416]{1,0:T(8,128)(2,1)S(1)}, u32[]{:S(2)}, u32[]{:S(2)}) %collective-permute-start.3) | collective-permute-done | bytes 53280 | tf_op jit(solution)/shard_map/ppermute | solution.py:339
  22.0 0.0 collective-permute-start.4
  22.0 0.0 collective-permute-done.5.refs_3_
  22.0 0.5 %collective-permute-start.6 = (bf16[64,416]{1,0:T(8,128)(2,1)S(1)}, bf16[64,416]{1,0:T(8,128)(2,1)S(1)}, u32[]{:S(2)}, u32[]{:S(2)}) collective-permute-start(bf16[64,416]{1,0:T(8,128)(2,1)S(1)} %collective-permute-done.5.refs_3_), channel_id=1, source_target_pairs={{0,1},{1,0},{2,3},{3,2},{4,5},{5,4},{6,7},{7,6},{8,9},{9,8},{10,11... | collective-permute-start | bytes 159752 | tf_op jit(solution)/shard_map/ppermute | solution.py:339
  22.6 0.0 collective-permute-done.8.refs_4_
  22.6 0.0 collective-permute-done.9.refs_5_
  22.6 0.5 %sample.2.refs_2_ = f32[1,256]{1,0:T(1,128)S(1)} custom-call(bf16[256,512]{1,0:T(8,128)(2,1)S(1)} %get-tuple-element.10.re_ref, bf16[256,512]{1,0:T(8,128)(2,1)S(1)} %get-tuple-element.11.im_ref, f32[256,416]{1,0:T(8,128)S(1)} %get-tuple-element.12.tail_re_ref, f32[256,416]{1,0:T(8,128)S(1)} %get-tuple-element.13.tail_im_ref, ...), custom_call_target="tpu_custom_call" | custom-call | flops 163577856 | bytes 1048576 | tf_op jit(solution)/shard_map/sample/pallas_call | solution.py:315
  23.1 0.2 collective-permute-done.4.refs_0_
  23.3 0.2 collective-permute-done.6.refs_1_
  23.5 0.9 %sample.3 = f32[1,256]{1,0:T(1,128)} custom-call(bf16[256,512]{1,0:T(8,128)(2,1)S(1)} %get-tuple-element.10.re_ref, bf16[256,512]{1,0:T(8,128)(2,1)S(1)} %get-tuple-element.11.im_ref, f32[256,416]{1,0:T(8,128)S(1)} %get-tuple-element.12.tail_re_ref, f32[256,416]{1,0:T(8,128)S(1)} %get-tuple-element.13.tail_im_ref, ...), custom_call_target="tpu_custom_call" | custom-call | flops 54525952 | bytes 1048576 | tf_op jit(solution)/shard_map/sample/pallas_call | solution.py:315
  (5 shorter events, 0.0 us)
Async XLA Ops:
  6.7 4.2 %collective-permute-start.1 = (bf16[16,416]{1,0:T(8,128)(2,1)S(1)}, bf16[16,416]{1,0:T(8,128)(2,1)S(1)}, u32[]{:S(2)}, u32[]{:S(2)}) collective-permute-start(bf16[16,416]{1,0:T(8,128)(2,1)S(1)} %get-tuple-element.14), channel_id=1, source_target_pairs={{0,1},{1,0},{2,3},{3,2},{4,5},{5,4},{6,7},{7,6},{8,9},{9,8},{10,11... | collective-permute-start | bytes 39944 | tf_op jit(solution)/shard_map/ppermute | solution.py:339
  7.2 5.4 %collective-permute-start = (bf16[16,416]{1,0:T(8,128)(2,1)S(1)}, bf16[16,416]{1,0:T(8,128)(2,1)S(1)}, u32[]{:S(2)}, u32[]{:S(2)}) collective-permute-start(bf16[16,416]{1,0:T(8,128)(2,1)S(1)} %get-tuple-element.14), channel_id=1, source_target_pairs={{0,16},{1,17},{2,18},{3,19},{4,20},{5,21},{6,22},{7,23},{8,24},{9,... | collective-permute-start | bytes 39944 | tf_op jit(solution)/shard_map/ppermute | solution.py:339
  10.9 4.0 %collective-permute-start.2 = (bf16[32,416]{1,0:T(8,128)(2,1)S(1)}, bf16[32,416]{1,0:T(8,128)(2,1)S(1)}, u32[]{:S(2)}, u32[]{:S(2)}) collective-permute-start(bf16[32,416]{1,0:T(8,128)(2,1)S(1)} %pad_maximum_fusion), channel_id=1, source_target_pairs={{0,8},{1,25},{2,10},{3,27},{4,12},{5,29},{6,14},{7,31},{8,0},{9,17... | collective-permute-start | bytes 79880 | tf_op jit(solution)/shard_map/ppermute | solution.py:339
  14.9 5.4 %collective-permute-start.7 = (bf16[64,416]{1,0:T(8,128)(2,1)S(1)}, bf16[64,416]{1,0:T(8,128)(2,1)S(1)}, u32[]{:S(2)}, u32[]{:S(2)}) collective-permute-start(bf16[64,416]{1,0:T(8,128)(2,1)S(1)} %constant_dynamic-update-slice_fusion.refs_0_), channel_id=1, source_target_pairs={{0,7},{1,6},{2,5},{3,4},{4,3},{5,2},{6,1},{7,0},{8,15},{9,14},{10,... | collective-permute-start | bytes 159752 | tf_op jit(solution)/shard_map/ppermute | solution.py:339
  17.8 4.3 %collective-permute-start.3 = (bf16[64,416]{1,0:T(8,128)(2,1)S(1)}, bf16[64,416]{1,0:T(8,128)(2,1)S(1)}, u32[]{:S(2)}, u32[]{:S(2)}) collective-permute-start(bf16[64,416]{1,0:T(8,128)(2,1)S(1)} %constant_dynamic-update-slice_fusion.refs_0_), channel_id=1, source_target_pairs={{0,5},{1,4},{2,7},{3,6},{4,1},{5,0},{6,3},{7,2},{8,13},{9,12},{10,... | collective-permute-start | bytes 159752 | tf_op jit(solution)/shard_map/ppermute | solution.py:339
  17.8 4.3 %collective-permute-start.5 = (bf16[64,416]{1,0:T(8,128)(2,1)S(1)}, bf16[64,416]{1,0:T(8,128)(2,1)S(1)}, u32[]{:S(2)}, u32[]{:S(2)}) collective-permute-start(bf16[64,416]{1,0:T(8,128)(2,1)S(1)} %constant_dynamic-update-slice_fusion.refs_0_), channel_id=1, source_target_pairs={{0,3},{1,2},{2,1},{3,0},{4,7},{5,6},{6,5},{7,4},{8,11},{9,10},{10,... | collective-permute-start | bytes 159752 | tf_op jit(solution)/shard_map/ppermute | solution.py:339
  18.5 4.0 %collective-permute-start.8 = (bf16[64,416]{1,0:T(8,128)(2,1)S(1)}, bf16[64,416]{1,0:T(8,128)(2,1)S(1)}, u32[]{:S(2)}, u32[]{:S(2)}) collective-permute-start(bf16[64,416]{1,0:T(8,128)(2,1)S(1)} %constant_dynamic-update-slice_fusion.refs_0_), channel_id=1, source_target_pairs={{0,1},{1,0},{2,3},{3,2},{4,5},{5,4},{6,7},{7,6},{8,9},{9,8},{10,11... | collective-permute-start | bytes 159752 | tf_op jit(solution)/shard_map/ppermute | solution.py:339
  20.3 2.3 %collective-permute-start.9 = (bf16[64,416]{1,0:T(8,128)(2,1)S(1)}, bf16[64,416]{1,0:T(8,128)(2,1)S(1)}, u32[]{:S(2)}, u32[]{:S(2)}) collective-permute-start(bf16[64,416]{1,0:T(8,128)(2,1)S(1)} %collective-permute-done.7.refs_1_), channel_id=1, source_target_pairs={{0,1},{1,0},{2,3},{3,2},{4,5},{5,4},{6,7},{7,6},{8,9},{9,8},{10,11... | collective-permute-start | bytes 159752 | tf_op jit(solution)/shard_map/ppermute | solution.py:339
  22.0 1.3 %collective-permute-start.4 = (bf16[64,416]{1,0:T(8,128)(2,1)S(1)}, bf16[64,416]{1,0:T(8,128)(2,1)S(1)}, u32[]{:S(2)}, u32[]{:S(2)}) collective-permute-start(bf16[64,416]{1,0:T(8,128)(2,1)S(1)} %collective-permute-done.3.refs_2_), channel_id=1, source_target_pairs={{0,1},{1,0},{2,3},{3,2},{4,5},{5,4},{6,7},{7,6},{8,9},{9,8},{10,11... | collective-permute-start | bytes 159752 | tf_op jit(solution)/shard_map/ppermute | solution.py:339
  22.0 1.4 %collective-permute-start.6 = (bf16[64,416]{1,0:T(8,128)(2,1)S(1)}, bf16[64,416]{1,0:T(8,128)(2,1)S(1)}, u32[]{:S(2)}, u32[]{:S(2)}) collective-permute-start(bf16[64,416]{1,0:T(8,128)(2,1)S(1)} %collective-permute-done.5.refs_3_), channel_id=1, source_target_pairs={{0,1},{1,0},{2,3},{3,2},{4,5},{5,4},{6,7},{7,6},{8,9},{9,8},{10,11... | collective-permute-start | bytes 159752 | tf_op jit(solution)/shard_map/ppermute | solution.py:339

commit v11 on v9

--- a/solution.py
+++ b/solution.py
@@ -20,7 +20,8 @@
     sin = jnp.zeros_like(x)
     for n in range(9, -1, -1):
         cos = cos * u + (-1) ** n * (2 * math.pi) ** (2 * n) / math.factorial(2 * n)
-        sin = sin * u + (-1) ** n * (2 * math.pi) ** (2 * n + 1) / math.factorial(2 * n + 1)
+        if n < 9:
+            sin = sin * u + (-1) ** n * (2 * math.pi) ** (2 * n + 1) / math.factorial(2 * n + 1)
     return cos, sin * x
 
 
@@ -183,7 +184,7 @@
         for i, (source, target) in enumerate(pairs)
     ]
     small, slot, big = copies[:2], copies[2:5], copies[5:]
-    for copy in copies:
+    for copy in big[:1] + small + slot + big[1:]:
         copy.start()
     mixed[...] = jnp.zeros_like(mixed)
 

time: 24.6 us -> 24.5 us (level)
  no operation moved by 1% of the time
where the time goes in v11:
time: 24.5 us; the launch traced here: 24.4 us
  starting transfers between devices  10 us (41%)
  Pallas kernels  8.2 us (33%)
  waiting for transfers between devices  6.14 us (25%)
    ppermute x10, starting transfers between devices, swap(): return lax.ppermute(x, ('strip', 'mr'), pairs)  10 us
    pallas_call x1, Pallas kernels, local_part(): pl.pallas_call(functools.partial(coef_kernel, sizes), out_shape=(jax.Shap...  6.72 us
    ppermute x10, waiting for transfers between devices, swap(): return lax.ppermute(x, ('strip', 'mr'), pairs)  6.14 us
    pallas_call x2, Pallas kernels, sample(): pl.pallas_call(functools.partial(sample_kernel, first), out_shape=jax.Sha...  1.48 us
  transfers between devices with their start and end apart: 10, of which 6 were waited for; matrix products, arithmetic and copies ran while one was open for 0% of the time, Pallas kernels for 2%

profile of v11, /device:TPU:0, one launch (start us, length us, event | category | flops | bytes accessed | tf_op | source)
XLA Modules:
  0.0 24.4 jit_solution(14225080505876903209)
XLA Ops:
  0.0 6.7 %coef.1 = (bf16[16,416]{1,0:T(8,128)(2,1)S(1)}, bf16[256,512]{1,0:T(8,128)(2,1)S(1)}, bf16[256,512]{1,0:T(8,128)(2,1)S(1)}, f32[256,416]{1,0:T(8,128)S(1)}, f32[256,416]{1,0:T(8,128)S(1)}) custom-call(bf16[2,8,2048]{2,1,0:T(8,128)(2,1)} %alm_hbm.1, f32[13,2048]{1,0:T(8,128)} %beam_hbm.1, bf16[8,416,2048]{2,1,0:T(8,128)(2,1)} %bitcast.3, ...), custom_call_target="tpu_custom_call" | custom-call | flops 27262976 | bytes 13631488 | tf_op jit(solution)/shard_map/coef/pallas_call | solution.py:241
  6.7 0.5 %collective-permute-start.1 = (bf16[16,416]{1,0:T(8,128)(2,1)S(1)}, bf16[16,416]{1,0:T(8,128)(2,1)S(1)}, u32[]{:S(2)}, u32[]{:S(2)}) collective-permute-start(bf16[16,416]{1,0:T(8,128)(2,1)S(1)} %get-tuple-element.14), channel_id=1, source_target_pairs={{0,1},{1,0},{2,3},{3,2},{4,5},{5,4},{6,7},{7,6},{8,9},{9,8},{10,11... | collective-permute-start | bytes 39944 | tf_op jit(solution)/shard_map/ppermute | solution.py:335
  7.3 3.7 %collective-permute-start = (bf16[16,416]{1,0:T(8,128)(2,1)S(1)}, bf16[16,416]{1,0:T(8,128)(2,1)S(1)}, u32[]{:S(2)}, u32[]{:S(2)}) collective-permute-start(bf16[16,416]{1,0:T(8,128)(2,1)S(1)} %get-tuple-element.14), channel_id=1, source_target_pairs={{0,16},{1,17},{2,18},{3,19},{4,20},{5,21},{6,22},{7,23},{8,24},{9,... | collective-permute-start | bytes 39944 | tf_op jit(solution)/shard_map/ppermute | solution.py:335
  10.9 0.0 collective-permute-done.1
  10.9 1.6 %collective-permute-start.2 = (bf16[32,416]{1,0:T(8,128)(2,1)S(1)}, bf16[32,416]{1,0:T(8,128)(2,1)S(1)}, u32[]{:S(2)}, u32[]{:S(2)}) collective-permute-start(bf16[32,416]{1,0:T(8,128)(2,1)S(1)} %pad_maximum_fusion), channel_id=1, source_target_pairs={{0,8},{1,25},{2,10},{3,27},{4,12},{5,29},{6,14},{7,31},{8,0},{9,17... | collective-permute-start | bytes 79880 | tf_op jit(solution)/shard_map/ppermute | solution.py:335
  12.6 0.1 collective-permute-done
  12.6 2.3 %collective-permute-done.2 = bf16[32,416]{1,0:T(8,128)(2,1)S(1)} collective-permute-done((bf16[32,416]{1,0:T(8,128)(2,1)S(1)}, bf16[32,416]{1,0:T(8,128)(2,1)S(1)}, u32[]{:S(2)}, u32[]{:S(2)}) %collective-permute-start.2) | collective-permute-done | bytes 26656 | tf_op jit(solution)/shard_map/ppermute | solution.py:335
  14.9 2.9 %collective-permute-start.7 = (bf16[64,416]{1,0:T(8,128)(2,1)S(1)}, bf16[64,416]{1,0:T(8,128)(2,1)S(1)}, u32[]{:S(2)}, u32[]{:S(2)}) collective-permute-start(bf16[64,416]{1,0:T(8,128)(2,1)S(1)} %constant_dynamic-update-slice_fusion.refs_0_), channel_id=1, source_target_pairs={{0,7},{1,6},{2,5},{3,4},{4,3},{5,2},{6,1},{7,0},{8,15},{9,14},{10,... | collective-permute-start | bytes 159752 | tf_op jit(solution)/shard_map/ppermute | solution.py:335
  17.8 0.0 collective-permute-start.3
  17.8 0.8 %collective-permute-start.5 = (bf16[64,416]{1,0:T(8,128)(2,1)S(1)}, bf16[64,416]{1,0:T(8,128)(2,1)S(1)}, u32[]{:S(2)}, u32[]{:S(2)}) collective-permute-start(bf16[64,416]{1,0:T(8,128)(2,1)S(1)} %constant_dynamic-update-slice_fusion.refs_0_), channel_id=1, source_target_pairs={{0,3},{1,2},{2,1},{3,0},{4,7},{5,6},{6,5},{7,4},{8,11},{9,10},{10,... | collective-permute-start | bytes 159752 | tf_op jit(solution)/shard_map/ppermute | solution.py:335
  18.5 0.0 collective-permute-start.8
  18.5 1.7 %collective-permute-done.7.refs_1_ = bf16[64,416]{1,0:T(8,128)(2,1)S(1)} collective-permute-done((bf16[64,416]{1,0:T(8,128)(2,1)S(1)}, bf16[64,416]{1,0:T(8,128)(2,1)S(1)}, u32[]{:S(2)}, u32[]{:S(2)}) %collective-permute-start.7) | collective-permute-done | bytes 53280 | tf_op jit(solution)/shard_map/ppermute | solution.py:335
  20.3 0.1 collective-permute-start.9
  20.3 1.7 %collective-permute-done.3.refs_2_ = bf16[64,416]{1,0:T(8,128)(2,1)S(1)} collective-permute-done((bf16[64,416]{1,0:T(8,128)(2,1)S(1)}, bf16[64,416]{1,0:T(8,128)(2,1)S(1)}, u32[]{:S(2)}, u32[]{:S(2)}) %collective-permute-start.3) | collective-permute-done | bytes 53280 | tf_op jit(solution)/shard_map/ppermute | solution.py:335
  22.0 0.0 collective-permute-start.4
  22.0 0.0 collective-permute-done.5.refs_3_
  22.1 0.5 %collective-permute-start.6 = (bf16[64,416]{1,0:T(8,128)(2,1)S(1)}, bf16[64,416]{1,0:T(8,128)(2,1)S(1)}, u32[]{:S(2)}, u32[]{:S(2)}) collective-permute-start(bf16[64,416]{1,0:T(8,128)(2,1)S(1)} %collective-permute-done.5.refs_3_), channel_id=1, source_target_pairs={{0,1},{1,0},{2,3},{3,2},{4,5},{5,4},{6,7},{7,6},{8,9},{9,8},{10,11... | collective-permute-start | bytes 159752 | tf_op jit(solution)/shard_map/ppermute | solution.py:335
  22.6 0.0 collective-permute-done.8.refs_4_
  22.6 0.0 collective-permute-done.9.refs_5_
  22.6 0.5 %sample.2.refs_2_ = f32[1,256]{1,0:T(1,128)S(1)} custom-call(bf16[256,512]{1,0:T(8,128)(2,1)S(1)} %get-tuple-element.10.re_ref, bf16[256,512]{1,0:T(8,128)(2,1)S(1)} %get-tuple-element.11.im_ref, f32[256,416]{1,0:T(8,128)S(1)} %get-tuple-element.12.tail_re_ref, f32[256,416]{1,0:T(8,128)S(1)} %get-tuple-element.13.tail_im_ref, ...), custom_call_target="tpu_custom_call" | custom-call | flops 163577856 | bytes 1048576 | tf_op jit(solution)/shard_map/sample/pallas_call | solution.py:311
  23.1 0.2 collective-permute-done.4.refs_0_
  23.3 0.2 collective-permute-done.6.refs_1_
  23.5 0.9 %sample.3 = f32[1,256]{1,0:T(1,128)} custom-call(bf16[256,512]{1,0:T(8,128)(2,1)S(1)} %get-tuple-element.10.re_ref, bf16[256,512]{1,0:T(8,128)(2,1)S(1)} %get-tuple-element.11.im_ref, f32[256,416]{1,0:T(8,128)S(1)} %get-tuple-element.12.tail_re_ref, f32[256,416]{1,0:T(8,128)S(1)} %get-tuple-element.13.tail_im_ref, ...), custom_call_target="tpu_custom_call" | custom-call | flops 54525952 | bytes 1048576 | tf_op jit(solution)/shard_map/sample/pallas_call | solution.py:311
  (5 shorter events, 0.0 us)
Async XLA Ops:
  6.7 4.2 %collective-permute-start.1 = (bf16[16,416]{1,0:T(8,128)(2,1)S(1)}, bf16[16,416]{1,0:T(8,128)(2,1)S(1)}, u32[]{:S(2)}, u32[]{:S(2)}) collective-permute-start(bf16[16,416]{1,0:T(8,128)(2,1)S(1)} %get-tuple-element.14), channel_id=1, source_target_pairs={{0,1},{1,0},{2,3},{3,2},{4,5},{5,4},{6,7},{7,6},{8,9},{9,8},{10,11... | collective-permute-start | bytes 39944 | tf_op jit(solution)/shard_map/ppermute | solution.py:335
  7.3 5.4 %collective-permute-start = (bf16[16,416]{1,0:T(8,128)(2,1)S(1)}, bf16[16,416]{1,0:T(8,128)(2,1)S(1)}, u32[]{:S(2)}, u32[]{:S(2)}) collective-permute-start(bf16[16,416]{1,0:T(8,128)(2,1)S(1)} %get-tuple-element.14), channel_id=1, source_target_pairs={{0,16},{1,17},{2,18},{3,19},{4,20},{5,21},{6,22},{7,23},{8,24},{9,... | collective-permute-start | bytes 39944 | tf_op jit(solution)/shard_map/ppermute | solution.py:335
  10.9 4.0 %collective-permute-start.2 = (bf16[32,416]{1,0:T(8,128)(2,1)S(1)}, bf16[32,416]{1,0:T(8,128)(2,1)S(1)}, u32[]{:S(2)}, u32[]{:S(2)}) collective-permute-start(bf16[32,416]{1,0:T(8,128)(2,1)S(1)} %pad_maximum_fusion), channel_id=1, source_target_pairs={{0,8},{1,25},{2,10},{3,27},{4,12},{5,29},{6,14},{7,31},{8,0},{9,17... | collective-permute-start | bytes 79880 | tf_op jit(solution)/shard_map/ppermute | solution.py:335
  14.9 5.3 %collective-permute-start.7 = (bf16[64,416]{1,0:T(8,128)(2,1)S(1)}, bf16[64,416]{1,0:T(8,128)(2,1)S(1)}, u32[]{:S(2)}, u32[]{:S(2)}) collective-permute-start(bf16[64,416]{1,0:T(8,128)(2,1)S(1)} %constant_dynamic-update-slice_fusion.refs_0_), channel_id=1, source_target_pairs={{0,7},{1,6},{2,5},{3,4},{4,3},{5,2},{6,1},{7,0},{8,15},{9,14},{10,... | collective-permute-start | bytes 159752 | tf_op jit(solution)/shard_map/ppermute | solution.py:335
  17.8 4.3 %collective-permute-start.3 = (bf16[64,416]{1,0:T(8,128)(2,1)S(1)}, bf16[64,416]{1,0:T(8,128)(2,1)S(1)}, u32[]{:S(2)}, u32[]{:S(2)}) collective-permute-start(bf16[64,416]{1,0:T(8,128)(2,1)S(1)} %constant_dynamic-update-slice_fusion.refs_0_), channel_id=1, source_target_pairs={{0,5},{1,4},{2,7},{3,6},{4,1},{5,0},{6,3},{7,2},{8,13},{9,12},{10,... | collective-permute-start | bytes 159752 | tf_op jit(solution)/shard_map/ppermute | solution.py:335
  17.8 4.3 %collective-permute-start.5 = (bf16[64,416]{1,0:T(8,128)(2,1)S(1)}, bf16[64,416]{1,0:T(8,128)(2,1)S(1)}, u32[]{:S(2)}, u32[]{:S(2)}) collective-permute-start(bf16[64,416]{1,0:T(8,128)(2,1)S(1)} %constant_dynamic-update-slice_fusion.refs_0_), channel_id=1, source_target_pairs={{0,3},{1,2},{2,1},{3,0},{4,7},{5,6},{6,5},{7,4},{8,11},{9,10},{10,... | collective-permute-start | bytes 159752 | tf_op jit(solution)/shard_map/ppermute | solution.py:335
  18.5 4.0 %collective-permute-start.8 = (bf16[64,416]{1,0:T(8,128)(2,1)S(1)}, bf16[64,416]{1,0:T(8,128)(2,1)S(1)}, u32[]{:S(2)}, u32[]{:S(2)}) collective-permute-start(bf16[64,416]{1,0:T(8,128)(2,1)S(1)} %constant_dynamic-update-slice_fusion.refs_0_), channel_id=1, source_target_pairs={{0,1},{1,0},{2,3},{3,2},{4,5},{5,4},{6,7},{7,6},{8,9},{9,8},{10,11... | collective-permute-start | bytes 159752 | tf_op jit(solution)/shard_map/ppermute | solution.py:335
  20.3 2.3 %collective-permute-start.9 = (bf16[64,416]{1,0:T(8,128)(2,1)S(1)}, bf16[64,416]{1,0:T(8,128)(2,1)S(1)}, u32[]{:S(2)}, u32[]{:S(2)}) collective-permute-start(bf16[64,416]{1,0:T(8,128)(2,1)S(1)} %collective-permute-done.7.refs_1_), channel_id=1, source_target_pairs={{0,1},{1,0},{2,3},{3,2},{4,5},{5,4},{6,7},{7,6},{8,9},{9,8},{10,11... | collective-permute-start | bytes 159752 | tf_op jit(solution)/shard_map/ppermute | solution.py:335
  22.0 1.3 %collective-permute-start.4 = (bf16[64,416]{1,0:T(8,128)(2,1)S(1)}, bf16[64,416]{1,0:T(8,128)(2,1)S(1)}, u32[]{:S(2)}, u32[]{:S(2)}) collective-permute-start(bf16[64,416]{1,0:T(8,128)(2,1)S(1)} %collective-permute-done.3.refs_2_), channel_id=1, source_target_pairs={{0,1},{1,0},{2,3},{3,2},{4,5},{5,4},{6,7},{7,6},{8,9},{9,8},{10,11... | collective-permute-start | bytes 159752 | tf_op jit(solution)/shard_map/ppermute | solution.py:335
  22.1 1.4 %collective-permute-start.6 = (bf16[64,416]{1,0:T(8,128)(2,1)S(1)}, bf16[64,416]{1,0:T(8,128)(2,1)S(1)}, u32[]{:S(2)}, u32[]{:S(2)}) collective-permute-start(bf16[64,416]{1,0:T(8,128)(2,1)S(1)} %collective-permute-done.5.refs_3_), channel_id=1, source_target_pairs={{0,1},{1,0},{2,3},{3,2},{4,5},{5,4},{6,7},{7,6},{8,9},{9,8},{10,11... | collective-permute-start | bytes 159752 | tf_op jit(solution)/shard_map/ppermute | solution.py:335

commit v12 on v9

--- a/solution.py
+++ b/solution.py
@@ -132,9 +132,9 @@
         im_ref[here, there] = im.astype(jnp.bfloat16)
     _, r_lane = divide(lane_row(), lats)
     across = jnp.zeros_like(col[0])
+    _, tap = divide(r_lane - col[13], lats)
     for a in range(4):
-        _, row = divide(col[13] + a, lats)
-        across = across + jnp.where(row == r_lane, col[a], 0.0)
+        across = across + jnp.where(tap == a, col[a], 0.0)
     _, psi_turns = divide(col[14] * lane_row(), psi_count)
     turn = cos_sin_turns(psi_turns * (1.0 / psi_count))
     along_re, along_im = times(turn, tap_sum(col[8:12], psi_steps))

time: 24.6 us -> 24.6 us (level)
  no operation moved by 1% of the time
where the time goes in v12:
time: 24.6 us; the launch traced here: 24.5 us
  starting transfers between devices  10 us (41%)
  Pallas kernels  8.26 us (34%)
  waiting for transfers between devices  6.15 us (25%)
    ppermute x10, starting transfers between devices, swap(): return lax.ppermute(x, ('strip', 'mr'), pairs)  10 us
    pallas_call x1, Pallas kernels, local_part(): pl.pallas_call(functools.partial(coef_kernel, sizes), out_shape=(jax.Shap...  6.78 us
    ppermute x10, waiting for transfers between devices, swap(): return lax.ppermute(x, ('strip', 'mr'), pairs)  6.15 us
    pallas_call x2, Pallas kernels, sample(): pl.pallas_call(functools.partial(sample_kernel, first), out_shape=jax.Sha...  1.48 us
  transfers between devices with their start and end apart: 10, of which 6 were waited for; matrix products, arithmetic and copies ran while one was open for 0% of the time, Pallas kernels for 2%

profile of v12, /device:TPU:0, one launch (start us, length us, event | category | flops | bytes accessed | tf_op | source)
XLA Modules:
  0.0 24.5 jit_solution(12434989917627962306)
XLA Ops:
  0.0 6.8 %coef.1 = (bf16[16,416]{1,0:T(8,128)(2,1)S(1)}, bf16[256,512]{1,0:T(8,128)(2,1)S(1)}, bf16[256,512]{1,0:T(8,128)(2,1)S(1)}, f32[256,416]{1,0:T(8,128)S(1)}, f32[256,416]{1,0:T(8,128)S(1)}) custom-call(bf16[2,8,2048]{2,1,0:T(8,128)(2,1)} %alm_hbm.1, f32[13,2048]{1,0:T(8,128)} %beam_hbm.1, bf16[8,416,2048]{2,1,0:T(8,128)(2,1)} %bitcast.3, ...), custom_call_target="tpu_custom_call" | custom-call | flops 27262976 | bytes 13631488 | tf_op jit(solution)/shard_map/coef/pallas_call | solution.py:240
  6.8 0.5 %collective-permute-start.1 = (bf16[16,416]{1,0:T(8,128)(2,1)S(1)}, bf16[16,416]{1,0:T(8,128)(2,1)S(1)}, u32[]{:S(2)}, u32[]{:S(2)}) collective-permute-start(bf16[16,416]{1,0:T(8,128)(2,1)S(1)} %get-tuple-element.14), channel_id=1, source_target_pairs={{0,1},{1,0},{2,3},{3,2},{4,5},{5,4},{6,7},{7,6},{8,9},{9,8},{10,11... | collective-permute-start | bytes 39944 | tf_op jit(solution)/shard_map/ppermute | solution.py:334
  7.3 3.7 %collective-permute-start = (bf16[16,416]{1,0:T(8,128)(2,1)S(1)}, bf16[16,416]{1,0:T(8,128)(2,1)S(1)}, u32[]{:S(2)}, u32[]{:S(2)}) collective-permute-start(bf16[16,416]{1,0:T(8,128)(2,1)S(1)} %get-tuple-element.14), channel_id=1, source_target_pairs={{0,16},{1,17},{2,18},{3,19},{4,20},{5,21},{6,22},{7,23},{8,24},{9,... | collective-permute-start | bytes 39944 | tf_op jit(solution)/shard_map/ppermute | solution.py:334
  11.0 0.0 collective-permute-done.1
  11.0 1.6 %collective-permute-start.2 = (bf16[32,416]{1,0:T(8,128)(2,1)S(1)}, bf16[32,416]{1,0:T(8,128)(2,1)S(1)}, u32[]{:S(2)}, u32[]{:S(2)}) collective-permute-start(bf16[32,416]{1,0:T(8,128)(2,1)S(1)} %pad_maximum_fusion), channel_id=1, source_target_pairs={{0,8},{1,25},{2,10},{3,27},{4,12},{5,29},{6,14},{7,31},{8,0},{9,17... | collective-permute-start | bytes 79880 | tf_op jit(solution)/shard_map/ppermute | solution.py:334
  12.6 0.1 collective-permute-done
  12.7 2.3 %collective-permute-done.2 = bf16[32,416]{1,0:T(8,128)(2,1)S(1)} collective-permute-done((bf16[32,416]{1,0:T(8,128)(2,1)S(1)}, bf16[32,416]{1,0:T(8,128)(2,1)S(1)}, u32[]{:S(2)}, u32[]{:S(2)}) %collective-permute-start.2) | collective-permute-done | bytes 26656 | tf_op jit(solution)/shard_map/ppermute | solution.py:334
  15.0 2.9 %collective-permute-start.7 = (bf16[64,416]{1,0:T(8,128)(2,1)S(1)}, bf16[64,416]{1,0:T(8,128)(2,1)S(1)}, u32[]{:S(2)}, u32[]{:S(2)}) collective-permute-start(bf16[64,416]{1,0:T(8,128)(2,1)S(1)} %constant_dynamic-update-slice_fusion.refs_0_), channel_id=1, source_target_pairs={{0,7},{1,6},{2,5},{3,4},{4,3},{5,2},{6,1},{7,0},{8,15},{9,14},{10,... | collective-permute-start | bytes 159752 | tf_op jit(solution)/shard_map/ppermute | solution.py:334
  17.8 0.0 collective-permute-start.3
  17.8 0.8 %collective-permute-start.5 = (bf16[64,416]{1,0:T(8,128)(2,1)S(1)}, bf16[64,416]{1,0:T(8,128)(2,1)S(1)}, u32[]{:S(2)}, u32[]{:S(2)}) collective-permute-start(bf16[64,416]{1,0:T(8,128)(2,1)S(1)} %constant_dynamic-update-slice_fusion.refs_0_), channel_id=1, source_target_pairs={{0,3},{1,2},{2,1},{3,0},{4,7},{5,6},{6,5},{7,4},{8,11},{9,10},{10,... | collective-permute-start | bytes 159752 | tf_op jit(solution)/shard_map/ppermute | solution.py:334
  18.6 0.0 collective-permute-start.8
  18.6 1.7 %collective-permute-done.7.refs_1_ = bf16[64,416]{1,0:T(8,128)(2,1)S(1)} collective-permute-done((bf16[64,416]{1,0:T(8,128)(2,1)S(1)}, bf16[64,416]{1,0:T(8,128)(2,1)S(1)}, u32[]{:S(2)}, u32[]{:S(2)}) %collective-permute-start.7) | collective-permute-done | bytes 53280 | tf_op jit(solution)/shard_map/ppermute | solution.py:334
  20.3 0.1 collective-permute-start.9
  20.4 1.7 %collective-permute-done.3.refs_2_ = bf16[64,416]{1,0:T(8,128)(2,1)S(1)} collective-permute-done((bf16[64,416]{1,0:T(8,128)(2,1)S(1)}, bf16[64,416]{1,0:T(8,128)(2,1)S(1)}, u32[]{:S(2)}, u32[]{:S(2)}) %collective-permute-start.3) | collective-permute-done | bytes 53280 | tf_op jit(solution)/shard_map/ppermute | solution.py:334
  22.1 0.0 collective-permute-start.4
  22.1 0.0 collective-permute-done.5.refs_3_
  22.1 0.5 %collective-permute-start.6 = (bf16[64,416]{1,0:T(8,128)(2,1)S(1)}, bf16[64,416]{1,0:T(8,128)(2,1)S(1)}, u32[]{:S(2)}, u32[]{:S(2)}) collective-permute-start(bf16[64,416]{1,0:T(8,128)(2,1)S(1)} %collective-permute-done.5.refs_3_), channel_id=1, source_target_pairs={{0,1},{1,0},{2,3},{3,2},{4,5},{5,4},{6,7},{7,6},{8,9},{9,8},{10,11... | collective-permute-start | bytes 159752 | tf_op jit(solution)/shard_map/ppermute | solution.py:334
  22.6 0.0 collective-permute-done.8.refs_4_
  22.6 0.0 collective-permute-done.9.refs_5_
  22.6 0.5 %sample.2.refs_2_ = f32[1,256]{1,0:T(1,128)S(1)} custom-call(bf16[256,512]{1,0:T(8,128)(2,1)S(1)} %get-tuple-element.10.re_ref, bf16[256,512]{1,0:T(8,128)(2,1)S(1)} %get-tuple-element.11.im_ref, f32[256,416]{1,0:T(8,128)S(1)} %get-tuple-element.12.tail_re_ref, f32[256,416]{1,0:T(8,128)S(1)} %get-tuple-element.13.tail_im_ref, ...), custom_call_target="tpu_custom_call" | custom-call | flops 163577856 | bytes 1048576 | tf_op jit(solution)/shard_map/sample/pallas_call | solution.py:310
  23.2 0.2 collective-permute-done.4.refs_0_
  23.4 0.2 collective-permute-done.6.refs_1_
  23.5 0.9 %sample.3 = f32[1,256]{1,0:T(1,128)} custom-call(bf16[256,512]{1,0:T(8,128)(2,1)S(1)} %get-tuple-element.10.re_ref, bf16[256,512]{1,0:T(8,128)(2,1)S(1)} %get-tuple-element.11.im_ref, f32[256,416]{1,0:T(8,128)S(1)} %get-tuple-element.12.tail_re_ref, f32[256,416]{1,0:T(8,128)S(1)} %get-tuple-element.13.tail_im_ref, ...), custom_call_target="tpu_custom_call" | custom-call | flops 54525952 | bytes 1048576 | tf_op jit(solution)/shard_map/sample/pallas_call | solution.py:310
  (5 shorter events, 0.0 us)
Async XLA Ops:
  6.8 4.2 %collective-permute-start.1 = (bf16[16,416]{1,0:T(8,128)(2,1)S(1)}, bf16[16,416]{1,0:T(8,128)(2,1)S(1)}, u32[]{:S(2)}, u32[]{:S(2)}) collective-permute-start(bf16[16,416]{1,0:T(8,128)(2,1)S(1)} %get-tuple-element.14), channel_id=1, source_target_pairs={{0,1},{1,0},{2,3},{3,2},{4,5},{5,4},{6,7},{7,6},{8,9},{9,8},{10,11... | collective-permute-start | bytes 39944 | tf_op jit(solution)/shard_map/ppermute | solution.py:334
  7.3 5.4 %collective-permute-start = (bf16[16,416]{1,0:T(8,128)(2,1)S(1)}, bf16[16,416]{1,0:T(8,128)(2,1)S(1)}, u32[]{:S(2)}, u32[]{:S(2)}) collective-permute-start(bf16[16,416]{1,0:T(8,128)(2,1)S(1)} %get-tuple-element.14), channel_id=1, source_target_pairs={{0,16},{1,17},{2,18},{3,19},{4,20},{5,21},{6,22},{7,23},{8,24},{9,... | collective-permute-start | bytes 39944 | tf_op jit(solution)/shard_map/ppermute | solution.py:334
  11.0 4.0 %collective-permute-start.2 = (bf16[32,416]{1,0:T(8,128)(2,1)S(1)}, bf16[32,416]{1,0:T(8,128)(2,1)S(1)}, u32[]{:S(2)}, u32[]{:S(2)}) collective-permute-start(bf16[32,416]{1,0:T(8,128)(2,1)S(1)} %pad_maximum_fusion), channel_id=1, source_target_pairs={{0,8},{1,25},{2,10},{3,27},{4,12},{5,29},{6,14},{7,31},{8,0},{9,17... | collective-permute-start | bytes 79880 | tf_op jit(solution)/shard_map/ppermute | solution.py:334
  15.0 5.4 %collective-permute-start.7 = (bf16[64,416]{1,0:T(8,128)(2,1)S(1)}, bf16[64,416]{1,0:T(8,128)(2,1)S(1)}, u32[]{:S(2)}, u32[]{:S(2)}) collective-permute-start(bf16[64,416]{1,0:T(8,128)(2,1)S(1)} %constant_dynamic-update-slice_fusion.refs_0_), channel_id=1, source_target_pairs={{0,7},{1,6},{2,5},{3,4},{4,3},{5,2},{6,1},{7,0},{8,15},{9,14},{10,... | collective-permute-start | bytes 159752 | tf_op jit(solution)/shard_map/ppermute | solution.py:334
  17.8 4.3 %collective-permute-start.3 = (bf16[64,416]{1,0:T(8,128)(2,1)S(1)}, bf16[64,416]{1,0:T(8,128)(2,1)S(1)}, u32[]{:S(2)}, u32[]{:S(2)}) collective-permute-start(bf16[64,416]{1,0:T(8,128)(2,1)S(1)} %constant_dynamic-update-slice_fusion.refs_0_), channel_id=1, source_target_pairs={{0,5},{1,4},{2,7},{3,6},{4,1},{5,0},{6,3},{7,2},{8,13},{9,12},{10,... | collective-permute-start | bytes 159752 | tf_op jit(solution)/shard_map/ppermute | solution.py:334
  17.8 4.3 %collective-permute-start.5 = (bf16[64,416]{1,0:T(8,128)(2,1)S(1)}, bf16[64,416]{1,0:T(8,128)(2,1)S(1)}, u32[]{:S(2)}, u32[]{:S(2)}) collective-permute-start(bf16[64,416]{1,0:T(8,128)(2,1)S(1)} %constant_dynamic-update-slice_fusion.refs_0_), channel_id=1, source_target_pairs={{0,3},{1,2},{2,1},{3,0},{4,7},{5,6},{6,5},{7,4},{8,11},{9,10},{10,... | collective-permute-start | bytes 159752 | tf_op jit(solution)/shard_map/ppermute | solution.py:334
  18.6 4.0 %collective-permute-start.8 = (bf16[64,416]{1,0:T(8,128)(2,1)S(1)}, bf16[64,416]{1,0:T(8,128)(2,1)S(1)}, u32[]{:S(2)}, u32[]{:S(2)}) collective-permute-start(bf16[64,416]{1,0:T(8,128)(2,1)S(1)} %constant_dynamic-update-slice_fusion.refs_0_), channel_id=1, source_target_pairs={{0,1},{1,0},{2,3},{3,2},{4,5},{5,4},{6,7},{7,6},{8,9},{9,8},{10,11... | collective-permute-start | bytes 159752 | tf_op jit(solution)/shard_map/ppermute | solution.py:334
  20.3 2.3 %collective-permute-start.9 = (bf16[64,416]{1,0:T(8,128)(2,1)S(1)}, bf16[64,416]{1,0:T(8,128)(2,1)S(1)}, u32[]{:S(2)}, u32[]{:S(2)}) collective-permute-start(bf16[64,416]{1,0:T(8,128)(2,1)S(1)} %collective-permute-done.7.refs_1_), channel_id=1, source_target_pairs={{0,1},{1,0},{2,3},{3,2},{4,5},{5,4},{6,7},{7,6},{8,9},{9,8},{10,11... | collective-permute-start | bytes 159752 | tf_op jit(solution)/shard_map/ppermute | solution.py:334
  22.1 1.3 %collective-permute-start.4 = (bf16[64,416]{1,0:T(8,128)(2,1)S(1)}, bf16[64,416]{1,0:T(8,128)(2,1)S(1)}, u32[]{:S(2)}, u32[]{:S(2)}) collective-permute-start(bf16[64,416]{1,0:T(8,128)(2,1)S(1)} %collective-permute-done.3.refs_2_), channel_id=1, source_target_pairs={{0,1},{1,0},{2,3},{3,2},{4,5},{5,4},{6,7},{7,6},{8,9},{9,8},{10,11... | collective-permute-start | bytes 159752 | tf_op jit(solution)/shard_map/ppermute | solution.py:334
  22.1 1.4 %collective-permute-start.6 = (bf16[64,416]{1,0:T(8,128)(2,1)S(1)}, bf16[64,416]{1,0:T(8,128)(2,1)S(1)}, u32[]{:S(2)}, u32[]{:S(2)}) collective-permute-start(bf16[64,416]{1,0:T(8,128)(2,1)S(1)} %collective-permute-done.5.refs_3_), channel_id=1, source_target_pairs={{0,1},{1,0},{2,3},{3,2},{4,5},{5,4},{6,7},{7,6},{8,9},{9,8},{10,11... | collective-permute-start | bytes 159752 | tf_op jit(solution)/shard_map/ppermute | solution.py:334
